TPU v7x, 256 devices: a whole 4x4x8 slice. The times are simulated.
256 devices in a mesh: grp: 4 (over x), tm: 64 (over z, y, core).
Axes of the slice: x: 4, y: 4, z: 8, core: 2. Of those that a mesh axis runs over, the one named last changes fastest.
Arguments:
- signal: bfloat16 [4, 8192, 512], P('grp', 'tm'), may hold values from -16 to 16
- damping: float32 [4, 8192], P('grp', 'tm'), may hold values from 0.25 to 1, as said below
- nu_log: float32 [1024], replicated, as said below
- theta: float32 [1024], replicated, may hold values from 0 to 0.63
- in_weight: bfloat16 [512, 2048], replicated, may hold values from -0.25 to 0.25
- out_weight: bfloat16 [512, 2048], replicated, may hold values from -0.125 to 0.125
- skip_gain: float32 [512], replicated, may hold values from 0.1 to 1.9
- cotangent: bfloat16 [4, 8192, 512], P('grp', 'tm'), may hold values from -16 to 16
Outputs:
- mixed: bfloat16 [4, 8192, 512], P('grp', 'tm')
- grad_signal: bfloat16 [4, 8192, 512], P('grp', 'tm')
- grad_in: float32 [512, 2048], P(('grp', 'tm'))
- grad_out: float32 [512, 2048], P(('grp', 'tm'))
Inputs may be any that keep to these rules, and one draw needn't show every extreme that they name: damping is 1 except at a few time steps of each record. exp(nu_log) lies between 0.01 / 8192 and 1/30.
All inputs are finite; a program needn't handle non-finite values.
Results may differ from a plain program's by a relative error of at most 0.0034.
Values sent between devices are 32-bit elements; how exact they have to be, the bound alone decides.
No kernel may reach another device: no remote copies, remote signals or barrier semaphores. Data moves between devices by JAX's collectives and lax.ppermute only.
A program may use at most 128 MiB of HBM per device.

v0:
```python
import math

import jax
import jax.numpy as jnp
from jax import lax
from jax.sharding import PartitionSpec as P


def prefix(part, axis, combine, identity, reverse):
    count = lax.axis_size(axis)
    place = lax.axis_index(axis)
    ahead = count - 1 - place if reverse else place
    gathered = jax.tree.map(lambda a: lax.all_gather(a, axis), part)
    state = jax.tree.map(lambda a, e: jnp.zeros_like(a) + jnp.asarray(e, a.dtype), part, identity)

    def one(turn, state):
        source = count - 1 - turn if reverse else turn
        return combine(
            state, jax.tree.map(lambda a: lax.dynamic_index_in_dim(a, source, 0, False), gathered)
        )

    return lax.fori_loop(0, ahead, one, state)


def combine(earlier, later):
    first_re, first_im, carry_re, carry_im = earlier
    second_re, second_im, next_re, next_im = later
    prod_re = second_re * first_re - second_im * first_im
    prod_im = second_re * first_im + second_im * first_re
    moved_re = second_re * carry_re - second_im * carry_im
    moved_im = second_re * carry_im + second_im * carry_re
    return (prod_re, prod_im, moved_re + next_re, moved_im + next_im)


def chain(decay_re, decay_im, drive_re, drive_im, backward):
    length, width = decay_re.shape
    inner = math.gcd(length, 16)
    outer = length // inner
    pieces = [
        item.reshape(outer, inner, width) for item in (decay_re, decay_im, drive_re, drive_im)
    ]
    carry = (
        jnp.ones((outer, width), jnp.float32),
        jnp.zeros((outer, width), jnp.float32),
        jnp.zeros((outer, width), jnp.float32),
        jnp.zeros((outer, width), jnp.float32),
    )
    order = list(range(inner))
    if backward:
        order = order[::-1]
    kept = {}
    for place in order:
        element = tuple((item[:, place] for item in pieces))
        carry = combine(carry, element)
        kept[place] = carry
    local = [jnp.stack([kept[place][member] for place in range(inner)], 1) for member in range(4)]
    summary = carry
    if backward:
        summary = tuple((jnp.flip(item, 0) for item in summary))
    inclusive = lax.associative_scan(combine, summary)
    ident = (
        jnp.ones((1, width), jnp.float32),
        jnp.zeros((1, width), jnp.float32),
        jnp.zeros((1, width), jnp.float32),
        jnp.zeros((1, width), jnp.float32),
    )
    exclusive = tuple(
        (
            jnp.concatenate([leading_operand, item[:-1]], 0)
            for leading_operand, item in zip(ident, inclusive)
        )
    )
    if backward:
        exclusive = tuple((jnp.flip(item, 0) for item in exclusive))
    enter_pre, enter_pim, enter_sre, enter_sim = [item[:, None, :] for item in exclusive]
    power_re, power_im, state_re, state_im = local
    total_re = state_re + power_re * enter_sre - power_im * enter_sim
    total_im = state_im + power_re * enter_sim + power_im * enter_sre
    whole_re = power_re * enter_pre - power_im * enter_pim
    whole_im = power_re * enter_pim + power_im * enter_pre
    return tuple((item.reshape(length, width) for item in (total_re, total_im, whole_re, whole_im)))


def body(signal, damping, nu_log, theta, in_weight, out_weight, skip_gain, cotangent):
    width = nu_log.shape[0]
    rate = jnp.exp(nu_log)
    magnitude = jnp.exp(-rate)
    lam_re = magnitude * jnp.cos(theta)
    lam_im = magnitude * jnp.sin(theta)
    scaling = jnp.sqrt(-jnp.expm1(-2.0 * rate))
    sig_rows = signal[0]
    upstream = cotangent[0]
    damp = damping[0][:, None]
    decay_re = damp * lam_re
    decay_im = damp * lam_im
    projected = jnp.dot(sig_rows, in_weight, preferred_element_type=jnp.float32)
    local_re, local_im, power_re, power_im = chain(
        decay_re, decay_im, scaling * projected[:, :width], scaling * projected[:, width:], False
    )
    grad_packed = jnp.dot(upstream, out_weight, preferred_element_type=jnp.float32)
    shift_re = jnp.concatenate([decay_re[1:], jnp.ones((1, width), jnp.float32)], 0)
    shift_im = jnp.concatenate([-decay_im[1:], jnp.zeros((1, width), jnp.float32)], 0)
    back_re, back_im, bpow_re, bpow_im = chain(
        shift_re, shift_im, grad_packed[:, :width], grad_packed[:, width:], True
    )
    forward_sum = (power_re[-1], power_im[-1], local_re[-1], local_im[-1])
    start_re = decay_re[0] * back_re[0] + decay_im[0] * back_im[0]
    start_im = decay_re[0] * back_im[0] - decay_im[0] * back_re[0]
    backward_sum = (power_re[-1], -power_im[-1], start_re, start_im)
    ident = (
        jnp.ones((width,), jnp.float32),
        jnp.zeros((width,), jnp.float32),
        jnp.zeros((width,), jnp.float32),
        jnp.zeros((width,), jnp.float32),
    )
    carry_fwd = prefix(forward_sum, "tm", combine, ident, False)
    carry_bwd = prefix(backward_sum, "tm", combine, ident, True)
    state_re = local_re + power_re * carry_fwd[2] - power_im * carry_fwd[3]
    state_im = local_im + power_re * carry_fwd[3] + power_im * carry_fwd[2]
    packed = jnp.concatenate([state_re, state_im], 1).astype(jnp.bfloat16)
    output = lax.dot_general(
        packed, out_weight, (((1,), (1,)), ((), ())), preferred_element_type=jnp.float32
    )
    output = (output + skip_gain * sig_rows.astype(jnp.float32)).astype(jnp.bfloat16)
    adj_re = back_re + bpow_re * carry_bwd[2] - bpow_im * carry_bwd[3]
    adj_im = back_im + bpow_re * carry_bwd[3] + bpow_im * carry_bwd[2]
    grad_drive = jnp.concatenate([scaling * adj_re, scaling * adj_im], 1).astype(jnp.bfloat16)
    grad_rows = lax.dot_general(
        grad_drive, in_weight, (((1,), (1,)), ((), ())), preferred_element_type=jnp.float32
    )
    grad_rows = (grad_rows + skip_gain * upstream.astype(jnp.float32)).astype(jnp.bfloat16)
    term_in = lax.dot_general(
        sig_rows, grad_drive, (((0,), (0,)), ((), ())), preferred_element_type=jnp.float32
    )
    term_out = lax.dot_general(
        upstream, packed, (((0,), (0,)), ((), ())), preferred_element_type=jnp.float32
    )
    summed = lax.psum_scatter(
        jnp.concatenate([term_in, term_out], 1), ("grp", "tm"), scatter_dimension=0, tiled=True
    )
    grad_in = summed[:, : 2 * width]
    grad_out = summed[:, 2 * width :]
    return (output[None], grad_rows[None], grad_in, grad_out)


def solution(mesh):
    placed = (P("grp", "tm", None), P("grp", "tm"), P(), P(), P(), P(), P(), P("grp", "tm", None))
    return jax.shard_map(
        body,
        mesh=mesh,
        in_specs=placed,
        out_specs=(
            P("grp", "tm", None),
            P("grp", "tm", None),
            P(("grp", "tm"), None),
            P(("grp", "tm"), None),
        ),
        check_vma=False,
    )
```

profile of v0, /device:TPU:1, one launch (start us, length us, event | category | flops | bytes accessed | tf_op | source)
XLA Modules:
  0.0 1057.5 jit_solution(7488104881296107607)
XLA Ops:
  7.3 2.2 fusion.16
  13.7 3.5 fusion.184
  46.6 3.8 slice.1035
  50.4 3.8 slice.1019
  54.3 3.9 slice.1017
  58.1 3.9 slice.1015
  62.0 3.9 slice.1022
  65.9 3.9 slice.1024
  69.7 3.9 slice.1027
  73.6 2.4 slice.1029
  76.1 1.5 add_add_fusion.33
  89.4 1.5 slice_add_fusion.8
  98.2 1.4 multiply_add_fusion.40
  102.0 1.4 constant_dynamic-update-slice_fusion.62
  103.5 1.4 constant_dynamic-update-slice_fusion.61
  104.9 1.6 constant_dynamic-update-slice_fusion.60
  106.5 1.5 constant_dynamic-update-slice_fusion.59
  108.0 1.5 constant_dynamic-update-slice_fusion.58
  109.5 1.5 constant_dynamic-update-slice_fusion.57
  111.0 1.5 constant_dynamic-update-slice_fusion.56
  112.4 1.5 constant_dynamic-update-slice_fusion.55
  113.9 1.5 constant_dynamic-update-slice_fusion.54
  115.4 1.5 constant_dynamic-update-slice_fusion.53
  116.9 1.4 constant_dynamic-update-slice_fusion.52
  118.3 1.4 constant_dynamic-update-slice_fusion.51
  132.1 1.4 subtract_add_fusion.34
  138.6 2.0 pad.446
  141.3 1.5 multiply_add_fusion.2
  143.1 49.1 %all-gather = f32[64,1,1024]{2,1,0:T(1,128)S(1)} all-gather(f32[1,1,1024]{2,1,0:T(1,128)S(1)} %slice_bitcast_fusion.2), channel_id=1, replica_groups=mesh['grp'=4,'tm'=64] {'tm'}, dimensions={0}, use_global_device_ids=true | all-gather | bytes 266240 | tf_op jit(solution)/shard_map/all_gather | solution.py:13
  194.0 43.2 %all-gather.1 = f32[64,1,1024]{2,1,0:T(1,128)S(1)} all-gather(f32[1,1,1024]{2,1,0:T(1,128)S(1)} %get-tuple-element.575), channel_id=1, replica_groups=mesh['grp'=4,'tm'=64] {'tm'}, dimensions={0}, use_global_device_ids=true | all-gather | bytes 266240 | tf_op jit(solution)/shard_map/all_gather | solution.py:13
  239.0 42.0 %all-gather.2 = f32[64,1,1024]{2,1,0:T(1,128)S(1)} all-gather(f32[1,1,1024]{2,1,0:T(1,128)S(1)} %slice_bitcast_fusion.1), channel_id=1, replica_groups=mesh['grp'=4,'tm'=64] {'tm'}, dimensions={0}, use_global_device_ids=true | all-gather | bytes 266240 | tf_op jit(solution)/shard_map/all_gather | solution.py:13
  282.9 43.2 %all-gather.3 = f32[64,1,1024]{2,1,0:T(1,128)S(1)} all-gather(f32[1,1,1024]{2,1,0:T(1,128)S(1)} %slice_bitcast_fusion), channel_id=1, replica_groups=mesh['grp'=4,'tm'=64] {'tm'}, dimensions={0}, use_global_device_ids=true | all-gather | bytes 266240 | tf_op jit(solution)/shard_map/all_gather | solution.py:13
  326.8 1.6 while.32
  328.5 1.5 constant_dynamic-update-slice_fusion.127
  330.5 3.9 slice.1058
  334.7 2.8 slice.1013
  337.5 3.8 slice.1062
  351.7 2.4 rev.18
  355.6 2.4 rev.17
  359.4 2.0 pad.451
  362.7 3.9 rev.19
  368.0 2.0 pad.270
  370.0 1.9 pad.450
  373.3 3.9 rev.20
  377.4 1.6 constant_dynamic-update-slice_fusion.93
  385.8 1.4 constant_dynamic-update-slice_fusion.87
  387.2 1.4 constant_dynamic-update-slice_fusion.86
  389.9 1.4 constant_dynamic-update-slice_fusion.84
  394.0 1.4 constant_dynamic-update-slice_fusion.81
  410.5 1.4 constant_dynamic-update-slice_fusion.98
  411.9 1.4 constant_dynamic-update-slice_fusion.97
  413.9 1.4 constant_dynamic-update-slice_fusion.77
  425.2 2.5 multiply_subtract_fusion.1
  430.0 142.1 %all-gather.4 = f32[64,1,1024]{2,1,0:T(1,128)S(1)} all-gather(f32[1,1,1024]{2,1,0:T(1,128)S(1)} %copy-done.112), channel_id=1, replica_groups=mesh['grp'=4,'tm'=64] {'tm'}, dimensions={0}, use_global_device_ids=true | all-gather | bytes 266240 | tf_op jit(solution)/shard_map/all_gather | solution.py:13
  575.8 42.3 %all-gather.5 = f32[64,1,1024]{2,1,0:T(1,128)S(1)} all-gather(f32[1,1,1024]{2,1,0:T(1,128)S(1)} %get-tuple-element.505), channel_id=1, replica_groups=mesh['grp'=4,'tm'=64] {'tm'}, dimensions={0}, use_global_device_ids=true | all-gather | bytes 266240 | tf_op jit(solution)/shard_map/all_gather | solution.py:13
  618.9 42.9 %all-gather.6 = f32[64,1,1024]{2,1,0:T(1,128)S(1)} all-gather(f32[1,1,1024]{2,1,0:T(1,128)S(1)} %get-tuple-element.504), channel_id=1, replica_groups=mesh['grp'=4,'tm'=64] {'tm'}, dimensions={0}, use_global_device_ids=true | all-gather | bytes 266240 | tf_op jit(solution)/shard_map/all_gather | solution.py:13
  662.5 100.5 %while.33 = (s32[]{:T(128)}, f32[1024]{0:T(1024)S(1)}, f32[1024]{0:T(1024)S(1)}, s32[]{:T(128)}, f32[64,1024]{1,0:T(8,128)}, /*index=5*/f32[64,1024]{1,0:T(8,128...) while((s32[]{:T(128)}, f32[1024]{0:T(1024)S(1)}, ...), condition=%wide.region_3.4_spmd, body=%wide.region_2.3_spmd.sunk | while | flops 8198 | bytes 65715 | solution.py:22
  763.0 1.4 subtract_convert_fusion
  767.1 4.2 pad_maximum_fusion
  772.3 1.5 fusion.3
  773.9 1.5 fusion.2
  775.4 269.1 %all-reduce.61.cloned.1.call-done = f32[512,4096]{0,1:T(8,128)} async-done(((f32[512,4096]{0,1:T(8,128)}), f32[512,4096]{0,1:T(8,128)}) %all-reduce.61.cloned.1.call-update) | async-done | bytes 8388624
  1044.4 3.2 fusion.178
  1047.6 2.2 copy.464
  (720 shorter events, 245.2 us)
Async XLA Ops:
  7.2 24.1 %copy-start = (bf16[512,2048]{1,0:T(8,128)(2,1)S(1)}, bf16[512,2048]{1,0:T(8,128)(2,1)}, u32[]{:S(2)}) copy-start(bf16[512,2048]{1,0:T(8,128)(2,1)} %param.17) | copy-start | bytes 6291460
  7.2 1037.2 %all-reduce.61.cloned.1.call-start = ((), (), s32[]{:S(2)}) async-start(), calls=%async_computation | async-start | bytes 16777216
  12.1 6.3 copy-start.44
  12.1 6.3 copy-start.46
  12.1 6.4 copy-start.34
  12.1 6.6 copy-start.32
  13.6 89.8 %copy-start.1 = (f32[8,16,1024]{2,0,1:T(8,128)}, f32[8,16,1024]{2,0,1:T(8,128)S(1)}, u32[]{:S(2)}) copy-start(f32[8,16,1024]{2,0,1:T(8,128)S(1)} %get-tuple-element.768) | copy-start | bytes 1572868
  13.6 89.8 %copy-start.3 = (f32[8,16,1024]{2,0,1:T(8,128)}, f32[8,16,1024]{2,0,1:T(8,128)S(1)}, u32[]{:S(2)}) copy-start(f32[8,16,1024]{2,0,1:T(8,128)S(1)} %get-tuple-element.769) | copy-start | bytes 1572868
  18.7 12.6 %copy-start.25 = (bf16[1,128,512]{2,1,0:T(8,128)(2,1)S(1)}, bf16[1,128,512]{2,1,0:T(8,128)(2,1)}, u32[]{:S(2)}) copy-start(bf16[1,128,512]{2,1,0:T(8,128)(2,1)} %param.19) | copy-start | bytes 393220
  19.0 12.7 %copy-start.74 = (f32[8,1024]{1,0:T(8,128)}, f32[8,1024]{1,0:T(8,128)S(1)}, u32[]{:S(2)}) copy-start(f32[8,1024]{1,0:T(8,128)S(1)} %fusion.80) | copy-start | bytes 98308
  37.5 70.5 %copy-start.62 = (f32[8,1,1024]{2,1,0:T(1,128)S(1)}, f32[8,1,1024]{2,1,0:T(1,128)}, u32[]{:S(2)}) copy-start(f32[8,1,1024]{2,1,0:T(1,128)} %get-tuple-element.634) | copy-start | bytes 98308
  38.2 31.5 %copy-start.75 = (f32[8,1024]{1,0:T(8,128)}, f32[8,1024]{1,0:T(8,128)S(1)}, u32[]{:S(2)}) copy-start(f32[8,1024]{1,0:T(8,128)S(1)} %get-tuple-element.675) | copy-start | bytes 98308
  73.6 40.3 %copy-start.52 = (f32[8,1,1024]{2,1,0:T(1,128)S(1)}, f32[8,1,1024]{2,1,0:T(1,128)}, u32[]{:S(2)}) copy-start(f32[8,1,1024]{2,1,0:T(1,128)} %copy-done.51) | copy-start | bytes 98308
  102.0 14.8 %copy-start.47 = (f32[8,1,1024]{2,1,0:T(1,128)S(1)}, f32[8,1,1024]{2,1,0:T(1,128)}, u32[]{:S(2)}) copy-start(f32[8,1,1024]{2,1,0:T(1,128)} %copy-done.46) | copy-start | bytes 98308
  102.0 14.8 %copy-start.54 = (f32[8,1,1024]{2,1,0:T(1,128)S(1)}, f32[8,1,1024]{2,1,0:T(1,128)}, u32[]{:S(2)}) copy-start(f32[8,1,1024]{2,1,0:T(1,128)} %copy-done.53) | copy-start | bytes 98308
  103.5 14.9 %copy-start.45 = (f32[8,1,1024]{2,1,0:T(1,128)S(1)}, f32[8,1,1024]{2,1,0:T(1,128)}, u32[]{:S(2)}) copy-start(f32[8,1,1024]{2,1,0:T(1,128)} %copy-done.44) | copy-start | bytes 98308
  103.5 14.9 %copy-start.50 = (f32[8,1,1024]{2,1,0:T(1,128)S(1)}, f32[8,1,1024]{2,1,0:T(1,128)}, u32[]{:S(2)}) copy-start(f32[8,1,1024]{2,1,0:T(1,128)} %copy-done.49) | copy-start | bytes 98308
  104.9 14.9 %copy-start.2 = (f32[8,16,1024]{2,0,1:T(8,128)S(1)}, f32[8,16,1024]{2,0,1:T(8,128)}, u32[]{:S(2)}) copy-start(f32[8,16,1024]{2,0,1:T(8,128)} %copy-done.1) | copy-start | bytes 1572868
  104.9 14.9 %copy-start.4 = (f32[8,16,1024]{2,0,1:T(8,128)S(1)}, f32[8,16,1024]{2,0,1:T(8,128)}, u32[]{:S(2)}) copy-start(f32[8,16,1024]{2,0,1:T(8,128)} %copy-done.3) | copy-start | bytes 1572868
  104.9 14.9 %copy-start.35 = (f32[8,1,1024]{2,1,0:T(1,128)S(1)}, f32[8,1,1024]{2,1,0:T(1,128)}, u32[]{:S(2)}) copy-start(f32[8,1,1024]{2,1,0:T(1,128)} %copy-done.34) | copy-start | bytes 98308
  104.9 14.9 %copy-start.39 = (f32[8,1,1024]{2,1,0:T(1,128)S(1)}, f32[8,1,1024]{2,1,0:T(1,128)}, u32[]{:S(2)}) copy-start(f32[8,1,1024]{2,1,0:T(1,128)} %copy-done.38) | copy-start | bytes 98308
  109.5 11.1 %copy-start.33 = (f32[8,1,1024]{2,1,0:T(1,128)S(1)}, f32[8,1,1024]{2,1,0:T(1,128)}, u32[]{:S(2)}) copy-start(f32[8,1,1024]{2,1,0:T(1,128)} %copy-done.32) | copy-start | bytes 98308
  109.5 11.1 %copy-start.37 = (f32[8,1,1024]{2,1,0:T(1,128)S(1)}, f32[8,1,1024]{2,1,0:T(1,128)}, u32[]{:S(2)}) copy-start(f32[8,1,1024]{2,1,0:T(1,128)} %copy-done.36) | copy-start | bytes 98308
  121.9 6.7 copy-start.110
  122.0 13.0 %copy-start.113 = (f32[1,1024]{1,0:T(1,128)S(1)}, f32[1,1024]{1,0:T(1,128)}, u32[]{:S(2)}) copy-start(f32[1,1024]{1,0:T(1,128)} %slice.1147) | copy-start | bytes 12292
  122.0 14.4 %slice-start = ((f32[8,1024]{1,0:T(8,128)}), f32[1,1024]{1,0:T(1,128)S(1)}, s32[]{:S(2)}) async-start(f32[8,1024]{1,0:T(8,128)} %copy-done.74), calls=%async_computation.1 | async-start | bytes 8192 | tf_op jit(solution)/shard_map/slice | solution.py:60
  122.1 19.2 %copy-start.20 = (f32[8,16,1024]{2,0,1:T(8,128)S(1)}, f32[8,16,1024]{2,0,1:T(8,128)}, u32[]{:S(2)}) copy-start(f32[8,16,1024]{2,0,1:T(8,128)} %get-tuple-element.359) | copy-start | bytes 1572868
  237.9 90.5 %copy-start.26 = (f32[8,1,1024]{2,0,1:T(8,128)S(1)}, f32[8,1,1024]{2,0,1:T(8,128)}, u32[]{:S(2)}) copy-start(f32[8,1,1024]{2,0,1:T(8,128)} %get-tuple-element.258) | copy-start | bytes 98308
  237.9 90.5 %copy-start.27 = (f32[8,1,1024]{2,0,1:T(8,128)S(1)}, f32[8,1,1024]{2,0,1:T(8,128)}, u32[]{:S(2)}) copy-start(f32[8,1,1024]{2,0,1:T(8,128)} %get-tuple-element.331) | copy-start | bytes 98308
  237.9 90.6 %copy-start.43 = (f32[8,1,1024]{2,1,0:T(1,128)S(1)}, f32[8,1,1024]{2,1,0:T(1,128)}, u32[]{:S(2)}) copy-start(f32[8,1,1024]{2,1,0:T(1,128)} %copy-done.42) | copy-start | bytes 98308
  238.2 96.2 %copy-start.105 = (f32[3,1024]{1,0:T(4,128)S(1)}, f32[3,1024]{1,0:T(4,128)}, u32[]{:S(2)}) copy-start(f32[3,1024]{1,0:T(4,128)} %slice.1052) | copy-start | bytes 36868
  238.2 103.1 %copy-start.111 = (f32[2,1024]{1,0:T(2,128)S(1)}, f32[2,1024]{1,0:T(2,128)}, u32[]{:S(2)}) copy-start(f32[2,1024]{1,0:T(2,128)} %pad_add_fusion.3) | copy-start | bytes 24580
  358.0 67.1 %copy-start.81 = (f32[8,1,1024]{2,0,1:T(8,128)S(1)}, f32[8,1,1024]{2,0,1:T(8,128)}, u32[]{:S(2)}) copy-start(f32[8,1,1024]{2,0,1:T(8,128)} %get-tuple-element.277) | copy-start | bytes 98308
  358.6 66.5 %copy-start.80 = (f32[8,1,1024]{2,0,1:T(8,128)S(1)}, f32[8,1,1024]{2,0,1:T(8,128)}, u32[]{:S(2)}) copy-start(f32[8,1,1024]{2,0,1:T(8,128)} %get-tuple-element.278) | copy-start | bytes 98308
  359.3 65.7 %copy-start.79 = (f32[8,1,1024]{2,0,1:T(8,128)S(1)}, f32[8,1,1024]{2,0,1:T(8,128)}, u32[]{:S(2)}) copy-start(f32[8,1,1024]{2,0,1:T(8,128)} %get-tuple-element.281) | copy-start | bytes 98308
  361.3 63.8 %copy-start.78 = (f32[8,1,1024]{2,0,1:T(8,128)S(1)}, f32[8,1,1024]{2,0,1:T(8,128)}, u32[]{:S(2)}) copy-start(f32[8,1,1024]{2,0,1:T(8,128)} %get-tuple-element.282) | copy-start | bytes 98308
  361.3 63.8 %copy-start.77 = (f32[8,1,1024]{2,0,1:T(8,128)S(1)}, f32[8,1,1024]{2,0,1:T(8,128)}, u32[]{:S(2)}) copy-start(f32[8,1,1024]{2,0,1:T(8,128)} %get-tuple-element.285) | copy-start | bytes 98308
  362.1 63.1 %copy-start.76 = (f32[8,1,1024]{2,0,1:T(8,128)S(1)}, f32[8,1,1024]{2,0,1:T(8,128)}, u32[]{:S(2)}) copy-start(f32[8,1,1024]{2,0,1:T(8,128)} %get-tuple-element.286) | copy-start | bytes 98308
  377.2 40.9 %copy-start.100 = (f32[8,1,1024]{2,0,1:T(8,128)S(1)}, f32[8,1,1024]{2,0,1:T(8,128)}, u32[]{:S(2)}) copy-start(f32[8,1,1024]{2,0,1:T(8,128)} %get-tuple-element.267) | copy-start | bytes 98308
  377.2 41.5 %copy-start.99 = (f32[8,1,1024]{2,0,1:T(8,128)S(1)}, f32[8,1,1024]{2,0,1:T(8,128)}, u32[]{:S(2)}) copy-start(f32[8,1,1024]{2,0,1:T(8,128)} %get-tuple-element.268) | copy-start | bytes 98308
  377.2 42.2 %copy-start.98 = (f32[8,1,1024]{2,0,1:T(8,128)S(1)}, f32[8,1,1024]{2,0,1:T(8,128)}, u32[]{:S(2)}) copy-start(f32[8,1,1024]{2,0,1:T(8,128)} %get-tuple-element.271) | copy-start | bytes 98308
  377.2 42.8 %copy-start.97 = (f32[8,1,1024]{2,0,1:T(8,128)S(1)}, f32[8,1,1024]{2,0,1:T(8,128)}, u32[]{:S(2)}) copy-start(f32[8,1,1024]{2,0,1:T(8,128)} %get-tuple-element.272) | copy-start | bytes 98308
  377.2 43.4 %copy-start.96 = (f32[8,1,1024]{2,0,1:T(8,128)S(1)}, f32[8,1,1024]{2,0,1:T(8,128)}, u32[]{:S(2)}) copy-start(f32[8,1,1024]{2,0,1:T(8,128)} %get-tuple-element.275) | copy-start | bytes 98308
  377.2 44.0 %copy-start.95 = (f32[8,1,1024]{2,0,1:T(8,128)S(1)}, f32[8,1,1024]{2,0,1:T(8,128)}, u32[]{:S(2)}) copy-start(f32[8,1,1024]{2,0,1:T(8,128)} %get-tuple-element.276) | copy-start | bytes 98308
  377.2 44.6 %copy-start.94 = (f32[8,1,1024]{2,0,1:T(8,128)S(1)}, f32[8,1,1024]{2,0,1:T(8,128)}, u32[]{:S(2)}) copy-start(f32[8,1,1024]{2,0,1:T(8,128)} %get-tuple-element.279) | copy-start | bytes 98308
  377.2 45.2 %copy-start.93 = (f32[8,1,1024]{2,0,1:T(8,128)S(1)}, f32[8,1,1024]{2,0,1:T(8,128)}, u32[]{:S(2)}) copy-start(f32[8,1,1024]{2,0,1:T(8,128)} %get-tuple-element.280) | copy-start | bytes 98308
  377.2 45.8 %copy-start.92 = (f32[8,1,1024]{2,0,1:T(8,128)S(1)}, f32[8,1,1024]{2,0,1:T(8,128)}, u32[]{:S(2)}) copy-start(f32[8,1,1024]{2,0,1:T(8,128)} %get-tuple-element.283) | copy-start | bytes 98308
  377.2 46.4 %copy-start.91 = (f32[8,1,1024]{2,0,1:T(8,128)S(1)}, f32[8,1,1024]{2,0,1:T(8,128)}, u32[]{:S(2)}) copy-start(f32[8,1,1024]{2,0,1:T(8,128)} %get-tuple-element.284) | copy-start | bytes 98308
  377.3 47.0 %copy-start.90 = (f32[8,1,1024]{2,0,1:T(8,128)S(1)}, f32[8,1,1024]{2,0,1:T(8,128)}, u32[]{:S(2)}) copy-start(f32[8,1,1024]{2,0,1:T(8,128)} %get-tuple-element.287) | copy-start | bytes 98308
  377.3 47.6 %copy-start.21 = (f32[8,16,1024]{2,0,1:T(8,128)S(1)}, f32[8,16,1024]{2,0,1:T(8,128)}, u32[]{:S(2)}) copy-start(f32[8,16,1024]{2,0,1:T(8,128)} %constant_dynamic-update-slice_fusion.126) | copy-start | bytes 1572868
  377.3 47.6 %copy-start.89 = (f32[8,1,1024]{2,0,1:T(8,128)S(1)}, f32[8,1,1024]{2,0,1:T(8,128)}, u32[]{:S(2)}) copy-start(f32[8,1,1024]{2,0,1:T(8,128)} %get-tuple-element.261) | copy-start | bytes 98308
  377.3 47.6 %copy-start.88 = (f32[8,1,1024]{2,0,1:T(8,128)S(1)}, f32[8,1,1024]{2,0,1:T(8,128)}, u32[]{:S(2)}) copy-start(f32[8,1,1024]{2,0,1:T(8,128)} %get-tuple-element.262) | copy-start | bytes 98308
  377.3 47.6 %copy-start.87 = (f32[8,1,1024]{2,0,1:T(8,128)S(1)}, f32[8,1,1024]{2,0,1:T(8,128)}, u32[]{:S(2)}) copy-start(f32[8,1,1024]{2,0,1:T(8,128)} %get-tuple-element.265) | copy-start | bytes 98308
  377.3 47.6 %copy-start.86 = (f32[8,1,1024]{2,0,1:T(8,128)S(1)}, f32[8,1,1024]{2,0,1:T(8,128)}, u32[]{:S(2)}) copy-start(f32[8,1,1024]{2,0,1:T(8,128)} %get-tuple-element.266) | copy-start | bytes 98308
  377.3 47.6 %copy-start.85 = (f32[8,1,1024]{2,0,1:T(8,128)S(1)}, f32[8,1,1024]{2,0,1:T(8,128)}, u32[]{:S(2)}) copy-start(f32[8,1,1024]{2,0,1:T(8,128)} %get-tuple-element.269) | copy-start | bytes 98308
  377.3 47.6 %copy-start.84 = (f32[8,1,1024]{2,0,1:T(8,128)S(1)}, f32[8,1,1024]{2,0,1:T(8,128)}, u32[]{:S(2)}) copy-start(f32[8,1,1024]{2,0,1:T(8,128)} %get-tuple-element.270) | copy-start | bytes 98308
  377.3 47.7 %copy-start.83 = (f32[8,1,1024]{2,0,1:T(8,128)S(1)}, f32[8,1,1024]{2,0,1:T(8,128)}, u32[]{:S(2)}) copy-start(f32[8,1,1024]{2,0,1:T(8,128)} %get-tuple-element.273) | copy-start | bytes 98308
  377.4 47.7 %copy-start.82 = (f32[8,1,1024]{2,0,1:T(8,128)S(1)}, f32[8,1,1024]{2,0,1:T(8,128)}, u32[]{:S(2)}) copy-start(f32[8,1,1024]{2,0,1:T(8,128)} %get-tuple-element.274) | copy-start | bytes 98308
  377.4 47.8 %copy-start.101 = (f32[8,1024]{1,0:T(8,128)S(1)}, f32[8,1024]{1,0:T(8,128)}, u32[]{:S(2)}) copy-start(f32[8,1024]{1,0:T(8,128)} %rev.18) | copy-start | bytes 98308
  377.4 47.8 %copy-start.102 = (f32[8,1024]{1,0:T(8,128)S(1)}, f32[8,1024]{1,0:T(8,128)}, u32[]{:S(2)}) copy-start(f32[8,1024]{1,0:T(8,128)} %rev.17) | copy-start | bytes 98308
  377.4 47.8 %copy-start.103 = (f32[8,1024]{1,0:T(8,128)S(1)}, f32[8,1024]{1,0:T(8,128)}, u32[]{:S(2)}) copy-start(f32[8,1024]{1,0:T(8,128)} %rev.19) | copy-start | bytes 98308
  377.4 47.8 %copy-start.104 = (f32[8,1024]{1,0:T(8,128)S(1)}, f32[8,1024]{1,0:T(8,128)}, u32[]{:S(2)}) copy-start(f32[8,1024]{1,0:T(8,128)} %rev.20) | copy-start | bytes 98308
  413.9 11.3 %copy-start.19 = (f32[8,16,1024]{2,0,1:T(8,128)S(1)}, f32[8,16,1024]{2,0,1:T(8,128)}, u32[]{:S(2)}) copy-start(f32[8,16,1024]{2,0,1:T(8,128)} %get-tuple-element.693) | copy-start | bytes 1572868
  430.0 144.2 %copy-start.15 = (f32[8,16,1024]{2,0,1:T(8,128)S(1)}, f32[8,16,1024]{2,0,1:T(8,128)}, u32[]{:S(2)}) copy-start(f32[8,16,1024]{2,0,1:T(8,128)} %get-tuple-element.506) | copy-start | bytes 1572868
  (56 other events, 128.3 us)
Sparse Core Ops, SparseCore 0:
  771.5 272.9 all-reduce.60
where the time goes:
time: 1080 us; the launch traced here: 1060 us
  blocking collectives  405 us (38%)
  local copies, waits for them, and re-layouts  279 us (26%)
  waiting for transfers between devices  269 us (25%)
  other arithmetic  79 us (7%)
  between operations  16.2 us (2%)
    all_gather x7, blocking collectives, prefix(): gathered = jax.tree.map(lambda a: lax.all_gather(a, axis), part)  405 us
    unnamed x2, waiting for transfers between devices  269 us
    dynamic_slice x126, local copies, waits for them, and re-layouts, one(): lax.dynamic_index_in_dim(a, source, 0, False)  99.5 us
    unnamed x315, local copies, waits for them, and re-layouts  71.5 us
    slice x67, local copies, waits for them, and re-layouts, chain(): inclusive = lax.associative_scan(combine, summary)  71.5 us
    unnamed x33, other arithmetic  25.9 us
  transfers between devices with their start and end apart: 1, of which 1 were waited for; matrix products, arithmetic and copies ran while one was open for 0% of the time, Pallas kernels for 0%

commit v1 on v0

v1 whole, which is shorter than its diff:
```python
import jax
import jax.numpy as jnp
import numpy as np
from jax import lax
from jax.experimental import pallas as pl
from jax.experimental.pallas import tpu as pltpu
from jax.sharding import Mesh, PartitionSpec as P

X, Z, Y, C = 4, 8, 4, 2
D, N = 512, 1024
TOK = 128
T = C * TOK
W = N // C
LANES = 128
CH = W // LANES
GROUPS = T // 8
BLOCKS = Z * Y
F32, BF16 = jnp.float32, jnp.bfloat16
NT = (((1,), (1,)), ((), ()))


def ring(size, step):
    return [(i, (i + step) % size) for i in range(size)]


def cmul(ar, ai, br, bi):
    return ar * br - ai * bi, ar * bi + ai * br


def rows8():
    return lax.broadcasted_iota(jnp.int32, (8, LANES), 0)


def fwd_factors(d, i):
    dd = d * pltpu.roll(d, 1, 0)
    dddd = dd * pltpu.roll(dd, 2, 0)
    m1 = jnp.where(i >= 1, d, 0.0)
    m2 = jnp.where(i >= 2, dd, 0.0)
    m4 = jnp.where(i >= 4, dddd, 0.0)
    return m1, m2, m4


def cum_fwd(d, i):
    p = d
    for k in (1, 2, 4):
        p = jnp.where(i >= k, p * pltpu.roll(p, k, 0), p)
    return p


def cum_bwd(d, i):
    p = d
    for k in (1, 2, 4):
        p = jnp.where(i < 8 - k, p * pltpu.roll(p, 8 - k, 0), p)
    return p


def bwd_factors(d, i):
    e = pltpu.roll(d, 7, 0)
    ee = e * pltpu.roll(e, 7, 0)
    eeee = ee * pltpu.roll(ee, 6, 0)
    m1 = jnp.where(i < 7, e, 0.0)
    m2 = jnp.where(i < 6, ee, 0.0)
    m4 = jnp.where(i < 4, eeee, 0.0)
    return m1, m2, m4


def scan8(sr, si, masks, powers, backward):
    for (k, m), (pr, pi) in zip(zip((1, 2, 4), masks), powers):
        shift = 8 - k if backward else k
        rr = m * pltpu.roll(sr, shift, 0)
        ri = m * pltpu.roll(si, shift, 0)
        if backward:
            sr, si = sr + (pr * rr + pi * ri), si + (pr * ri - pi * rr)
        else:
            sr, si = sr + (pr * rr - pi * ri), si + (pr * ri + pi * rr)
    return sr, si


def powers_of(par_ref, j):
    lr = jnp.broadcast_to(par_ref[j : j + 1, :], (8, LANES))
    li = jnp.broadcast_to(par_ref[4 + j : 5 + j, :], (8, LANES))
    p1 = (lr, li)
    p2 = cmul(*p1, *p1)
    p4 = cmul(*p2, *p2)
    p8 = cmul(*p4, *p4)
    return p1, p2, p4, p8


def local_kernel(
    idx, par, damp, sig, cot, other, win_re, win_im, wout_re, wout_im,
    sig_all, cot_all, fre, fim, bre, bim, msg,
):
    c = idx[0]
    own = pl.ds(pl.multiple_of(c * TOK, TOK), TOK)
    oth = pl.ds(pl.multiple_of((1 - c) * TOK, TOK), TOK)
    sig_all[own, :] = sig[...]
    cot_all[own, :] = cot[...]
    sig_all[oth, :] = other[:, :D].astype(BF16)
    cot_all[oth, :] = other[:, D:].astype(BF16)
    s = sig_all[...]
    u = cot_all[...]
    fre[...] = jnp.dot(s, win_re[...], preferred_element_type=F32)
    fim[...] = jnp.dot(s, win_im[...], preferred_element_type=F32)
    bre[...] = jnp.dot(u, wout_re[...], preferred_element_type=F32)
    bim[...] = jnp.dot(u, wout_im[...], preferred_element_type=F32)
    i = rows8()
    pw = [powers_of(par, j) for j in range(CH)]
    gam = [jnp.broadcast_to(par[8 + j : 9 + j, :], (8, LANES)) for j in range(CH)]

    def step(g, carry):
        ff, mm, prod = carry
        rf = pl.ds(pl.multiple_of(g * 8, 8), 8)
        rb = pl.ds(pl.multiple_of((GROUPS - 1 - g) * 8, 8), 8)
        df = damp[rf, :]
        db = damp[rb, :]
        mf = fwd_factors(df, i)
        mb = bwd_factors(db, i)
        cf = cum_fwd(df, i)
        cb = cum_bwd(db, i)
        nf, nm = [], []
        for j in range(CH):
            col = pl.ds(j * LANES, LANES)
            p1, p2, p4, p8 = pw[j]
            sr, si = scan8(
                gam[j] * fre[rf, col], gam[j] * fim[rf, col], mf, (p1, p2, p4), False
            )
            fre[rf, col] = sr
            fim[rf, col] = si
            ar, ai = cmul(*p8, *ff[j])
            nf.append((sr + cf * ar, si + cf * ai))
            sr, si = scan8(bre[rb, col], bim[rb, col], mb, (p1, p2, p4), True)
            bre[rb, col] = sr
            bim[rb, col] = si
            vr, vi = cmul(p1[0], -p1[1], sr, si)
            ar, ai = cmul(p8[0], -p8[1], *mm[j])
            nm.append((db * vr + cb * ar, db * vi + cb * ai))
        return nf, nm, prod * cf

    zero = jnp.zeros((8, LANES), F32)
    start = [(zero, zero) for _ in range(CH)]
    ff, mm, prod = lax.fori_loop(0, GROUPS, step, (start, start, zero + 1.0))
    rows = (
        [ff[j][0][7:8] for j in range(CH)]
        + [ff[j][1][7:8] for j in range(CH)]
        + [mm[j][0][0:1] for j in range(CH)]
        + [mm[j][1][0:1] for j in range(CH)]
    )
    message = jnp.concatenate(rows + [jnp.broadcast_to(prod[7:8], (8, LANES))], 0)
    msg[...] = jnp.broadcast_to(message[None], msg.shape)


def local_call(idx, par, damp, sig, cot, other, in_weight, out_weight):
    whole = lambda shape: pl.BlockSpec(shape, lambda s, ix: (0,) * len(shape))
    half = lambda k: pl.BlockSpec((D, W), lambda s, ix: (0, k * C + ix[0]))
    shapes = (
        [((T, D), BF16)] * 2 + [((T, W), F32)] * 4 + [((BLOCKS, 24, LANES), F32)]
    )
    return pl.pallas_call(
        local_kernel,
        grid_spec=pltpu.PrefetchScalarGridSpec(
            num_scalar_prefetch=1,
            grid=(1,),
            in_specs=[
                whole((16, LANES)), whole((T, LANES)), whole((TOK, D)), whole((TOK, D)),
                whole((TOK, 2 * D)), half(0), half(1), half(0), half(1),
            ],
            out_specs=[whole(s) for s, _ in shapes],
        ),
        out_shape=[jax.ShapeDtypeStruct(s, t) for s, t in shapes],
        name="local",
    )(idx, par, damp, sig, cot, other, in_weight, in_weight, out_weight, out_weight)


def one_hot(order):
    r = lax.broadcasted_iota(jnp.int32, (D, D), 0)
    k = lax.broadcasted_iota(jnp.int32, (D, D), 1)
    hi, mid, z, low = r >> 7, (r >> 5) & 3, (r >> 2) & 7, r & 3
    x, y = (hi, mid) if order == "xy" else (mid, hi)
    old = x * 128 + z * 16 + y * 4 + low
    return jnp.where(old == k, 1.0, 0.0).astype(BF16)


def grads_kernel(idx, par, damp, sig, cot, fre, fim, bre, bim, got, *rest):
    outs, packed, drive = rest[:8], rest[8], rest[9]
    sr_, si_, ar_, ai_, lhs_in, lhs_out = rest[10:]
    x, y, q = idx[1], idx[2], idx[3]
    i = rows8()
    lam_r, lam_i = par[0:CH, :], par[4 : 4 + CH, :]
    pr, pi = lam_r, lam_i
    for _ in range(8):
        pr, pi = cmul(pr, pi, pr, pi)

    def joined(b, carry):
        fr, fi, mr, mi = carry
        dec = got[b, 16 : 16 + CH, :]
        tr, ti = cmul(dec * pr, dec * pi, fr, fi)
        on = b < q
        fr = jnp.where(on, tr + got[b, 0:CH, :], fr)
        fi = jnp.where(on, ti + got[b, 4 : 4 + CH, :], fi)
        e = BLOCKS - 1 - b
        dec = got[e, 16 : 16 + CH, :]
        tr, ti = cmul(dec * pr, -(dec * pi), mr, mi)
        on = e > q
        mr = jnp.where(on, tr + got[e, 8 : 8 + CH, :], mr)
        mi = jnp.where(on, ti + got[e, 12 : 12 + CH, :], mi)
        return fr, fi, mr, mi

    zero = jnp.zeros((CH, LANES), F32)
    fr, fi, mr, mi = lax.fori_loop(0, BLOCKS, joined, (zero,) * 4)
    spread = lambda a, j: jnp.broadcast_to(a[j : j + 1, :], (8, LANES))
    tabs, backs, gams, eights, ones = [], [], [], [], []
    for j in range(CH):
        p1, p2, p4, p8 = powers_of(par, j)
        tr, ti = zero8 = (jnp.ones((8, LANES), F32), jnp.zeros((8, LANES), F32))
        for bit, p in ((1, p1), (2, p2), (4, p4)):
            nr, ni = cmul(tr, ti, *p)
            on = (i & bit) != 0
            tr, ti = jnp.where(on, nr, tr), jnp.where(on, ni, ti)
        tabs.append(cmul(tr, ti, *p1))
        tr, ti = zero8
        for bit, p in ((1, p1), (2, p2), (4, p4)):
            nr, ni = cmul(tr, ti, *p)
            on = ((7 - i) & bit) != 0
            tr, ti = jnp.where(on, nr, tr), jnp.where(on, ni, ti)
        backs.append((tr, -ti))
        gams.append(jnp.broadcast_to(par[8 + j : 9 + j, :], (8, LANES)))
        ones.append(p1)

    def step(g, carry):
        ff, mm = carry
        rf = pl.ds(pl.multiple_of(g * 8, 8), 8)
        rb = pl.ds(pl.multiple_of((GROUPS - 1 - g) * 8, 8), 8)
        cf = cum_fwd(damp[rf, :], i)
        db = damp[rb, :]
        e = jnp.where(i < 7, pltpu.roll(db, 7, 0), 1.0)
        cb = cum_bwd(e, i)
        nf, nm = [], []
        for j in range(CH):
            col = pl.ds(j * LANES, LANES)
            colb = pl.ds(W + j * LANES, LANES)
            tr, ti = cmul(*tabs[j], *ff[j])
            sr = fre[rf, col] + cf * tr
            si = fim[rf, col] + cf * ti
            sr_[rf, col] = sr
            sr_[rf, colb] = si
            nf.append((spread(sr, 7), spread(si, 7)))
            tr, ti = cmul(*backs[j], *mm[j])
            vr = bre[rb, col] + cb * tr
            vi = bim[rb, col] + cb * ti
            ar_[rb, col] = gams[j] * vr
            ar_[rb, colb] = gams[j] * vi
            tr, ti = cmul(ones[j][0], -ones[j][1], vr, vi)
            nm.append((spread(db * tr, 0), spread(db * ti, 0)))
        return nf, nm

    lax.fori_loop(
        0, GROUPS, step,
        (
            [(spread(fr, j), spread(fi, j)) for j in range(CH)],
            [(spread(mr, j), spread(mi, j)) for j in range(CH)],
        ),
    )
    packed[...] = sr_[...].astype(BF16)
    drive[...] = ar_[...].astype(BF16)
    lhs_in[...] = lax.dot_general(
        one_hot("xy"), sig[...], NT, preferred_element_type=F32
    ).astype(BF16)
    lhs_out[...] = lax.dot_general(
        one_hot("yx"), cot[...], NT, preferred_element_type=F32
    ).astype(BF16)
    for d in range(4):
        rows = pl.ds(pl.multiple_of(((x + d) & 3) * 128, 128), 128)
        outs[d][...] = jnp.dot(lhs_in[rows, :], drive[...], preferred_element_type=F32)
        rows = pl.ds(pl.multiple_of(((y + d) & 3) * 128, 128), 128)
        outs[4 + d][...] = jnp.dot(lhs_out[rows, :], packed[...], preferred_element_type=F32)


def grads_call(idx, par, damp, sig, cot, fre, fim, bre, bim, got):
    whole = lambda shape: pl.BlockSpec(shape, lambda s, ix: (0,) * len(shape))
    shapes = [((128, 2 * W), F32)] * 8 + [((T, 2 * W), BF16)] * 2
    return pl.pallas_call(
        grads_kernel,
        grid_spec=pltpu.PrefetchScalarGridSpec(
            num_scalar_prefetch=1,
            grid=(1,),
            in_specs=[
                whole((16, LANES)), whole((T, LANES)), whole((T, D)), whole((T, D)),
                whole((T, W)), whole((T, W)), whole((T, W)), whole((T, W)),
                whole((BLOCKS, 24, LANES)),
            ],
            out_specs=[whole(s) for s, _ in shapes],
            scratch_shapes=[
                pltpu.VMEM((T, 2 * W), F32), pltpu.VMEM((8, LANES), F32),
                pltpu.VMEM((T, 2 * W), F32), pltpu.VMEM((8, LANES), F32),
                pltpu.VMEM((D, T), BF16), pltpu.VMEM((D, T), BF16),
            ],
        ),
        out_shape=[jax.ShapeDtypeStruct(s, t) for s, t in shapes],
        name="grads",
    )(idx, par, damp, sig, cot, fre, fim, bre, bim, got)


def rows_kernel(idx, packed, drive, win_re, win_im, wout_re, wout_im, own, oth):
    c = idx[0]
    for out, at in ((own, c), (oth, 1 - c)):
        rows = pl.ds(pl.multiple_of(at * TOK, TOK), TOK)
        out[:, :D] = lax.dot_general(
            packed[rows, :W], wout_re[...], NT, preferred_element_type=F32
        ) + lax.dot_general(packed[rows, W:], wout_im[...], NT, preferred_element_type=F32)
        out[:, D:] = lax.dot_general(
            drive[rows, :W], win_re[...], NT, preferred_element_type=F32
        ) + lax.dot_general(drive[rows, W:], win_im[...], NT, preferred_element_type=F32)


def rows_call(idx, packed, drive, in_weight, out_weight):
    whole = lambda shape: pl.BlockSpec(shape, lambda s, ix: (0,) * len(shape))
    half = lambda k: pl.BlockSpec((D, W), lambda s, ix: (0, k * C + ix[0]))
    return pl.pallas_call(
        rows_kernel,
        grid_spec=pltpu.PrefetchScalarGridSpec(
            num_scalar_prefetch=1,
            grid=(1,),
            in_specs=[whole((T, 2 * W)), whole((T, 2 * W)), half(0), half(1), half(0), half(1)],
            out_specs=[whole((TOK, 2 * D))] * 2,
        ),
        out_shape=[jax.ShapeDtypeStruct((TOK, 2 * D), F32)] * 2,
        name="rows",
    )(idx, packed, drive, in_weight, in_weight, out_weight, out_weight)


def sum_kernel(slot, idx, a, b, c, d, *outs):
    at = idx[slot]
    total = a[...] + b[...] + c[...] + d[...]
    scratch = outs[4]
    scratch[...] = total
    for k in range(4):
        outs[k][...] = scratch[pl.ds(pl.multiple_of(((at + k) & 3) * 32, 32), 32), :]


def sum_call(slot, idx, parts):
    whole = lambda shape: pl.BlockSpec(shape, lambda s, ix: (0,) * len(shape))
    return pl.pallas_call(
        lambda *refs: sum_kernel(slot, *refs),
        grid_spec=pltpu.PrefetchScalarGridSpec(
            num_scalar_prefetch=1,
            grid=(1,),
            in_specs=[whole((128, 2 * W))] * 4,
            out_specs=[whole((32, 2 * W))] * 4,
            scratch_shapes=[pltpu.VMEM((128, 2 * W), F32)],
        ),
        out_shape=[jax.ShapeDtypeStruct((32, 2 * W), F32)] * 4,
        name="sums",
    )(idx, *parts)


def body(signal, damping, nu_log, theta, in_weight, out_weight, skip_gain, cotangent):
    x, z = lax.axis_index("x"), lax.axis_index("z")
    y, c = lax.axis_index("y"), lax.axis_index("c")
    idx = jnp.stack([c, x, y, z * Y + y]).astype(jnp.int32)
    rate = jnp.exp(nu_log)
    magnitude = jnp.exp(-rate)
    par = jnp.concatenate(
        [magnitude * jnp.cos(theta), magnitude * jnp.sin(theta), jnp.sqrt(-jnp.expm1(-2.0 * rate)), rate]
    ).reshape(4, C, CH, LANES)
    par = lax.dynamic_index_in_dim(par, c, 1, False).reshape(16, LANES)
    sig, cot = signal[0], cotangent[0]
    wide = jnp.concatenate([sig, cot], 1).astype(F32)
    swap = ring(C, 1)
    other = lax.ppermute(wide, "c", swap)
    damp_other = lax.ppermute(damping, "c", swap)
    damp = jnp.where(
        c == 0,
        jnp.concatenate([damping[0], damp_other[0]]),
        jnp.concatenate([damp_other[0], damping[0]]),
    )
    damp = jnp.broadcast_to(damp[:, None], (T, LANES))
    sig_all, cot_all, fre, fim, bre, bim, msg = local_call(
        idx, par, damp, sig, cot, other, in_weight, out_weight
    )
    got = lax.all_to_all(msg, ("z", "y"), 0, 0)
    made = grads_call(idx, par, damp, sig_all, cot_all, fre, fim, bre, bim, got)
    one, two, packed, drive = made[:4], made[4:8], made[8], made[9]

    def hop(parts, axis, size):
        return [parts[0]] + [
            lax.ppermute(parts[d], axis, ring(size, d)) for d in (1, 3, 2)
        ]

    one = hop(one, "x", X)
    two = hop(two, "y", Y)
    own, oth = rows_call(idx, packed, drive, in_weight, out_weight)
    own = own + lax.ppermute(oth, "c", swap)
    gain = jnp.concatenate([skip_gain, skip_gain])
    rows = (own + gain * wide).astype(BF16)
    one = hop(sum_call(2, idx, one), "y", Y)
    two = hop(sum_call(1, idx, two), "x", X)
    small = jnp.concatenate(
        [
            (one[0] + one[1] + one[2] + one[3]).reshape(Z, 4, 2 * W),
            (two[0] + two[1] + two[2] + two[3]).reshape(Z, 4, 2 * W),
        ],
        1,
    )
    small = lax.all_to_all(small, "z", 0, 0).sum(0).reshape(2, C, 2, 2 * W)
    keep = lax.dynamic_index_in_dim(small, c, 1, False)
    send = lax.dynamic_index_in_dim(small, 1 - c, 1, False)
    come = lax.ppermute(send, "c", swap)
    first = jnp.where(c == 0, keep, come).reshape(2, 2, 2, 1, W)
    second = jnp.where(c == 0, come, keep).reshape(2, 2, 2, 1, W)
    full = jnp.concatenate([first, second], 3).reshape(2, 2, 2 * N)
    return rows[None, :, :D], rows[None, :, D:], full[0], full[1]


def solution(mesh):
    grid = Mesh(np.asarray(mesh.devices).reshape(X, Z, Y, C), ("x", "z", "y", "c"))
    tm = ("z", "y", "c")
    placed = (P("x", tm, None), P("x", tm), P(), P(), P(), P(), P(), P("x", tm, None))
    rows = P(("x",) + tm, None)
    return jax.shard_map(
        body,
        mesh=grid,
        in_specs=placed,
        out_specs=(P("x", tm, None), P("x", tm, None), rows, rows),
        check_vma=False,
    )
```

time: 1080 us -> 122 us (0.11); the launches traced: 1060 us -> 122 us
  blocking collectives: 405 us -> 23.4 us
  local copies, waits for them, and re-layouts: 279 us -> 4.62 us
  waiting for transfers between devices: 269 us -> 32.3 us
  other arithmetic: 79 us -> 5.67 us
  starting transfers between devices: 0.04 us -> 29.4 us
  Pallas kernels: 0 us -> 25.4 us
  between operations: 16.2 us -> 0.82 us
    all_gather x7 -> x0, blocking collectives: 405 us -> none  [prefix(): gathered = jax.tree.map(lambda a: lax.all_gather(a, axis), part)]
    unnamed x2 -> x0, waiting for transfers between devices: 269 us -> none
    dynamic_slice x126 -> x0, local copies, waits for them, and re-layouts: 99.5 us -> none  [one(): lax.dynamic_index_in_dim(a, source, 0, False)]
    slice x84 -> x0, local copies, waits for them, and re-layouts: 83.9 us -> none  [the longest x67 71.5 us: chain(): inclusive = lax.associative_scan(combine, summary)]
    unnamed x315 -> x24, local copies, waits for them, and re-layouts: 71.5 us -> 1.65 us
    add x125 -> x2, other arithmetic: 27.2 us -> 0.96 us  [the longest x1 0.93 us: body(): two[0] + two[1] + two[2] + two[3]]
    ppermute x0 -> x16, starting transfers between devices: none -> 26 us  [the longest x12 16.3 us: hop(): lax.ppermute(parts[d], axis, ring(size, d))]
    unnamed x33 -> x0, other arithmetic: 25.9 us -> none
  transfers between devices with their start and end apart: 1 -> 17, of which waited for: 1 -> 6; matrix products, arithmetic and copies ran while one was open for 0% -> 5% of each run, Pallas kernels for 0% -> 9%
where the time goes in v1:
time: 122 us
  waiting for transfers between devices  32.3 us (26%)
  starting transfers between devices  29.4 us (24%)
  Pallas kernels  25.4 us (21%)
  blocking collectives  23.4 us (19%)
  other arithmetic  5.67 us (5%)
  local copies, waits for them, and re-layouts  4.62 us (4%)
    all_to_all x1, blocking collectives, body(): got = lax.all_to_all(msg, ('z', 'y'), 0, 0)  23.4 us
    ppermute x12, waiting for transfers between devices, hop(): lax.ppermute(parts[d], axis, ring(size, d))  22.2 us
    ppermute x12, starting transfers between devices, hop(): lax.ppermute(parts[d], axis, ring(size, d))  16.3 us
    all_to_all x1, waiting for transfers between devices, body(): small = lax.all_to_all(small, 'z', 0, 0).sum(0).reshape(2, C, 2, 2 * W)  9.96 us
    pallas_call x1, Pallas kernels, local_call(): pl.pallas_call(local_kernel, grid_spec=pltpu.PrefetchScalarGridSpec(num_s...  7.24 us
    pallas_call x1, Pallas kernels, grads_call(): pl.pallas_call(grads_kernel, grid_spec=pltpu.PrefetchScalarGridSpec(num_s...  6.96 us
    pallas_call x2, Pallas kernels, sum_call(): pl.pallas_call(lambda *refs: sum_kernel(slot, *refs), grid_spec=pltpu.Pre...  6.39 us
    pallas_call x1, Pallas kernels, rows_call(): pl.pallas_call(rows_kernel, grid_spec=pltpu.PrefetchScalarGridSpec(num_sc...  4.78 us
  transfers between devices with their start and end apart: 17, of which 6 were waited for; matrix products, arithmetic and copies ran while one was open for 5% of the time, Pallas kernels for 9%

profile of v1, /device:TPU:1, one launch (start us, length us, event | category | flops | bytes accessed | tf_op | source)
XLA Modules:
  0.0 121.5 jit_solution(7899881674662386214)
XLA Ops:
  0.6 3.3 %collective-permute-start = (f32[1,128]{1,0:T(1,128)}, f32[1,128]{1,0:T(1,128)S(1)}, u32[]{:S(2)}, u32[]{:S(2)}) collective-permute-start(f32[1,128]{1,0:T(1,128)} %param.9), channel_id=1, source_target_pairs={{0,1},{1,0},{2,3},{3,2},{4,5},{5,4},{6,7},{7,6},{8,9},{9,8},{10,11... | collective-permute-start | bytes 1544 | tf_op jit(solution)/shard_map/ppermute | solution.py:370
  3.9 1.0 maximum_convert_fusion
  4.9 0.1 collective-permute-start.1
  5.0 0.7 fusion.4
  5.8 0.6 fusion.3
  6.4 0.7 pad_add_fusion.idx.refs_0_
  7.1 0.0 collective-permute-done
  7.1 0.7 maximum_select_fusion
  7.8 0.0 collective-permute-done.1.other
  7.8 0.0 copy-start.9
  7.8 0.8 broadcast_in_dim.6.damp
  8.7 0.0 copy-done.9
  8.7 7.2 %local.1 = (bf16[256,512]{1,0:T(8,128)(2,1)}, bf16[256,512]{1,0:T(8,128)(2,1)}, f32[256,512]{1,0:T(8,128)}, f32[256,512]{1,0:T(8,128)}, f32[256,512]{1,0:T(8,128...) custom-call(s32[4]{0:T(128)} %pad_add_fusion.idx.refs_0_, f32[16,128]{1,0:T(8,128)} %bitcast.28, ...), custom_call_target="tpu_custom_call" | custom-call | tf_op jit(solution)/shard_map/local/pallas_call | solution.py:158
  15.9 23.4 %all_to_all.10.got = f32[32,24,128]{2,1,0:T(8,128)} all-to-all(f32[32,24,128]{2,1,0:T(8,128)} %get-tuple-element.37), channel_id=1, replica_groups=mesh['x'=4,'z'=8,'y'=4,'c'=2] {'z','y'}, dimensions={0} | all-to-all | bytes 786432 | tf_op jit(solution)/shard_map/all_to_all | solution.py:380
  39.3 7.0 %grads.1 = (f32[128,1024]{1,0:T(8,128)}, f32[128,1024]{1,0:T(8,128)}, f32[128,1024]{1,0:T(8,128)}, f32[128,1024]{1,0:T(8,128)}, f32[128,1024]{1,0:T(8,128)}, /*i...) custom-call(s32[4]{0:T(128)} %pad_add_fusion.idx.refs_0_, ...), custom_call_target="tpu_custom_call" | custom-call | tf_op jit(solution)/shard_map/grads/pallas_call | solution.py:281
  46.3 1.2 collective-permute-start.3
  47.5 1.5 %collective-permute-start.4 = (f32[128,1024]{1,0:T(8,128)}, f32[128,1024]{1,0:T(8,128)S(1)}, u32[]{:S(2)}, u32[]{:S(2)}) collective-permute-start(f32[128,1024]{1,0:T(8,128)} %get-tuple-element.44), channel_id=1, source_target_pairs={{0,192},{64,0},{128,64},{192,128},{1,193},{65,1},{129,65},{193,129... | collective-permute-start | bytes 1572872 | tf_op jit(solution)/shard_map/ppermute | solution.py:386
  48.9 1.5 %collective-permute-start.5 = (f32[128,1024]{1,0:T(8,128)}, f32[128,1024]{1,0:T(8,128)S(1)}, u32[]{:S(2)}, u32[]{:S(2)}) collective-permute-start(f32[128,1024]{1,0:T(8,128)} %get-tuple-element.45), channel_id=1, source_target_pairs={{0,128},{64,192},{128,0},{192,64},{1,129},{65,193},{129,1},{193,65... | collective-permute-start | bytes 1572872 | tf_op jit(solution)/shard_map/ppermute | solution.py:386
  50.5 1.9 %collective-permute-start.10 = (f32[128,1024]{1,0:T(8,128)}, f32[128,1024]{1,0:T(8,128)S(1)}, u32[]{:S(2)}, u32[]{:S(2)}) collective-permute-start(f32[128,1024]{1,0:T(8,128)} %get-tuple-element.52), channel_id=1, source_target_pairs={{0,6},{2,0},{4,2},{6,4},{1,7},{3,1},{5,3},{7,5},{8,14},{10,8},{12,... | collective-permute-start | bytes 1572872 | tf_op jit(solution)/shard_map/ppermute | solution.py:386
  52.4 0.8 collective-permute-start.11
  53.2 5.6 %collective-permute-done.3.refs_2_ = f32[128,1024]{1,0:T(8,128)S(1)} collective-permute-done((f32[128,1024]{1,0:T(8,128)}, f32[128,1024]{1,0:T(8,128)S(1)}, u32[]{:S(2)}, u32[]{:S(2)}) %collective-permute-start.3) | collective-permute-done | bytes 524320 | tf_op jit(solution)/shard_map/ppermute | solution.py:386
  58.8 1.6 %collective-permute-start.9 = (f32[128,1024]{1,0:T(8,128)}, f32[128,1024]{1,0:T(8,128)S(1)}, u32[]{:S(2)}, u32[]{:S(2)}) collective-permute-start(f32[128,1024]{1,0:T(8,128)} %get-tuple-element.51), channel_id=1, source_target_pairs={{0,2},{2,4},{4,6},{6,0},{1,3},{3,5},{5,7},{7,1},{8,10},{10,12},{12... | collective-permute-start | bytes 1572872 | tf_op jit(solution)/shard_map/ppermute | solution.py:386
  60.3 0.0 collective-permute-done.4.refs_3_
  60.3 10.6 %collective-permute-done.5.refs_4_ = f32[128,1024]{1,0:T(8,128)S(1)} collective-permute-done((f32[128,1024]{1,0:T(8,128)}, f32[128,1024]{1,0:T(8,128)S(1)}, u32[]{:S(2)}, u32[]{:S(2)}) %collective-permute-start.5) | collective-permute-done | bytes 524320 | tf_op jit(solution)/shard_map/ppermute | solution.py:386
  70.9 0.0 copy-done.6
  71.0 0.0 copy-done.7
  71.0 0.8 copy-done.8
  71.8 3.2 %sums.2 = (f32[32,1024]{1,0:T(8,128)}, f32[32,1024]{1,0:T(8,128)}, f32[32,1024]{1,0:T(8,128)}, f32[32,1024]{1,0:T(8,128)}) custom-call(s32[4]{0:T(128)} %pad_add_fusion.idx.refs_0_, f32[128,1024]{1,0:T(8,128)} %get-tuple-element.42.refs_1_, f32[128,1024]{1,0:T(8,128)} %copy-done.6, f32[128,1024]{1,0:T(8,128)} %copy-done.7, f32[128,1024]{1,0:T(8,128)} %copy-done.8), custom_call_target="tpu_custom_call" | custom-call | tf_op jit(solution)/shard_map/sums/pallas_call | solution.py:342
  74.9 1.6 %collective-permute-start.6 = (f32[32,1024]{1,0:T(8,128)}, f32[32,1024]{1,0:T(8,128)S(1)}, u32[]{:S(2)}, u32[]{:S(2)}) collective-permute-start(f32[32,1024]{1,0:T(8,128)} %get-tuple-element.47), channel_id=1, source_target_pairs={{0,2},{2,4},{4,6},{6,0},{1,3},{3,5},{5,7},{7,1},{8,10},{10,12},{12... | collective-permute-start | bytes 393224 | tf_op jit(solution)/shard_map/ppermute | solution.py:386
  76.5 1.1 collective-permute-start.7
  77.6 0.0 collective-permute-done.10.refs_3_
  77.6 1.9 %collective-permute-start.8 = (f32[32,1024]{1,0:T(8,128)}, f32[32,1024]{1,0:T(8,128)S(1)}, u32[]{:S(2)}, u32[]{:S(2)}) collective-permute-start(f32[32,1024]{1,0:T(8,128)} %get-tuple-element.49), channel_id=1, source_target_pairs={{0,4},{2,6},{4,0},{6,2},{1,5},{3,7},{5,1},{7,3},{8,12},{10,14},{12... | collective-permute-start | bytes 393224 | tf_op jit(solution)/shard_map/ppermute | solution.py:386
  79.5 4.8 %rows.1 = (f32[128,1024]{1,0:T(8,128)}, f32[128,1024]{1,0:T(8,128)}) custom-call(s32[4]{0:T(128)} %pad_add_fusion.idx.refs_0_, bf16[256,1024]{1,0:T(8,128)(2,1)} %get-tuple-element.38.packed, bf16[256,1024]{1,0:T(8,128)(2,1)} %get-tuple-element.39.drive, bf16[512,2048]{1,0:T(8,128)(2,1)} %win_im.3, bf16[512,2048]{1,0:T(8,128)(2,1)} %win_im.3, ...), custom_call_target="tpu_custom_call" | custom-call | tf_op jit(solution)/shard_map/rows/pallas_call | solution.py:318
  84.3 0.0 copy-done.3
  84.3 0.0 collective-permute-done.11.refs_4_
  84.3 0.0 copy-start.4
  84.3 3.6 %collective-permute-start.2 = (f32[128,1024]{1,0:T(8,128)}, f32[128,1024]{1,0:T(8,128)S(1)}, u32[]{:S(2)}, u32[]{:S(2)}) collective-permute-start(f32[128,1024]{1,0:T(8,128)} %get-tuple-element.41), channel_id=1, source_target_pairs={{0,1},{1,0},{2,3},{3,2},{4,5},{5,4},{6,7},{7,6},{8,9},{9,8},{10,11... | collective-permute-start | bytes 1572872 | tf_op jit(solution)/shard_map/ppermute | solution.py:392
  87.9 0.0 collective-permute-done.9.refs_2_
  87.9 0.0 copy-done.4
  87.9 0.8 copy-done.5
  88.7 3.2 %sums.3 = (f32[32,1024]{1,0:T(8,128)}, f32[32,1024]{1,0:T(8,128)}, f32[32,1024]{1,0:T(8,128)}, f32[32,1024]{1,0:T(8,128)}) custom-call(s32[4]{0:T(128)} %pad_add_fusion.idx.refs_0_, f32[128,1024]{1,0:T(8,128)} %get-tuple-element.50.refs_1_, f32[128,1024]{1,0:T(8,128)} %copy-done.5, f32[128,1024]{1,0:T(8,128)} %copy-done.3, f32[128,1024]{1,0:T(8,128)} %copy-done.4), custom_call_target="tpu_custom_call" | custom-call | tf_op jit(solution)/shard_map/sums/pallas_call | solution.py:342
  92.0 0.9 collective-permute-start.12
  92.8 0.0 collective-permute-done.6
  92.8 1.8 %collective-permute-start.13 = (f32[32,1024]{1,0:T(8,128)}, f32[32,1024]{1,0:T(8,128)S(1)}, u32[]{:S(2)}, u32[]{:S(2)}) collective-permute-start(f32[32,1024]{1,0:T(8,128)} %get-tuple-element.56), channel_id=1, source_target_pairs={{0,192},{64,0},{128,64},{192,128},{1,193},{65,1},{129,65},{193,129... | collective-permute-start | bytes 393224 | tf_op jit(solution)/shard_map/ppermute | solution.py:386
  94.6 0.0 collective-permute-done.7
  94.6 0.5 collective-permute-start.14
  95.2 0.0 collective-permute-done.8
  95.2 0.0 copy-done.10
  95.2 3.1 %collective-permute-done.12 = f32[32,1024]{1,0:T(8,128)S(1)} collective-permute-done((f32[32,1024]{1,0:T(8,128)}, f32[32,1024]{1,0:T(8,128)S(1)}, u32[]{:S(2)}, u32[]{:S(2)}) %collective-permute-start.12) | collective-permute-done | bytes 131104 | tf_op jit(solution)/shard_map/ppermute | solution.py:386
  98.3 0.0 collective-permute-done.13
  98.3 2.9 %collective-permute-done.14 = f32[32,1024]{1,0:T(8,128)S(1)} collective-permute-done((f32[32,1024]{1,0:T(8,128)}, f32[32,1024]{1,0:T(8,128)S(1)}, u32[]{:S(2)}, u32[]{:S(2)}) %collective-permute-start.14) | collective-permute-done | bytes 131104 | tf_op jit(solution)/shard_map/ppermute | solution.py:386
  101.3 0.9 add_add_fusion
  102.2 0.8 pad_maximum_fusion
  103.0 3.4 %all-to-all-start.1 = ((f32[8,8,1024]{2,1,0:T(8,128)}), f32[8,8,1024]{2,1,0:T(8,128)S(1)}, u32[]{:S(2)}, u32[]{:S(2)}) async-start(f32[8,8,1024]{2,1,0:T(8,128)} %pad_maximum_fusion), calls=%async_computation.1 | async-start | bytes 524288 | tf_op jit(solution)/shard_map/all_to_all | solution.py:404
  106.4 0.0 copy-done.11
  106.4 0.0 collective-permute-done.2
  106.4 0.0 copy-done
  106.5 0.1 add_convert_fusion
  106.6 10.0 %all-to-all-done.1 = f32[8,8,1024]{2,1,0:T(8,128)S(1)} async-done(((f32[8,8,1024]{2,1,0:T(8,128)}), f32[8,8,1024]{2,1,0:T(8,128)S(1)}, u32[]{:S(2)}, u32[]{:S(2)}) %all-to-all-start.1) | async-done | bytes 262176 | tf_op jit(solution)/shard_map/all_to_all | solution.py:404
  116.6 2.7 %collective-permute-start.15 = (f32[2,2,1024]{2,1,0:T(2,128)S(1)}, f32[2,2,1024]{2,1,0:T(2,128)S(1)}, u32[]{:S(2)}, u32[]{:S(2)}) collective-permute-start(f32[2,2,1024]{2,1,0:T(2,128)S(1)} %dynamic-slice_bitcast_fusion), channel_id=1, source_target_pairs={{0,1},{1,0},{2,3},{3,2},{4,5},{5,4},{6,7},{7,6},{8,9},{9,8},{10,11... | collective-permute-start | bytes 49160 | tf_op jit(solution)/shard_map/ppermute | solution.py:407
  119.3 0.7 slice_bitcast_fusion
  120.0 0.1 collective-permute-done.15
  120.3 0.6 squeeze.29
  120.9 0.6 squeeze.30
  (23 shorter events, 0.3 us)
Async XLA Ops:
  0.6 6.4 %collective-permute-start = (f32[1,128]{1,0:T(1,128)}, f32[1,128]{1,0:T(1,128)S(1)}, u32[]{:S(2)}, u32[]{:S(2)}) collective-permute-start(f32[1,128]{1,0:T(1,128)} %param.9), channel_id=1, source_target_pairs={{0,1},{1,0},{2,3},{3,2},{4,5},{5,4},{6,7},{7,6},{8,9},{9,8},{10,11... | collective-permute-start | bytes 1544 | tf_op jit(solution)/shard_map/ppermute | solution.py:370
  4.9 2.9 %collective-permute-start.1 = (f32[128,1024]{1,0:T(8,128)S(1)}, f32[128,1024]{1,0:T(8,128)S(1)}, u32[]{:S(2)}, u32[]{:S(2)}) collective-permute-start(f32[128,1024]{1,0:T(8,128)S(1)} %maximum_convert_fusion), channel_id=1, source_target_pairs={{0,1},{1,0},{2,3},{3,2},{4,5},{5,4},{6,7},{7,6},{8,9},{9,8},{10,11... | collective-permute-start | bytes 1572872 | tf_op jit(solution)/shard_map/ppermute | solution.py:369
  7.8 0.8 copy-start.9
  46.3 12.5 %collective-permute-start.3 = (f32[128,1024]{1,0:T(8,128)}, f32[128,1024]{1,0:T(8,128)S(1)}, u32[]{:S(2)}, u32[]{:S(2)}) collective-permute-start(f32[128,1024]{1,0:T(8,128)} %get-tuple-element.43), channel_id=1, source_target_pairs={{0,64},{64,128},{128,192},{192,0},{1,65},{65,129},{129,193},{193,1... | collective-permute-start | bytes 1572872 | tf_op jit(solution)/shard_map/ppermute | solution.py:386
  47.5 12.9 %collective-permute-start.4 = (f32[128,1024]{1,0:T(8,128)}, f32[128,1024]{1,0:T(8,128)S(1)}, u32[]{:S(2)}, u32[]{:S(2)}) collective-permute-start(f32[128,1024]{1,0:T(8,128)} %get-tuple-element.44), channel_id=1, source_target_pairs={{0,192},{64,0},{128,64},{192,128},{1,193},{65,1},{129,65},{193,129... | collective-permute-start | bytes 1572872 | tf_op jit(solution)/shard_map/ppermute | solution.py:386
  48.9 22.0 %collective-permute-start.5 = (f32[128,1024]{1,0:T(8,128)}, f32[128,1024]{1,0:T(8,128)S(1)}, u32[]{:S(2)}, u32[]{:S(2)}) collective-permute-start(f32[128,1024]{1,0:T(8,128)} %get-tuple-element.45), channel_id=1, source_target_pairs={{0,128},{64,192},{128,0},{192,64},{1,129},{65,193},{129,1},{193,65... | collective-permute-start | bytes 1572872 | tf_op jit(solution)/shard_map/ppermute | solution.py:386
  50.5 27.1 %collective-permute-start.10 = (f32[128,1024]{1,0:T(8,128)}, f32[128,1024]{1,0:T(8,128)S(1)}, u32[]{:S(2)}, u32[]{:S(2)}) collective-permute-start(f32[128,1024]{1,0:T(8,128)} %get-tuple-element.52), channel_id=1, source_target_pairs={{0,6},{2,0},{4,2},{6,4},{1,7},{3,1},{5,3},{7,5},{8,14},{10,8},{12,... | collective-permute-start | bytes 1572872 | tf_op jit(solution)/shard_map/ppermute | solution.py:386
  52.4 32.0 %collective-permute-start.11 = (f32[128,1024]{1,0:T(8,128)}, f32[128,1024]{1,0:T(8,128)S(1)}, u32[]{:S(2)}, u32[]{:S(2)}) collective-permute-start(f32[128,1024]{1,0:T(8,128)} %get-tuple-element.53), channel_id=1, source_target_pairs={{0,4},{2,6},{4,0},{6,2},{1,5},{3,7},{5,1},{7,3},{8,12},{10,14},{12... | collective-permute-start | bytes 1572872 | tf_op jit(solution)/shard_map/ppermute | solution.py:386
  58.7 12.2 %copy-start.6 = (f32[128,1024]{1,0:T(8,128)}, f32[128,1024]{1,0:T(8,128)S(1)}, u32[]{:S(2)}) copy-start(f32[128,1024]{1,0:T(8,128)S(1)} %collective-permute-done.3.refs_2_) | copy-start | bytes 1572868
  58.8 29.1 %collective-permute-start.9 = (f32[128,1024]{1,0:T(8,128)}, f32[128,1024]{1,0:T(8,128)S(1)}, u32[]{:S(2)}, u32[]{:S(2)}) collective-permute-start(f32[128,1024]{1,0:T(8,128)} %get-tuple-element.51), channel_id=1, source_target_pairs={{0,2},{2,4},{4,6},{6,0},{1,3},{3,5},{5,7},{7,1},{8,10},{10,12},{12... | collective-permute-start | bytes 1572872 | tf_op jit(solution)/shard_map/ppermute | solution.py:386
  60.3 10.6 %copy-start.7 = (f32[128,1024]{1,0:T(8,128)}, f32[128,1024]{1,0:T(8,128)S(1)}, u32[]{:S(2)}) copy-start(f32[128,1024]{1,0:T(8,128)S(1)} %collective-permute-done.4.refs_3_) | copy-start | bytes 1572868
  70.9 0.8 copy-start.8
  74.9 17.9 %collective-permute-start.6 = (f32[32,1024]{1,0:T(8,128)}, f32[32,1024]{1,0:T(8,128)S(1)}, u32[]{:S(2)}, u32[]{:S(2)}) collective-permute-start(f32[32,1024]{1,0:T(8,128)} %get-tuple-element.47), channel_id=1, source_target_pairs={{0,2},{2,4},{4,6},{6,0},{1,3},{3,5},{5,7},{7,1},{8,10},{10,12},{12... | collective-permute-start | bytes 393224 | tf_op jit(solution)/shard_map/ppermute | solution.py:386
  76.5 18.1 %collective-permute-start.7 = (f32[32,1024]{1,0:T(8,128)}, f32[32,1024]{1,0:T(8,128)S(1)}, u32[]{:S(2)}, u32[]{:S(2)}) collective-permute-start(f32[32,1024]{1,0:T(8,128)} %get-tuple-element.48), channel_id=1, source_target_pairs={{0,6},{2,0},{4,2},{6,4},{1,7},{3,1},{5,3},{7,5},{8,14},{10,8},{12,... | collective-permute-start | bytes 393224 | tf_op jit(solution)/shard_map/ppermute | solution.py:386
  77.6 6.7 %copy-start.3 = (f32[128,1024]{1,0:T(8,128)}, f32[128,1024]{1,0:T(8,128)S(1)}, u32[]{:S(2)}) copy-start(f32[128,1024]{1,0:T(8,128)S(1)} %collective-permute-done.10.refs_3_) | copy-start | bytes 1572868
  77.6 17.6 %collective-permute-start.8 = (f32[32,1024]{1,0:T(8,128)}, f32[32,1024]{1,0:T(8,128)S(1)}, u32[]{:S(2)}, u32[]{:S(2)}) collective-permute-start(f32[32,1024]{1,0:T(8,128)} %get-tuple-element.49), channel_id=1, source_target_pairs={{0,4},{2,6},{4,0},{6,2},{1,5},{3,7},{5,1},{7,3},{8,12},{10,14},{12... | collective-permute-start | bytes 393224 | tf_op jit(solution)/shard_map/ppermute | solution.py:386
  84.3 10.9 %copy-start.10 = (f32[32,1024]{1,0:T(8,128)S(1)}, f32[32,1024]{1,0:T(8,128)}, u32[]{:S(2)}) copy-start(f32[32,1024]{1,0:T(8,128)} %get-tuple-element.46) | copy-start | bytes 393220
  84.3 3.6 %copy-start.4 = (f32[128,1024]{1,0:T(8,128)}, f32[128,1024]{1,0:T(8,128)S(1)}, u32[]{:S(2)}) copy-start(f32[128,1024]{1,0:T(8,128)S(1)} %collective-permute-done.11.refs_4_) | copy-start | bytes 1572868
  84.3 22.1 %collective-permute-start.2 = (f32[128,1024]{1,0:T(8,128)}, f32[128,1024]{1,0:T(8,128)S(1)}, u32[]{:S(2)}, u32[]{:S(2)}) collective-permute-start(f32[128,1024]{1,0:T(8,128)} %get-tuple-element.41), channel_id=1, source_target_pairs={{0,1},{1,0},{2,3},{3,2},{4,5},{5,4},{6,7},{7,6},{8,9},{9,8},{10,11... | collective-permute-start | bytes 1572872 | tf_op jit(solution)/shard_map/ppermute | solution.py:392
  87.9 0.8 copy-start.5
  88.7 17.7 %copy-start.11 = (f32[512]{0:T(512)S(1)}, f32[512]{0:T(512)}, u32[]{:S(2)}) copy-start(f32[512]{0:T(512)} %param.14) | copy-start | bytes 6148
  88.7 17.7 %copy-start = (bf16[1,128,512]{2,1,0:T(8,128)(2,1)S(1)}, bf16[1,128,512]{2,1,0:T(8,128)(2,1)}, u32[]{:S(2)}) copy-start(bf16[1,128,512]{2,1,0:T(8,128)(2,1)} %param.8) | copy-start | bytes 393220
  88.7 17.7 %copy-start.1 = (bf16[1,128,512]{2,1,0:T(8,128)(2,1)S(1)}, bf16[1,128,512]{2,1,0:T(8,128)(2,1)}, u32[]{:S(2)}) copy-start(bf16[1,128,512]{2,1,0:T(8,128)(2,1)} %param.15) | copy-start | bytes 393220
  88.7 17.7 %copy-start.2 = (f32[128,1024]{1,0:T(8,128)S(1)}, f32[128,1024]{1,0:T(8,128)}, u32[]{:S(2)}) copy-start(f32[128,1024]{1,0:T(8,128)} %get-tuple-element.40) | copy-start | bytes 1572868
  92.0 6.4 %collective-permute-start.12 = (f32[32,1024]{1,0:T(8,128)}, f32[32,1024]{1,0:T(8,128)S(1)}, u32[]{:S(2)}, u32[]{:S(2)}) collective-permute-start(f32[32,1024]{1,0:T(8,128)} %get-tuple-element.55), channel_id=1, source_target_pairs={{0,64},{64,128},{128,192},{192,0},{1,65},{65,129},{129,193},{193,1... | collective-permute-start | bytes 393224 | tf_op jit(solution)/shard_map/ppermute | solution.py:386
  92.8 5.5 %collective-permute-start.13 = (f32[32,1024]{1,0:T(8,128)}, f32[32,1024]{1,0:T(8,128)S(1)}, u32[]{:S(2)}, u32[]{:S(2)}) collective-permute-start(f32[32,1024]{1,0:T(8,128)} %get-tuple-element.56), channel_id=1, source_target_pairs={{0,192},{64,0},{128,64},{192,128},{1,193},{65,1},{129,65},{193,129... | collective-permute-start | bytes 393224 | tf_op jit(solution)/shard_map/ppermute | solution.py:386
  94.6 6.6 %collective-permute-start.14 = (f32[32,1024]{1,0:T(8,128)}, f32[32,1024]{1,0:T(8,128)S(1)}, u32[]{:S(2)}, u32[]{:S(2)}) collective-permute-start(f32[32,1024]{1,0:T(8,128)} %get-tuple-element.57), channel_id=1, source_target_pairs={{0,128},{64,192},{128,0},{192,64},{1,129},{65,193},{129,1},{193,65... | collective-permute-start | bytes 393224 | tf_op jit(solution)/shard_map/ppermute | solution.py:386
  103.0 13.5 %all-to-all-start.1 = ((f32[8,8,1024]{2,1,0:T(8,128)}), f32[8,8,1024]{2,1,0:T(8,128)S(1)}, u32[]{:S(2)}, u32[]{:S(2)}) async-start(f32[8,8,1024]{2,1,0:T(8,128)} %pad_maximum_fusion), calls=%async_computation.1 | async-start | bytes 524288 | tf_op jit(solution)/shard_map/all_to_all | solution.py:404
  116.6 3.5 %collective-permute-start.15 = (f32[2,2,1024]{2,1,0:T(2,128)S(1)}, f32[2,2,1024]{2,1,0:T(2,128)S(1)}, u32[]{:S(2)}, u32[]{:S(2)}) collective-permute-start(f32[2,2,1024]{2,1,0:T(2,128)S(1)} %dynamic-slice_bitcast_fusion), channel_id=1, source_target_pairs={{0,1},{1,0},{2,3},{3,2},{4,5},{5,4},{6,7},{7,6},{8,9},{9,8},{10,11... | collective-permute-start | bytes 49160 | tf_op jit(solution)/shard_map/ppermute | solution.py:407

commit v2 on v1

v2 whole, which is shorter than its diff:
```python
import jax
import jax.numpy as jnp
import numpy as np
from jax import lax
from jax.experimental import pallas as pl
from jax.experimental.pallas import tpu as pltpu
from jax.sharding import Mesh, PartitionSpec as P


X, Z, Y, C = 4, 8, 4, 2
D, N = 512, 1024
TOK = 128
T = C * TOK
W = N // C
LANES = 128
CH = W // LANES
GROUPS = T // 8
BLOCKS = Z * Y
F32, BF16 = jnp.float32, jnp.bfloat16
NT = (((1,), (1,)), ((), ()))
VMEM = 20 << 20
LOCAL_VMEM = 49 << 20
MSG = 4 * W + LANES


def ring(size, step):
    return [(i, (i + step) % size) for i in range(size)]


def cmul(ar, ai, br, bi):
    return ar * br - ai * bi, ar * bi + ai * br


def rows8():
    return lax.broadcasted_iota(jnp.int32, (8, LANES), 0)


def fwd_factors(d, i):
    dd = d * pltpu.roll(d, 1, 0)
    dddd = dd * pltpu.roll(dd, 2, 0)
    m1 = jnp.where(i >= 1, d, 0.0)
    m2 = jnp.where(i >= 2, dd, 0.0)
    m4 = jnp.where(i >= 4, dddd, 0.0)
    return m1, m2, m4


def cum_fwd(d, i):
    p = d
    for k in (1, 2, 4):
        p = jnp.where(i >= k, p * pltpu.roll(p, k, 0), p)
    return p


def cum_bwd(d, i):
    p = d
    for k in (1, 2, 4):
        p = jnp.where(i < 8 - k, p * pltpu.roll(p, 8 - k, 0), p)
    return p


def bwd_factors(d, i):
    e = pltpu.roll(d, 7, 0)
    ee = e * pltpu.roll(e, 7, 0)
    eeee = ee * pltpu.roll(ee, 6, 0)
    m1 = jnp.where(i < 7, e, 0.0)
    m2 = jnp.where(i < 6, ee, 0.0)
    m4 = jnp.where(i < 4, eeee, 0.0)
    return m1, m2, m4


def scan8(sr, si, masks, powers, backward):
    for (k, m), (pr, pi) in zip(zip((1, 2, 4), masks), powers):
        shift = 8 - k if backward else k
        rr = m * pltpu.roll(sr, shift, 0)
        ri = m * pltpu.roll(si, shift, 0)
        if backward:
            sr, si = sr + (pr * rr + pi * ri), si + (pr * ri - pi * rr)
        else:
            sr, si = sr + (pr * rr - pi * ri), si + (pr * ri + pi * rr)
    return sr, si


def powers_of(par_ref, j):
    lr = jnp.broadcast_to(par_ref[j : j + 1, :], (8, LANES))
    li = jnp.broadcast_to(par_ref[4 + j : 5 + j, :], (8, LANES))
    p1 = (lr, li)
    p2 = cmul(*p1, *p1)
    p4 = cmul(*p2, *p2)
    p8 = cmul(*p4, *p4)
    return p1, p2, p4, p8


def local_kernel(
    idx, par, mine, other, win, wout,
    sig_all, cot_all, fre, fim, bre, bim, msg, damp, weights, sems,
):
    c = idx[0]
    copies = []
    for k in range(4):
        cols = pl.ds(pl.multiple_of((k % 2) * N + c * W, W), W)
        copies.append(
            pltpu.make_async_copy(
                (win, wout)[k // 2].at[:, cols], weights.at[k], sems.at[k]
            )
        )
        copies[k].start()
    own = pl.ds(pl.multiple_of(c * TOK, TOK), TOK)
    oth = pl.ds(pl.multiple_of((1 - c) * TOK, TOK), TOK)
    for at, half in ((own, mine), (oth, other)):
        damp[at, :] = jnp.broadcast_to(half[TOK : TOK + 1, :LANES], (TOK, LANES)).T
        sig_all[at, :] = half[:TOK, :D].astype(BF16)
        cot_all[at, :] = half[:TOK, D:].astype(BF16)
    s = sig_all[...]
    u = cot_all[...]
    for k, (lhs, out) in enumerate(((s, fre), (s, fim), (u, bre), (u, bim))):
        copies[k].wait()
        out[...] = jnp.dot(lhs, weights[k], preferred_element_type=F32)
    i = rows8()
    pw = [powers_of(par, j) for j in range(CH)]
    gam = [jnp.broadcast_to(par[8 + j : 9 + j, :], (8, LANES)) for j in range(CH)]

    def step(g, carry):
        ff, mm, prod = carry
        rf = pl.ds(pl.multiple_of(g * 8, 8), 8)
        rb = pl.ds(pl.multiple_of((GROUPS - 1 - g) * 8, 8), 8)
        df = damp[rf, :]
        db = damp[rb, :]
        mf = fwd_factors(df, i)
        mb = bwd_factors(db, i)
        cf = cum_fwd(df, i)
        cb = cum_bwd(db, i)
        nf, nm = [], []
        for j in range(CH):
            col = pl.ds(j * LANES, LANES)
            p1, p2, p4, p8 = pw[j]
            sr, si = scan8(
                gam[j] * fre[rf, col], gam[j] * fim[rf, col], mf, (p1, p2, p4), False
            )
            fre[rf, col] = sr
            fim[rf, col] = si
            ar, ai = cmul(*p8, *ff[j])
            nf.append((sr + cf * ar, si + cf * ai))
            sr, si = scan8(bre[rb, col], bim[rb, col], mb, (p1, p2, p4), True)
            bre[rb, col] = sr
            bim[rb, col] = si
            vr, vi = cmul(p1[0], -p1[1], sr, si)
            ar, ai = cmul(p8[0], -p8[1], *mm[j])
            nm.append((db * vr + cb * ar, db * vi + cb * ai))
        return nf, nm, prod * cf

    zero = jnp.zeros((8, LANES), F32)
    start = [(zero, zero) for _ in range(CH)]
    ff, mm, prod = lax.fori_loop(0, GROUPS, step, (start, start, zero + 1.0))
    rows = (
        [ff[j][0][7:8] for j in range(CH)]
        + [ff[j][1][7:8] for j in range(CH)]
        + [mm[j][0][0:1] for j in range(CH)]
        + [mm[j][1][0:1] for j in range(CH)]
        + [prod[7:8]]
    )
    for k, row in enumerate(rows):
        msg[:, :, k * LANES : (k + 1) * LANES] = jnp.broadcast_to(
            row[None], (BLOCKS, 1, LANES)
        )


def local_call(idx, par, mine, other, in_weight, out_weight):
    shapes = (
        [((T, D), BF16)] * 2 + [((T, W), F32)] * 4
        + [((BLOCKS, 1, MSG), F32), ((T, LANES), F32)]
    )
    far = pl.BlockSpec(memory_space=pltpu.HBM)
    return pl.pallas_call(
        local_kernel,
        grid_spec=pltpu.PrefetchScalarGridSpec(
            num_scalar_prefetch=1,
            grid=(1,),
            in_specs=[
                whole((16, LANES)), whole((TOK + 8, 2 * D)), whole((TOK + 8, 2 * D)), far, far,
            ],
            out_specs=[whole(s) for s, _ in shapes],
            scratch_shapes=[pltpu.VMEM((4, D, W), BF16), pltpu.SemaphoreType.DMA((4,))],
        ),
        out_shape=[jax.ShapeDtypeStruct(s, t) for s, t in shapes],
        compiler_params=params(LOCAL_VMEM),
        name="local",
    )(idx, par, mine, other, in_weight, out_weight)


def one_hot(order):
    r = lax.broadcasted_iota(jnp.int32, (D, D), 0)
    k = lax.broadcasted_iota(jnp.int32, (D, D), 1)
    hi, mid, z, low = r >> 7, (r >> 5) & 3, (r >> 2) & 7, r & 3
    x, y = (hi, mid) if order == "xy" else (mid, hi)
    old = x * 128 + z * 16 + y * 4 + low
    return jnp.where(old == k, 1.0, 0.0).astype(BF16)


def grads_kernel(
    idx, par, damp, sig, cot, fre, fim, bre, bim, got,
    first, second, packed, drive, lhs_in, lhs_out, sr_, ar_,
):
    x, y, q = idx[1], idx[2], idx[3]
    i = rows8()
    blocks = []
    for j in range(CH):
        pr, pi = powers_of(par, j)[3]
        for _ in range(5):
            pr, pi = cmul(pr, pi, pr, pi)
        blocks.append((pr, pi))

    def row(b, k):
        return jnp.broadcast_to(got[b, :, k * LANES : (k + 1) * LANES], (8, LANES))

    def joined(b, carry):
        ff, mm = carry
        e = BLOCKS - 1 - b
        dec_f, dec_m = row(b, 4 * CH), row(e, 4 * CH)
        nf, nm = [], []
        for j in range(CH):
            pr, pi = blocks[j]
            tr, ti = cmul(dec_f * pr, dec_f * pi, *ff[j])
            on = b < q
            nf.append((
                jnp.where(on, tr + row(b, j), ff[j][0]),
                jnp.where(on, ti + row(b, CH + j), ff[j][1]),
            ))
            tr, ti = cmul(dec_m * pr, -(dec_m * pi), *mm[j])
            on = e > q
            nm.append((
                jnp.where(on, tr + row(e, 2 * CH + j), mm[j][0]),
                jnp.where(on, ti + row(e, 3 * CH + j), mm[j][1]),
            ))
        return nf, nm

    zero = jnp.zeros((8, LANES), F32)
    ff, mm = lax.fori_loop(0, BLOCKS, joined, ([(zero, zero)] * CH, [(zero, zero)] * CH))
    spread = lambda a, j: jnp.broadcast_to(a[j : j + 1, :], (8, LANES))
    tabs, backs, gams, ones = [], [], [], []
    for j in range(CH):
        p1, p2, p4, _ = powers_of(par, j)
        tr, ti = zero8 = (jnp.ones((8, LANES), F32), jnp.zeros((8, LANES), F32))
        for bit, p in ((1, p1), (2, p2), (4, p4)):
            nr, ni = cmul(tr, ti, *p)
            on = (i & bit) != 0
            tr, ti = jnp.where(on, nr, tr), jnp.where(on, ni, ti)
        tabs.append(cmul(tr, ti, *p1))
        tr, ti = zero8
        for bit, p in ((1, p1), (2, p2), (4, p4)):
            nr, ni = cmul(tr, ti, *p)
            on = ((7 - i) & bit) != 0
            tr, ti = jnp.where(on, nr, tr), jnp.where(on, ni, ti)
        backs.append((tr, -ti))
        gams.append(jnp.broadcast_to(par[8 + j : 9 + j, :], (8, LANES)))
        ones.append(p1)

    def step(g, carry):
        ff, mm = carry
        rf = pl.ds(pl.multiple_of(g * 8, 8), 8)
        rb = pl.ds(pl.multiple_of((GROUPS - 1 - g) * 8, 8), 8)
        cf = cum_fwd(damp[rf, :], i)
        db = damp[rb, :]
        e = jnp.where(i < 7, pltpu.roll(db, 7, 0), 1.0)
        cb = cum_bwd(e, i)
        nf, nm = [], []
        for j in range(CH):
            col = pl.ds(j * LANES, LANES)
            colb = pl.ds(W + j * LANES, LANES)
            tr, ti = cmul(*tabs[j], *ff[j])
            sr = fre[rf, col] + cf * tr
            si = fim[rf, col] + cf * ti
            sr_[rf, col] = sr
            sr_[rf, colb] = si
            nf.append((spread(sr, 7), spread(si, 7)))
            tr, ti = cmul(*backs[j], *mm[j])
            vr = bre[rb, col] + cb * tr
            vi = bim[rb, col] + cb * ti
            ar_[rb, col] = gams[j] * vr
            ar_[rb, colb] = gams[j] * vi
            tr, ti = cmul(ones[j][0], -ones[j][1], vr, vi)
            nm.append((spread(db * tr, 0), spread(db * ti, 0)))
        return nf, nm

    lax.fori_loop(0, GROUPS, step, (ff, mm))
    packed[...] = sr_[...].astype(BF16)
    drive[...] = ar_[...].astype(BF16)
    lhs_in[...] = lax.dot_general(
        one_hot("xy"), sig[...], NT, preferred_element_type=F32
    ).astype(BF16)
    lhs_out[...] = lax.dot_general(
        one_hot("yx"), cot[...], NT, preferred_element_type=F32
    ).astype(BF16)
    first[...] = jnp.dot(lhs_in[part(x, 2), :], drive[...], preferred_element_type=F32)
    second[...] = jnp.dot(lhs_out[part(y, 2), :], packed[...], preferred_element_type=F32)


def part(at, d):
    return pl.ds(pl.multiple_of(((at + d) & 3) * 128, 128), 128)


def params(limit=VMEM):
    return pltpu.CompilerParams(vmem_limit_bytes=limit)


def whole(shape):
    return pl.BlockSpec(shape, lambda s, ix: (0,) * len(shape))


def grads_call(idx, par, damp, sig, cot, fre, fim, bre, bim, got):
    shapes = [((128, 2 * W), F32)] * 2 + [((T, 2 * W), BF16)] * 2 + [((D, T), BF16)] * 2
    return pl.pallas_call(
        grads_kernel,
        grid_spec=pltpu.PrefetchScalarGridSpec(
            num_scalar_prefetch=1,
            grid=(1,),
            in_specs=[
                whole((16, LANES)), whole((T, LANES)), whole((T, D)), whole((T, D)),
                whole((T, W)), whole((T, W)), whole((T, W)), whole((T, W)),
                whole((BLOCKS, 1, MSG)),
            ],
            out_specs=[whole(s) for s, _ in shapes],
            scratch_shapes=[pltpu.VMEM((T, 2 * W), F32), pltpu.VMEM((T, 2 * W), F32)],
        ),
        out_shape=[jax.ShapeDtypeStruct(s, t) for s, t in shapes],
        compiler_params=params(),
        name="grads",
    )(idx, par, damp, sig, cot, fre, fim, bre, bim, got)


def second_kernel(idx, packed, drive, lhs_in, lhs_out, first1, second1, first3, second3):
    x, y = idx[1], idx[2]
    for d, first, second in ((1, first1, second1), (3, first3, second3)):
        first[...] = jnp.dot(lhs_in[part(x, d), :], drive[...], preferred_element_type=F32)
        second[...] = jnp.dot(lhs_out[part(y, d), :], packed[...], preferred_element_type=F32)


def second_call(idx, packed, drive, lhs_in, lhs_out):
    return pl.pallas_call(
        second_kernel,
        grid_spec=pltpu.PrefetchScalarGridSpec(
            num_scalar_prefetch=1,
            grid=(1,),
            in_specs=[whole((T, 2 * W)), whole((T, 2 * W)), whole((D, T)), whole((D, T))],
            out_specs=[whole((128, 2 * W))] * 4,
        ),
        out_shape=[jax.ShapeDtypeStruct((128, 2 * W), F32)] * 4,
        compiler_params=params(),
        name="second",
    )(idx, packed, drive, lhs_in, lhs_out)


def rows_kernel(
    idx, packed, drive, lhs_in, lhs_out, win_re, win_im, wout_re, wout_im,
    own, oth, first, second,
):
    c, x, y = idx[0], idx[1], idx[2]
    first[...] = jnp.dot(lhs_in[part(x, 0), :], drive[...], preferred_element_type=F32)
    second[...] = jnp.dot(lhs_out[part(y, 0), :], packed[...], preferred_element_type=F32)
    for out, at in ((own, c), (oth, 1 - c)):
        rows = pl.ds(pl.multiple_of(at * TOK, TOK), TOK)
        out[:, :D] = lax.dot_general(
            packed[rows, :W], wout_re[...], NT, preferred_element_type=F32
        ) + lax.dot_general(packed[rows, W:], wout_im[...], NT, preferred_element_type=F32)
        out[:, D:] = lax.dot_general(
            drive[rows, :W], win_re[...], NT, preferred_element_type=F32
        ) + lax.dot_general(drive[rows, W:], win_im[...], NT, preferred_element_type=F32)


def rows_call(idx, packed, drive, lhs_in, lhs_out, in_weight, out_weight):
    half = lambda k: pl.BlockSpec((D, W), lambda s, ix: (0, k * C + ix[0]))
    return pl.pallas_call(
        rows_kernel,
        grid_spec=pltpu.PrefetchScalarGridSpec(
            num_scalar_prefetch=1,
            grid=(1,),
            in_specs=[
                whole((T, 2 * W)), whole((T, 2 * W)), whole((D, T)), whole((D, T)),
                half(0), half(1), half(0), half(1),
            ],
            out_specs=[whole((TOK, 2 * D))] * 4,
        ),
        out_shape=[jax.ShapeDtypeStruct((TOK, 2 * D), F32)] * 4,
        compiler_params=params(),
        name="rows",
    )(idx, packed, drive, lhs_in, lhs_out, in_weight, in_weight, out_weight, out_weight)


def gathered(parts, at):
    out = []
    for k in range(4):
        first = ((at + k) & 3) * 32
        out.append(sum(lax.dynamic_slice(p, (first, 0), (32, 2 * W)) for p in parts))
    return out


def joined_kernel(a0, a1, a2, a3, b0, b1, b2, b3, out):
    for k, parts in enumerate(((a0, a1, a2, a3), (b0, b1, b2, b3))):
        total = parts[0][...] + parts[1][...] + parts[2][...] + parts[3][...]
        out[:, 4 * k : 4 * k + 4, :] = total.reshape(Z, 4, 2 * W)


def joined_call(one, two):
    return pl.pallas_call(
        joined_kernel,
        out_shape=jax.ShapeDtypeStruct((Z, 8, 2 * W), F32),
        compiler_params=params(),
        name="joined",
    )(*one, *two)


def body(signal, damping, nu_log, theta, in_weight, out_weight, skip_gain, cotangent):
    x, z = lax.axis_index("x"), lax.axis_index("z")
    y, c = lax.axis_index("y"), lax.axis_index("c")
    idx = jnp.stack([c, x, y, z * Y + y]).astype(jnp.int32)
    rate = jnp.exp(nu_log)
    magnitude = jnp.exp(-rate)
    par = jnp.concatenate(
        [magnitude * jnp.cos(theta), magnitude * jnp.sin(theta), jnp.sqrt(-jnp.expm1(-2.0 * rate)), rate]
    ).reshape(4, C, CH, LANES)
    par = lax.dynamic_index_in_dim(par, c, 1, False).reshape(16, LANES)
    sig, cot = signal[0], cotangent[0]
    wide = jnp.concatenate([sig, cot], 1).astype(F32)
    mine = jnp.concatenate([wide, jnp.pad(damping, ((0, 7), (0, 2 * D - TOK)))], 0)
    swap = ring(C, 1)
    other = lax.ppermute(mine, "c", swap)
    sig_all, cot_all, fre, fim, bre, bim, msg, damp = local_call(
        idx, par, mine, other, in_weight, out_weight
    )
    got = lax.all_to_all(msg, ("z", "y"), 0, 0)
    first2, second2, packed, drive, lhs_in, lhs_out = grads_call(
        idx, par, damp, sig_all, cot_all, fre, fim, bre, bim, got
    )

    def hop(part, axis, d):
        return lax.ppermute(part, axis, ring(4, d))

    one, two = [hop(first2, "x", 2)], [hop(second2, "y", 2)]
    first1, second1, first3, second3 = second_call(idx, packed, drive, lhs_in, lhs_out)
    one += [hop(first1, "x", 1), hop(first3, "x", 3)]
    two += [hop(second1, "y", 1), hop(second3, "y", 3)]
    own, oth, first, second = rows_call(
        idx, packed, drive, lhs_in, lhs_out, in_weight, out_weight
    )
    own = own + lax.ppermute(oth, "c", swap)
    gain = jnp.concatenate([skip_gain, skip_gain])
    rows = (own + gain * mine[:TOK]).astype(BF16)
    one = gathered([first] + one, y)
    one = [one[0]] + [hop(one[d], "y", d) for d in (2, 1, 3)]
    two = gathered([second] + two, x)
    two = [two[0]] + [hop(two[d], "x", d) for d in (2, 1, 3)]
    small = joined_call(one, two)
    small = lax.all_to_all(small, "z", 0, 0).sum(0).reshape(2, C, 2, 2 * W)
    keep = lax.dynamic_index_in_dim(small, c, 1, False)
    send = lax.dynamic_index_in_dim(small, 1 - c, 1, False)
    come = lax.ppermute(send, "c", swap)
    first = jnp.where(c == 0, keep, come).reshape(2, 2, 2, 1, W)
    second = jnp.where(c == 0, come, keep).reshape(2, 2, 2, 1, W)
    full = jnp.concatenate([first, second], 3).reshape(2, 2, 2 * N)
    return rows[None, :, :D], rows[None, :, D:], full[0], full[1]


def solution(mesh):
    grid = Mesh(np.asarray(mesh.devices).reshape(X, Z, Y, C), ("x", "z", "y", "c"))
    tm = ("z", "y", "c")
    placed = (P("x", tm, None), P("x", tm), P(), P(), P(), P(), P(), P("x", tm, None))
    rows = P(("x",) + tm, None)

    return jax.shard_map(
        body,
        mesh=grid,
        in_specs=placed,
        out_specs=(P("x", tm, None), P("x", tm, None), rows, rows),
        check_vma=False,
    )
```

time: 122 us -> 114 us (0.934)
  starting transfers between devices: 29.4 us -> 41.4 us
  waiting for transfers between devices: 32.3 us -> 21.2 us
  Pallas kernels: 25.4 us -> 15.1 us
  local copies, waits for them, and re-layouts: 4.62 us -> 7.72 us
  blocking collectives: 23.4 us -> 21.4 us
    ppermute x14 -> x13, waiting for transfers between devices: 22.2 us -> 11 us  [the longest x12 10.3 us: hop(): return lax.ppermute(part, axis, ring(4, d))]
    ppermute x1, starting transfers between devices: 3.58 us -> 13.4 us  [body(): own = own + lax.ppermute(oth, 'c', swap)]
    unnamed x24 -> x26, local copies, waits for them, and re-layouts: 1.65 us -> 5.65 us
    pallas_call x2, Pallas kernels: 6.39 us -> 2.72 us  [the longest x1 1.98 us: second_call(): pl.pallas_call(second_kernel, grid_spec=pltpu.PrefetchScalarGridSpec(num_...]
    pallas_call x1, Pallas kernels: 6.96 us -> 3.93 us  [grads_call(): pl.pallas_call(grads_kernel, grid_spec=pltpu.PrefetchScalarGridSpec(num_s...]
    ppermute x14 -> x13, starting transfers between devices: 19.7 us -> 22 us  [the longest x12 18.7 us: hop(): return lax.ppermute(part, axis, ring(4, d))]
    add x2, other arithmetic: 0.96 us -> 3.12 us  [gathered(): sum((lax.dynamic_slice(p, (first, 0), (32, 2 * W)) for p in parts))]
    all_to_all x1, blocking collectives: 23.4 us -> 21.4 us  [body(): got = lax.all_to_all(msg, ('z', 'y'), 0, 0)]
  transfers between devices with their start and end apart: 17 -> 16, of which waited for: 6 -> 7; matrix products, arithmetic and copies ran while one was open for 5% -> 4% of each run, Pallas kernels for 9% -> 3%
where the time goes in v2:
time: 114 us; the launch traced here: 113 us
  starting transfers between devices  41.4 us (36%)
  blocking collectives  21.4 us (19%)
  waiting for transfers between devices  21.2 us (19%)
  Pallas kernels  15.1 us (13%)
  local copies, waits for them, and re-layouts  7.72 us (7%)
  other arithmetic  5.84 us (5%)
    all_to_all x1, blocking collectives, body(): got = lax.all_to_all(msg, ('z', 'y'), 0, 0)  21.4 us
    ppermute x12, starting transfers between devices, hop(): return lax.ppermute(part, axis, ring(4, d))  18.7 us
    ppermute x1, starting transfers between devices, body(): own = own + lax.ppermute(oth, 'c', swap)  13.4 us
    ppermute x12, waiting for transfers between devices, hop(): return lax.ppermute(part, axis, ring(4, d))  10.3 us
    all_to_all x1, waiting for transfers between devices, body(): small = lax.all_to_all(small, 'z', 0, 0).sum(0).reshape(2, C, 2, 2 * W)  10 us
    unnamed x26, local copies, waits for them, and re-layouts  5.65 us
    pallas_call x1, Pallas kernels, local_call(): pl.pallas_call(local_kernel, grid_spec=pltpu.PrefetchScalarGridSpec(num_s...  5.4 us
    pallas_call x1, Pallas kernels, grads_call(): pl.pallas_call(grads_kernel, grid_spec=pltpu.PrefetchScalarGridSpec(num_s...  3.93 us
  transfers between devices with their start and end apart: 16, of which 7 were waited for; matrix products, arithmetic and copies ran while one was open for 4% of the time, Pallas kernels for 3%

profile of v2, /device:TPU:1, one launch (start us, length us, event | category | flops | bytes accessed | tf_op | source)
XLA Modules:
  0.0 113.4 jit_solution(4210555698902491988)
XLA Ops:
  0.6 1.0 maximum_convert_fusion
  1.7 0.7 select_maximum_fusion.mine
  2.4 3.3 %collective-permute-start = (f32[136,1024]{1,0:T(8,128)S(1)}, f32[136,1024]{1,0:T(8,128)S(1)}, u32[]{:S(2)}, u32[]{:S(2)}) collective-permute-start(f32[136,1024]{1,0:T(8,128)S(1)} %select_maximum_fusion.mine), channel_id=1, source_target_pairs={{0,1},{1,0},{2,3},{3,2},{4,5},{5,4},{6,7},{7,6},{8,9},{9,8},{10,11... | collective-permute-start | bytes 1671176 | tf_op jit(solution)/shard_map/ppermute | solution.py:425
  5.6 0.1 pad_add_fusion.idx
  5.7 0.7 fusion.4
  6.5 0.7 collective-permute-done.other
  7.2 5.4 %local.1 = (bf16[256,512]{1,0:T(8,128)(2,1)S(1)}, bf16[256,512]{1,0:T(8,128)(2,1)S(1)}, f32[256,512]{1,0:T(8,128)S(1)}, f32[256,512]{1,0:T(8,128)S(1)}, f32[256,...) custom-call(s32[4]{0:T(128)S(1)} %pad_add_fusion.idx, ...), custom_call_target="tpu_custom_call" | custom-call | tf_op jit(solution)/shard_map/local/pallas_call | solution.py:173
  12.6 21.4 %all_to_all.10.got = f32[32,1,2176]{2,1,0:T(1,128)S(1)} all-to-all(f32[32,1,2176]{2,1,0:T(1,128)S(1)} %get-tuple-element.33), channel_id=1, replica_groups=mesh['x'=4,'z'=8,'y'=4,'c'=2] {'z','y'}, dimensions={0} | all-to-all | bytes 557056 | tf_op jit(solution)/shard_map/all_to_all | solution.py:429
  34.0 3.9 %grads.1 = (f32[128,1024]{1,0:T(8,128)}, f32[128,1024]{1,0:T(8,128)}, bf16[256,1024]{1,0:T(8,128)(2,1)S(1)}, bf16[256,1024]{1,0:T(8,128)(2,1)S(1)}, bf16[512,256...) custom-call(s32[4]{0:T(128)S(1)} %pad_add_fusion.idx, f32[16,128]{1,0:T(8,128)S(1)} %bitcast.21, ...), custom_call_target="tpu_custom_call" | custom-call | tf_op jit(solution)/shard_map/grads/pallas_call | solution.py:311
  37.9 2.0 %second.1 = (f32[128,1024]{1,0:T(8,128)}, f32[128,1024]{1,0:T(8,128)}, f32[128,1024]{1,0:T(8,128)S(1)}, f32[128,1024]{1,0:T(8,128)}) custom-call(s32[4]{0:T(128)S(1)} %pad_add_fusion.idx, bf16[256,1024]{1,0:T(8,128)(2,1)S(1)} %get-tuple-element.34.packed, bf16[256,1024]{1,0:T(8,128)(2,1)S(1)} %get-tuple-element.35.drive, ...), custom_call_target="tpu_custom_call" | custom-call | tf_op jit(solution)/shard_map/second/pallas_call | solution.py:338
  39.9 0.0 copy-start.2
  39.9 0.7 copy-done.2
  40.6 2.5 %collective-permute-start.4 = (f32[128,1024]{1,0:T(8,128)S(1)}, f32[128,1024]{1,0:T(8,128)S(1)}, u32[]{:S(2)}, u32[]{:S(2)}) collective-permute-start(f32[128,1024]{1,0:T(8,128)S(1)} %get-tuple-element.43), channel_id=1, source_target_pairs={{0,192},{64,0},{128,64},{192,128},{1,193},{65,1},{129,65},{193,129... | collective-permute-start | bytes 1572872 | tf_op jit(solution)/shard_map/ppermute | solution.py:435
  43.1 0.0 collective-permute-start.3
  43.1 1.7 %collective-permute-start.2 = (f32[128,1024]{1,0:T(8,128)}, f32[128,1024]{1,0:T(8,128)}, u32[]{:S(2)}, u32[]{:S(2)}) collective-permute-start(f32[128,1024]{1,0:T(8,128)} %get-tuple-element.41), channel_id=1, source_target_pairs={{0,128},{64,192},{128,0},{192,64},{1,129},{65,193},{129,1},{193,65... | collective-permute-start | bytes 1572872 | tf_op jit(solution)/shard_map/ppermute | solution.py:435
  44.8 1.3 %collective-permute-start.10 = (f32[128,1024]{1,0:T(8,128)}, f32[128,1024]{1,0:T(8,128)}, u32[]{:S(2)}, u32[]{:S(2)}) collective-permute-start(f32[128,1024]{1,0:T(8,128)} %get-tuple-element.47), channel_id=1, source_target_pairs={{0,6},{2,0},{4,2},{6,4},{1,7},{3,1},{5,3},{7,5},{8,14},{10,8},{12,... | collective-permute-start | bytes 1572872 | tf_op jit(solution)/shard_map/ppermute | solution.py:435
  46.1 0.2 collective-permute-start.9
  46.3 6.7 %collective-permute-done.4 = f32[128,1024]{1,0:T(8,128)S(1)} collective-permute-done((f32[128,1024]{1,0:T(8,128)S(1)}, f32[128,1024]{1,0:T(8,128)S(1)}, u32[]{:S(2)}, u32[]{:S(2)}) %collective-permute-start.4) | collective-permute-done | bytes 524320 | tf_op jit(solution)/shard_map/ppermute | solution.py:435
  53.0 0.8 copy-done.10
  53.8 2.0 %collective-permute-start.8 = (f32[128,1024]{1,0:T(8,128)}, f32[128,1024]{1,0:T(8,128)}, u32[]{:S(2)}, u32[]{:S(2)}) collective-permute-start(f32[128,1024]{1,0:T(8,128)} %get-tuple-element.45), channel_id=1, source_target_pairs={{0,4},{2,6},{4,0},{6,2},{1,5},{3,7},{5,1},{7,3},{8,12},{10,14},{12... | collective-permute-start | bytes 1572872 | tf_op jit(solution)/shard_map/ppermute | solution.py:435
  55.8 0.0 copy-done
  55.8 1.6 %copy-done.1 = bf16[512,2048]{1,0:T(8,128)(2,1)S(1)} copy-done((bf16[512,2048]{1,0:T(8,128)(2,1)S(1)}, bf16[512,2048]{1,0:T(8,128)(2,1)}, u32[]{:S(2)}) %copy-start.1) | copy-done | bytes 2097176
  57.4 0.9 copy-done.3
  58.4 3.0 %rows.1 = (f32[128,1024]{1,0:T(8,128)S(1)}, f32[128,1024]{1,0:T(8,128)}, f32[128,1024]{1,0:T(8,128)S(1)}, f32[128,1024]{1,0:T(8,128)S(1)}) custom-call(s32[4]{0:T(128)S(1)} %pad_add_fusion.idx, bf16[256,1024]{1,0:T(8,128)(2,1)S(1)} %get-tuple-element.34.packed, bf16[256,1024]{1,0:T(8,128)(2,1)S(1)} %get-tuple-element.35.drive, ...), custom_call_target="tpu_custom_call" | custom-call | tf_op jit(solution)/shard_map/rows/pallas_call | solution.py:371
  61.4 0.8 copy-done.4
  62.2 0.8 copy-done.6
  63.0 0.0 collective-permute-done.3
  63.0 13.4 %collective-permute-start.1 = (f32[128,1024]{1,0:T(8,128)}, f32[128,1024]{1,0:T(8,128)S(1)}, u32[]{:S(2)}, u32[]{:S(2)}) collective-permute-start(f32[128,1024]{1,0:T(8,128)} %get-tuple-element.39), channel_id=1, source_target_pairs={{0,1},{1,0},{2,3},{3,2},{4,5},{5,4},{6,7},{7,6},{8,9},{9,8},{10,11... | collective-permute-start | bytes 1572872 | tf_op jit(solution)/shard_map/ppermute | solution.py:444
  76.4 0.0 collective-permute-done.2
  76.4 0.0 copy-done.11
  76.4 1.5 %dynamic-slice_add_fusion.4 = (f32[32,1024]{1,0:T(8,128)S(1)}, f32[32,1024]{1,0:T(8,128)S(1)}, f32[32,1024]{1,0:T(8,128)S(1)}, f32[32,1024]{1,0:T(8,128)S(1)}) fusion(f32[128,1024]{1,0:T(8,128)S(1)} %copy-done.11, s32[]{:T(128)S(6)} %select_n.74, f32[128,1024]{1,0:T(8,128)} %collective-permute-done.3, f32[128,1024]{1,0:T(8,128)} %collective-permute-done.2, ...), kind=kLoop, calls=%fused_computation.10 | loop fusion | flops 393216 | bytes 2621456 | tf_op jit(solution)/shard_map/add | solution.py:392
  77.9 1.4 %collective-permute-start.5 = (f32[32,1024]{1,0:T(8,128)S(1)}, f32[32,1024]{1,0:T(8,128)S(1)}, u32[]{:S(2)}, u32[]{:S(2)}) collective-permute-start(f32[32,1024]{1,0:T(8,128)S(1)} %get-tuple-element.54), channel_id=1, source_target_pairs={{0,4},{2,6},{4,0},{6,2},{1,5},{3,7},{5,1},{7,3},{8,12},{10,14},{12... | collective-permute-start | bytes 393224 | tf_op jit(solution)/shard_map/ppermute | solution.py:435
  79.2 0.0 collective-permute-done.10
  79.2 0.0 collective-permute-start.6
  79.3 0.0 collective-permute-done.9
  79.3 2.6 %collective-permute-start.7 = (f32[32,1024]{1,0:T(8,128)S(1)}, f32[32,1024]{1,0:T(8,128)S(1)}, u32[]{:S(2)}, u32[]{:S(2)}) collective-permute-start(f32[32,1024]{1,0:T(8,128)S(1)} %get-tuple-element.52), channel_id=1, source_target_pairs={{0,6},{2,0},{4,2},{6,4},{1,7},{3,1},{5,3},{7,5},{8,14},{10,8},{12,... | collective-permute-start | bytes 393224 | tf_op jit(solution)/shard_map/ppermute | solution.py:435
  81.9 0.0 collective-permute-done.8
  81.9 0.0 copy-done.7
  81.9 0.0 copy-start.8
  82.0 0.0 copy-start.9
  82.0 1.7 %dynamic-slice_add_fusion = (f32[32,1024]{1,0:T(8,128)S(1)}, f32[32,1024]{1,0:T(8,128)S(1)}, f32[32,1024]{1,0:T(8,128)S(1)}, f32[32,1024]{1,0:T(8,128)S(1)}) fusion(f32[128,1024]{1,0:T(8,128)} %collective-permute-done.10, s32[]{:T(128)S(6)} %select_n.78, f32[128,1024]{1,0:T(8,128)} %collective-permute-done.9, f32[128,1024]{1,0:T(8,128)} %collective-permute-done.8, ...), kind=kLoop, calls=%fused_computation.6 | loop fusion | flops 393216 | bytes 2621456 | tf_op jit(solution)/shard_map/add | solution.py:392
  83.6 0.3 collective-permute-start.11
  83.9 0.5 collective-permute-done.5.a1
  84.4 3.4 %collective-permute-start.12 = (f32[32,1024]{1,0:T(8,128)S(1)}, f32[32,1024]{1,0:T(8,128)S(1)}, u32[]{:S(2)}, u32[]{:S(2)}) collective-permute-start(f32[32,1024]{1,0:T(8,128)S(1)} %get-tuple-element.49), channel_id=1, source_target_pairs={{0,64},{64,128},{128,192},{192,0},{1,65},{65,129},{129,193},{193,1... | collective-permute-start | bytes 393224 | tf_op jit(solution)/shard_map/ppermute | solution.py:435
  87.9 0.0 collective-permute-done.6.a2
  87.9 3.2 %collective-permute-start.13 = (f32[32,1024]{1,0:T(8,128)S(1)}, f32[32,1024]{1,0:T(8,128)S(1)}, u32[]{:S(2)}, u32[]{:S(2)}) collective-permute-start(f32[32,1024]{1,0:T(8,128)S(1)} %get-tuple-element.48), channel_id=1, source_target_pairs={{0,192},{64,0},{128,64},{192,128},{1,193},{65,1},{129,65},{193,129... | collective-permute-start | bytes 393224 | tf_op jit(solution)/shard_map/ppermute | solution.py:435
  91.1 0.0 collective-permute-done.7.a3
  91.1 0.0 collective-permute-done.11.b1
  91.1 2.4 %collective-permute-done.12.b2 = f32[32,1024]{1,0:T(8,128)S(1)} collective-permute-done((f32[32,1024]{1,0:T(8,128)S(1)}, f32[32,1024]{1,0:T(8,128)S(1)}, u32[]{:S(2)}, u32[]{:S(2)}) %collective-permute-start.12) | collective-permute-done | bytes 131104 | tf_op jit(solution)/shard_map/ppermute | solution.py:435
  93.5 0.6 collective-permute-done.13.b3
  94.1 0.7 joined.1
  94.8 3.4 %all-to-all-start.1 = ((f32[8,8,1024]{2,1,0:T(8,128)}), f32[8,8,1024]{2,1,0:T(8,128)S(1)}, u32[]{:S(2)}, u32[]{:S(2)}) async-start(f32[8,8,1024]{2,1,0:T(8,128)} %joined.1), calls=%async_computation.1 | async-start | bytes 524288 | tf_op jit(solution)/shard_map/all_to_all | solution.py:452
  98.3 0.0 copy-done.12
  98.3 0.0 collective-permute-done.1
  98.3 0.0 copy-done.5
  98.3 0.0 copy-done.8
  98.3 0.0 copy-done.9
  98.3 0.1 add_convert_fusion
  98.4 10.0 %all-to-all-done.1 = f32[8,8,1024]{2,1,0:T(8,128)S(1)} async-done(((f32[8,8,1024]{2,1,0:T(8,128)}), f32[8,8,1024]{2,1,0:T(8,128)S(1)}, u32[]{:S(2)}, u32[]{:S(2)}) %all-to-all-start.1) | async-done | bytes 262176 | tf_op jit(solution)/shard_map/all_to_all | solution.py:452
  108.5 2.6 %collective-permute-start.14 = (f32[2,2,1024]{2,1,0:T(2,128)S(1)}, f32[2,2,1024]{2,1,0:T(2,128)S(1)}, u32[]{:S(2)}, u32[]{:S(2)}) collective-permute-start(f32[2,2,1024]{2,1,0:T(2,128)S(1)} %dynamic-slice_bitcast_fusion), channel_id=1, source_target_pairs={{0,1},{1,0},{2,3},{3,2},{4,5},{5,4},{6,7},{7,6},{8,9},{9,8},{10,11... | collective-permute-start | bytes 49160 | tf_op jit(solution)/shard_map/ppermute | solution.py:455
  111.2 0.7 slice_bitcast_fusion
  111.9 0.1 collective-permute-done.14
  112.1 0.6 squeeze.25
  112.8 0.6 squeeze.26
  (19 shorter events, 0.2 us)
Async XLA Ops:
  2.4 4.9 %collective-permute-start = (f32[136,1024]{1,0:T(8,128)S(1)}, f32[136,1024]{1,0:T(8,128)S(1)}, u32[]{:S(2)}, u32[]{:S(2)}) collective-permute-start(f32[136,1024]{1,0:T(8,128)S(1)} %select_maximum_fusion.mine), channel_id=1, source_target_pairs={{0,1},{1,0},{2,3},{3,2},{4,5},{5,4},{6,7},{7,6},{8,9},{9,8},{10,11... | collective-permute-start | bytes 1671176 | tf_op jit(solution)/shard_map/ppermute | solution.py:425
  34.0 21.8 %copy-start = (bf16[512,2048]{1,0:T(8,128)(2,1)S(1)}, bf16[512,2048]{1,0:T(8,128)(2,1)}, u32[]{:S(2)}) copy-start(bf16[512,2048]{1,0:T(8,128)(2,1)} %win_im.1) | copy-start | bytes 6291460
  39.9 0.7 copy-start.2
  40.6 12.4 %collective-permute-start.4 = (f32[128,1024]{1,0:T(8,128)S(1)}, f32[128,1024]{1,0:T(8,128)S(1)}, u32[]{:S(2)}, u32[]{:S(2)}) collective-permute-start(f32[128,1024]{1,0:T(8,128)S(1)} %get-tuple-element.43), channel_id=1, source_target_pairs={{0,192},{64,0},{128,64},{192,128},{1,193},{65,1},{129,65},{193,129... | collective-permute-start | bytes 1572872 | tf_op jit(solution)/shard_map/ppermute | solution.py:435
  43.1 19.9 %collective-permute-start.3 = (f32[128,1024]{1,0:T(8,128)}, f32[128,1024]{1,0:T(8,128)}, u32[]{:S(2)}, u32[]{:S(2)}) collective-permute-start(f32[128,1024]{1,0:T(8,128)} %get-tuple-element.42), channel_id=1, source_target_pairs={{0,64},{64,128},{128,192},{192,0},{1,65},{65,129},{129,193},{193,1... | collective-permute-start | bytes 1572872 | tf_op jit(solution)/shard_map/ppermute | solution.py:435
  43.1 33.3 %collective-permute-start.2 = (f32[128,1024]{1,0:T(8,128)}, f32[128,1024]{1,0:T(8,128)}, u32[]{:S(2)}, u32[]{:S(2)}) collective-permute-start(f32[128,1024]{1,0:T(8,128)} %get-tuple-element.41), channel_id=1, source_target_pairs={{0,128},{64,192},{128,0},{192,64},{1,129},{65,193},{129,1},{193,65... | collective-permute-start | bytes 1572872 | tf_op jit(solution)/shard_map/ppermute | solution.py:435
  44.8 34.4 %collective-permute-start.10 = (f32[128,1024]{1,0:T(8,128)}, f32[128,1024]{1,0:T(8,128)}, u32[]{:S(2)}, u32[]{:S(2)}) collective-permute-start(f32[128,1024]{1,0:T(8,128)} %get-tuple-element.47), channel_id=1, source_target_pairs={{0,6},{2,0},{4,2},{6,4},{1,7},{3,1},{5,3},{7,5},{8,14},{10,8},{12,... | collective-permute-start | bytes 1572872 | tf_op jit(solution)/shard_map/ppermute | solution.py:435
  46.1 33.2 %collective-permute-start.9 = (f32[128,1024]{1,0:T(8,128)}, f32[128,1024]{1,0:T(8,128)}, u32[]{:S(2)}, u32[]{:S(2)}) collective-permute-start(f32[128,1024]{1,0:T(8,128)} %get-tuple-element.46), channel_id=1, source_target_pairs={{0,2},{2,4},{4,6},{6,0},{1,3},{3,5},{5,7},{7,1},{8,10},{10,12},{12... | collective-permute-start | bytes 1572872 | tf_op jit(solution)/shard_map/ppermute | solution.py:435
  53.0 0.8 copy-start.10
  53.8 28.1 %collective-permute-start.8 = (f32[128,1024]{1,0:T(8,128)}, f32[128,1024]{1,0:T(8,128)}, u32[]{:S(2)}, u32[]{:S(2)}) collective-permute-start(f32[128,1024]{1,0:T(8,128)} %get-tuple-element.45), channel_id=1, source_target_pairs={{0,4},{2,6},{4,0},{6,2},{1,5},{3,7},{5,1},{7,3},{8,12},{10,14},{12... | collective-permute-start | bytes 1572872 | tf_op jit(solution)/shard_map/ppermute | solution.py:435
  55.8 1.6 %copy-start.1 = (bf16[512,2048]{1,0:T(8,128)(2,1)S(1)}, bf16[512,2048]{1,0:T(8,128)(2,1)}, u32[]{:S(2)}) copy-start(bf16[512,2048]{1,0:T(8,128)(2,1)} %wout_im.1) | copy-start | bytes 6291460
  57.4 0.9 copy-start.3
  58.4 18.0 %copy-start.11 = (f32[128,1024]{1,0:T(8,128)S(1)}, f32[128,1024]{1,0:T(8,128)}, u32[]{:S(2)}) copy-start(f32[128,1024]{1,0:T(8,128)} %copy-done.10) | copy-start | bytes 1572868
  61.4 0.8 copy-start.4
  62.2 0.8 copy-start.6
  63.0 18.9 %copy-start.7 = (f32[128,1024]{1,0:T(8,128)S(1)}, f32[128,1024]{1,0:T(8,128)}, u32[]{:S(2)}) copy-start(f32[128,1024]{1,0:T(8,128)} %copy-done.6) | copy-start | bytes 1572868
  63.0 35.3 %collective-permute-start.1 = (f32[128,1024]{1,0:T(8,128)}, f32[128,1024]{1,0:T(8,128)S(1)}, u32[]{:S(2)}, u32[]{:S(2)}) collective-permute-start(f32[128,1024]{1,0:T(8,128)} %get-tuple-element.39), channel_id=1, source_target_pairs={{0,1},{1,0},{2,3},{3,2},{4,5},{5,4},{6,7},{7,6},{8,9},{9,8},{10,11... | collective-permute-start | bytes 1572872 | tf_op jit(solution)/shard_map/ppermute | solution.py:444
  77.9 6.6 %collective-permute-start.5 = (f32[32,1024]{1,0:T(8,128)S(1)}, f32[32,1024]{1,0:T(8,128)S(1)}, u32[]{:S(2)}, u32[]{:S(2)}) collective-permute-start(f32[32,1024]{1,0:T(8,128)S(1)} %get-tuple-element.54), channel_id=1, source_target_pairs={{0,4},{2,6},{4,0},{6,2},{1,5},{3,7},{5,1},{7,3},{8,12},{10,14},{12... | collective-permute-start | bytes 393224 | tf_op jit(solution)/shard_map/ppermute | solution.py:435
  79.2 8.6 %collective-permute-start.6 = (f32[32,1024]{1,0:T(8,128)S(1)}, f32[32,1024]{1,0:T(8,128)S(1)}, u32[]{:S(2)}, u32[]{:S(2)}) collective-permute-start(f32[32,1024]{1,0:T(8,128)S(1)} %get-tuple-element.53), channel_id=1, source_target_pairs={{0,2},{2,4},{4,6},{6,0},{1,3},{3,5},{5,7},{7,1},{8,10},{10,12},{12... | collective-permute-start | bytes 393224 | tf_op jit(solution)/shard_map/ppermute | solution.py:435
  79.3 11.8 %collective-permute-start.7 = (f32[32,1024]{1,0:T(8,128)S(1)}, f32[32,1024]{1,0:T(8,128)S(1)}, u32[]{:S(2)}, u32[]{:S(2)}) collective-permute-start(f32[32,1024]{1,0:T(8,128)S(1)} %get-tuple-element.52), channel_id=1, source_target_pairs={{0,6},{2,0},{4,2},{6,4},{1,7},{3,1},{5,3},{7,5},{8,14},{10,8},{12,... | collective-permute-start | bytes 393224 | tf_op jit(solution)/shard_map/ppermute | solution.py:435
  81.9 16.3 %copy-start.12 = (f32[512]{0:T(512)S(1)}, f32[512]{0:T(512)}, u32[]{:S(2)}) copy-start(f32[512]{0:T(512)} %param.14) | copy-start | bytes 6148
  81.9 16.4 %copy-start.5 = (f32[128,1024]{1,0:T(8,128)S(1)}, f32[128,1024]{1,0:T(8,128)}, u32[]{:S(2)}) copy-start(f32[128,1024]{1,0:T(8,128)} %copy-done.4) | copy-start | bytes 1572868
  81.9 16.4 %copy-start.8 = (bf16[1,128,512]{2,1,0:T(8,128)(2,1)S(1)}, bf16[1,128,512]{2,1,0:T(8,128)(2,1)}, u32[]{:S(2)}) copy-start(bf16[1,128,512]{2,1,0:T(8,128)(2,1)} %param.15) | copy-start | bytes 393220
  82.0 16.4 %copy-start.9 = (bf16[1,128,512]{2,1,0:T(8,128)(2,1)S(1)}, bf16[1,128,512]{2,1,0:T(8,128)(2,1)}, u32[]{:S(2)}) copy-start(bf16[1,128,512]{2,1,0:T(8,128)(2,1)} %param.8) | copy-start | bytes 393220
  83.6 7.5 %collective-permute-start.11 = (f32[32,1024]{1,0:T(8,128)S(1)}, f32[32,1024]{1,0:T(8,128)S(1)}, u32[]{:S(2)}, u32[]{:S(2)}) collective-permute-start(f32[32,1024]{1,0:T(8,128)S(1)} %get-tuple-element.50), channel_id=1, source_target_pairs={{0,128},{64,192},{128,0},{192,64},{1,129},{65,193},{129,1},{193,65... | collective-permute-start | bytes 393224 | tf_op jit(solution)/shard_map/ppermute | solution.py:435
  84.4 9.1 %collective-permute-start.12 = (f32[32,1024]{1,0:T(8,128)S(1)}, f32[32,1024]{1,0:T(8,128)S(1)}, u32[]{:S(2)}, u32[]{:S(2)}) collective-permute-start(f32[32,1024]{1,0:T(8,128)S(1)} %get-tuple-element.49), channel_id=1, source_target_pairs={{0,64},{64,128},{128,192},{192,0},{1,65},{65,129},{129,193},{193,1... | collective-permute-start | bytes 393224 | tf_op jit(solution)/shard_map/ppermute | solution.py:435
  87.9 6.2 %collective-permute-start.13 = (f32[32,1024]{1,0:T(8,128)S(1)}, f32[32,1024]{1,0:T(8,128)S(1)}, u32[]{:S(2)}, u32[]{:S(2)}) collective-permute-start(f32[32,1024]{1,0:T(8,128)S(1)} %get-tuple-element.48), channel_id=1, source_target_pairs={{0,192},{64,0},{128,64},{192,128},{1,193},{65,1},{129,65},{193,129... | collective-permute-start | bytes 393224 | tf_op jit(solution)/shard_map/ppermute | solution.py:435
  94.8 13.6 %all-to-all-start.1 = ((f32[8,8,1024]{2,1,0:T(8,128)}), f32[8,8,1024]{2,1,0:T(8,128)S(1)}, u32[]{:S(2)}, u32[]{:S(2)}) async-start(f32[8,8,1024]{2,1,0:T(8,128)} %joined.1), calls=%async_computation.1 | async-start | bytes 524288 | tf_op jit(solution)/shard_map/all_to_all | solution.py:452
  108.5 3.5 %collective-permute-start.14 = (f32[2,2,1024]{2,1,0:T(2,128)S(1)}, f32[2,2,1024]{2,1,0:T(2,128)S(1)}, u32[]{:S(2)}, u32[]{:S(2)}) collective-permute-start(f32[2,2,1024]{2,1,0:T(2,128)S(1)} %dynamic-slice_bitcast_fusion), channel_id=1, source_target_pairs={{0,1},{1,0},{2,3},{3,2},{4,5},{5,4},{6,7},{7,6},{8,9},{9,8},{10,11... | collective-permute-start | bytes 49160 | tf_op jit(solution)/shard_map/ppermute | solution.py:455

commit v3 on v2

v3 whole, which is shorter than its diff:
```python
import jax
import jax.numpy as jnp
import numpy as np
from jax import lax
from jax.experimental import pallas as pl
from jax.experimental.pallas import tpu as pltpu
from jax.sharding import Mesh, PartitionSpec as P


X, Z, Y, C = 4, 8, 4, 2
D, N = 512, 1024
TOK = 128
T = C * TOK
W = N // C
H = W // 2
LANES = 128
CH = W // LANES
GROUPS = T // 8
BLOCKS = Z * Y
F32, BF16 = jnp.float32, jnp.bfloat16
NT = (((1,), (1,)), ((), ()))
VMEM = 24 << 20
PAIR_VMEM = 24 << 20
LOCAL_VMEM = 51 << 20
MSG = 4 * W + LANES


def ring(size, step):
    return [(i, (i + step) % size) for i in range(size)]


def cmul(ar, ai, br, bi):
    return ar * br - ai * bi, ar * bi + ai * br


def rows8():
    return lax.broadcasted_iota(jnp.int32, (8, LANES), 0)


def fwd_factors(d, i):
    dd = d * pltpu.roll(d, 1, 0)
    dddd = dd * pltpu.roll(dd, 2, 0)
    m1 = jnp.where(i >= 1, d, 0.0)
    m2 = jnp.where(i >= 2, dd, 0.0)
    m4 = jnp.where(i >= 4, dddd, 0.0)
    return m1, m2, m4


def cum_fwd(d, i):
    p = d
    for k in (1, 2, 4):
        p = jnp.where(i >= k, p * pltpu.roll(p, k, 0), p)
    return p


def cum_bwd(d, i):
    p = d
    for k in (1, 2, 4):
        p = jnp.where(i < 8 - k, p * pltpu.roll(p, 8 - k, 0), p)
    return p


def bwd_factors(d, i):
    e = pltpu.roll(d, 7, 0)
    ee = e * pltpu.roll(e, 7, 0)
    eeee = ee * pltpu.roll(ee, 6, 0)
    m1 = jnp.where(i < 7, e, 0.0)
    m2 = jnp.where(i < 6, ee, 0.0)
    m4 = jnp.where(i < 4, eeee, 0.0)
    return m1, m2, m4


def scan8(sr, si, masks, powers, backward):
    for (k, m), (pr, pi) in zip(zip((1, 2, 4), masks), powers):
        shift = 8 - k if backward else k
        rr = m * pltpu.roll(sr, shift, 0)
        ri = m * pltpu.roll(si, shift, 0)
        if backward:
            sr, si = sr + (pr * rr + pi * ri), si + (pr * ri - pi * rr)
        else:
            sr, si = sr + (pr * rr - pi * ri), si + (pr * ri + pi * rr)
    return sr, si


def powers_of(par_ref, j):
    lr = jnp.broadcast_to(par_ref[j : j + 1, :], (8, LANES))
    li = jnp.broadcast_to(par_ref[4 + j : 5 + j, :], (8, LANES))
    p1 = (lr, li)
    p2 = cmul(*p1, *p1)
    p4 = cmul(*p2, *p2)
    p8 = cmul(*p4, *p4)
    return p1, p2, p4, p8


def local_kernel(
    idx, par, mine, other, win, wout, msg,
    sig_all, cot_all, fre, fim, bre, bim, damp, weights, sems,
):
    c = idx[0]
    copies = []
    for k in range(4):
        cols = pl.ds(pl.multiple_of((k % 2) * N + c * W, W), W)
        copies.append(
            pltpu.make_async_copy(
                (win, wout)[k // 2].at[:, cols], weights.at[k], sems.at[k]
            )
        )
        copies[k].start()
    own = pl.ds(pl.multiple_of(c * TOK, TOK), TOK)
    oth = pl.ds(pl.multiple_of((1 - c) * TOK, TOK), TOK)
    for at, half in ((own, mine), (oth, other)):
        damp[at, :] = jnp.broadcast_to(half[TOK : TOK + 1, :LANES], (TOK, LANES)).T
        sig_all[at, :] = half[:TOK, :D].astype(BF16)
        cot_all[at, :] = half[:TOK, D:].astype(BF16)
    s = sig_all[...]
    u = cot_all[...]
    for k, (lhs, out) in enumerate(((s, fre), (s, fim), (u, bre), (u, bim))):
        copies[k].wait()
        out[...] = jnp.dot(lhs, weights[k], preferred_element_type=F32)
    i = rows8()
    pw = [powers_of(par, j) for j in range(CH)]
    gam = [jnp.broadcast_to(par[8 + j : 9 + j, :], (8, LANES)) for j in range(CH)]

    def step(g, carry):
        ff, mm, prod = carry
        rf = pl.ds(pl.multiple_of(g * 8, 8), 8)
        rb = pl.ds(pl.multiple_of((GROUPS - 1 - g) * 8, 8), 8)
        df = damp[rf, :]
        db = damp[rb, :]
        mf = fwd_factors(df, i)
        mb = bwd_factors(db, i)
        cf = cum_fwd(df, i)
        cb = cum_bwd(db, i)
        nf, nm = [], []
        for j in range(CH):
            col = pl.ds(j * LANES, LANES)
            p1, p2, p4, p8 = pw[j]
            sr, si = scan8(
                gam[j] * fre[rf, col], gam[j] * fim[rf, col], mf, (p1, p2, p4), False
            )
            ar, ai = cmul(*p8, *ff[j])
            nf.append((sr + cf * ar, si + cf * ai))
            sr, si = scan8(bre[rb, col], bim[rb, col], mb, (p1, p2, p4), True)
            vr, vi = cmul(p1[0], -p1[1], sr, si)
            ar, ai = cmul(p8[0], -p8[1], *mm[j])
            nm.append((db * vr + cb * ar, db * vi + cb * ai))
        return nf, nm, prod * cf

    zero = jnp.zeros((8, LANES), F32)
    start = [(zero, zero) for _ in range(CH)]
    ff, mm, prod = lax.fori_loop(0, GROUPS, step, (start, start, zero + 1.0), unroll=2)
    rows = (
        [ff[j][0][7:8] for j in range(CH)]
        + [ff[j][1][7:8] for j in range(CH)]
        + [mm[j][0][0:1] for j in range(CH)]
        + [mm[j][1][0:1] for j in range(CH)]
        + [prod[7:8]]
    )
    for k, row in enumerate(rows):
        msg[:, :, k * LANES : (k + 1) * LANES] = jnp.broadcast_to(
            row[None], (BLOCKS, 1, LANES)
        )


def local_call(idx, par, mine, other, in_weight, out_weight):
    far = pl.BlockSpec(memory_space=pltpu.HBM)
    return pl.pallas_call(
        local_kernel,
        grid_spec=pltpu.PrefetchScalarGridSpec(
            num_scalar_prefetch=1,
            grid=(1,),
            in_specs=[
                whole((16, LANES)), whole((TOK + 8, 2 * D)), whole((TOK + 8, 2 * D)), far, far,
            ],
            out_specs=whole((BLOCKS, 1, MSG)),
            scratch_shapes=[pltpu.VMEM((T, D), BF16)] * 2
            + [pltpu.VMEM((T, W), F32)] * 4
            + [pltpu.VMEM((T, LANES), F32), pltpu.VMEM((4, D, W), BF16)]
            + [pltpu.SemaphoreType.DMA((4,))],
        ),
        out_shape=jax.ShapeDtypeStruct((BLOCKS, 1, MSG), F32),
        compiler_params=params(LOCAL_VMEM),
        name="local",
    )(idx, par, mine, other, in_weight, out_weight)


def one_hot(order):
    r = lax.broadcasted_iota(jnp.int32, (D, D), 0)
    k = lax.broadcasted_iota(jnp.int32, (D, D), 1)
    z, low = (r >> 3) & 7, r & 7
    x, v = (r >> 7, (r >> 6) & 1) if order == "xy" else ((r >> 6) & 3, r >> 8)
    old = x * 128 + z * 16 + v * 8 + low
    return jnp.where(old == k, 1.0, 0.0).astype(BF16)


def tables(p1, p2, p4, i):
    one = (jnp.ones((8, LANES), F32), jnp.zeros((8, LANES), F32))
    tr, ti = one
    for bit, p in ((1, p1), (2, p2), (4, p4)):
        nr, ni = cmul(tr, ti, *p)
        on = (i & bit) != 0
        tr, ti = jnp.where(on, nr, tr), jnp.where(on, ni, ti)
    up = cmul(tr, ti, *p1)
    tr, ti = one
    for bit, p in ((1, p1), (2, p2), (4, p4)):
        nr, ni = cmul(tr, ti, *p)
        on = ((7 - i) & bit) != 0
        tr, ti = jnp.where(on, nr, tr), jnp.where(on, ni, ti)
    return up, (tr, -ti)


def spread(a, j):
    return jnp.broadcast_to(a[j : j + 1, :], (8, LANES))


def arriving(got, dec, places, blocks, columns):
    def joined(b, carry):
        ff, mm = carry
        e = BLOCKS - 1 - b

        def row(at, k):
            return jnp.broadcast_to(got[at, :, columns(k)], (8, LANES))

        dec_f = jnp.broadcast_to(dec[pl.ds(b, 1), :], (8, LANES))
        dec_m = jnp.broadcast_to(dec[pl.ds(e, 1), :], (8, LANES))
        nf, nm = [], []
        for n, (q, j) in enumerate(places):
            pr, pi = blocks[n]
            tr, ti = cmul(dec_f * pr, dec_f * pi, *ff[n])
            on = b < q
            nf.append((
                jnp.where(on, tr + row(b, (0, j)), ff[n][0]),
                jnp.where(on, ti + row(b, (1, j)), ff[n][1]),
            ))
            tr, ti = cmul(dec_m * pr, -(dec_m * pi), *mm[n])
            on = e > q
            nm.append((
                jnp.where(on, tr + row(e, (2, j)), mm[n][0]),
                jnp.where(on, ti + row(e, (3, j)), mm[n][1]),
            ))
        return nf, nm

    zero = jnp.zeros((8, LANES), F32)
    start = [(zero, zero)] * len(places)
    return lax.fori_loop(0, BLOCKS, joined, (start, start))


def states(
    idx, par, halves, got, dec, win, wout, shift, places,
    packed, drive, sig, cot, damp, fre, fim, bre, bim, sr_, ar_, weights, sems,
    between=lambda: None,
):
    c = idx[0]
    width = fre.shape[1]
    chunks = width // LANES
    copies = []
    for k in range(4):
        first = (k % 2) * N + c * W + shift * LANES
        copies.append(
            pltpu.make_async_copy(
                (win, wout)[k // 2].at[:, pl.ds(pl.multiple_of(first, width), width)],
                weights.at[k], sems.at[k],
            )
        )
        copies[k].start()
    for k, (near, far) in enumerate(halves):
        for half, at in ((near, c), (far, 1 - c)):
            rows = pl.ds(pl.multiple_of(k * T + at * TOK, TOK), TOK)
            damp[rows, :] = jnp.broadcast_to(half[TOK : TOK + 1, :LANES], (TOK, LANES)).T
            sig[rows, :] = half[:TOK, :D].astype(BF16)
            cot[rows, :] = half[:TOK, D:].astype(BF16)
    between()
    for k, (lhs, out) in enumerate(((sig, fre), (sig, fim), (cot, bre), (cot, bim))):
        copies[k].wait()
        out[...] = jnp.dot(lhs[...], weights[k], preferred_element_type=F32)
    i = rows8()
    pw, blocks, tabs, gams = [], [], [], []
    for j in range(chunks):
        take = lambda k: jnp.broadcast_to(par[pl.ds(4 * k + shift + j, 1), :], (8, LANES))
        p1 = (take(0), take(1))
        p2 = cmul(*p1, *p1)
        p4 = cmul(*p2, *p2)
        pr, pi = cmul(*p4, *p4)
        for _ in range(5):
            pr, pi = cmul(pr, pi, pr, pi)
        pw.append((p1, p2, p4))
        blocks.append((pr, pi))
        tabs.append(tables(p1, p2, p4, i))
        gams.append(take(2))

    def columns(k):
        return pl.ds(pl.multiple_of((k[0] * CH + shift + k[1]) * LANES, LANES), LANES)

    ff, mm = arriving(
        got, dec, [(q, j) for q in places for j in range(chunks)],
        blocks * len(places), columns,
    )

    def step(g, carry):
        ff, mm = carry
        nf, nm = [], []
        for k in range(len(places)):
            rf = pl.ds(pl.multiple_of(k * T + g * 8, 8), 8)
            rb = pl.ds(pl.multiple_of(k * T + (GROUPS - 1 - g) * 8, 8), 8)
            df, db = damp[rf, :], damp[rb, :]
            mf, mb = fwd_factors(df, i), bwd_factors(db, i)
            cf = cum_fwd(df, i)
            cb = cum_bwd(jnp.where(i < 7, pltpu.roll(db, 7, 0), 1.0), i)
            for j in range(chunks):
                n = chunks * k + j
                col = pl.ds(j * LANES, LANES)
                colb = pl.ds(width + j * LANES, LANES)
                p1 = pw[j][0]
                sr, si = scan8(
                    gams[j] * fre[rf, col], gams[j] * fim[rf, col], mf, pw[j], False
                )
                tr, ti = cmul(*tabs[j][0], *ff[n])
                sr, si = sr + cf * tr, si + cf * ti
                sr_[rf, col] = sr
                sr_[rf, colb] = si
                nf.append((spread(sr, 7), spread(si, 7)))
                vr, vi = scan8(bre[rb, col], bim[rb, col], mb, pw[j], True)
                tr, ti = cmul(*tabs[j][1], *mm[n])
                vr, vi = vr + cb * tr, vi + cb * ti
                ar_[rb, col] = gams[j] * vr
                ar_[rb, colb] = gams[j] * vi
                tr, ti = cmul(p1[0], -p1[1], vr, vi)
                nm.append((spread(db * tr, 0), spread(db * ti, 0)))
        return nf, nm

    lax.fori_loop(0, GROUPS, step, (ff, mm))
    packed[...] = sr_[...].astype(BF16)
    drive[...] = ar_[...].astype(BF16)


def scratch(tokens, width):
    return (
        [pltpu.VMEM((tokens, D), BF16)] * 2
        + [pltpu.VMEM((tokens, LANES), F32)]
        + [pltpu.VMEM((tokens, width), F32)] * 4
        + [pltpu.VMEM((tokens, 2 * width), F32)] * 2
        + [pltpu.VMEM((4, D, width), BF16), pltpu.SemaphoreType.DMA((4,))]
    )


def pair_kernel(
    idx, par, mine, other, pmine, pother, got, dec, win, wout,
    first, second, packed, drive, lhs_in, lhs_out, *rest,
):
    x, v, w, q = idx[1], idx[2], idx[3], idx[4]
    sig, cot = rest[:2]

    def turned():
        lhs_in[...] = lax.dot_general(
            one_hot("xy"), sig[...], NT, preferred_element_type=F32
        ).astype(BF16)
        lhs_out[...] = lax.dot_general(
            one_hot("yx"), cot[...], NT, preferred_element_type=F32
        ).astype(BF16)

    states(
        idx, par, ((mine, other), (pmine, pother)), got, dec, win, wout, 2 * w, (q, q ^ 1),
        packed, drive, *rest, between=turned,
    )
    second[...] = jnp.dot(lhs_out[side(1 - v), :], packed[...], preferred_element_type=F32)
    first[...] = jnp.dot(lhs_in[part(x, 2), :], drive[...], preferred_element_type=F32)


def part(at, d):
    return pl.ds(pl.multiple_of(((at + d) & 3) * 128, 128), 128)


def side(at):
    return pl.ds(pl.multiple_of(at * 256, 256), 256)


def pair_call(idx, par, mine, other, pmine, pother, got, dec, in_weight, out_weight):
    shapes = [((128, 2 * H), F32), ((256, 2 * H), F32)]
    shapes += [((2 * T, 2 * H), BF16)] * 2 + [((D, 2 * T), BF16)] * 2
    far = pl.BlockSpec(memory_space=pltpu.HBM)
    return pl.pallas_call(
        pair_kernel,
        grid_spec=pltpu.PrefetchScalarGridSpec(
            num_scalar_prefetch=1,
            grid=(1,),
            in_specs=[whole((16, LANES))] + [whole((TOK + 8, 2 * D))] * 4
            + [whole((BLOCKS, 1, MSG)), whole((BLOCKS, LANES)), far, far],
            out_specs=[whole(s) for s, _ in shapes],
            scratch_shapes=scratch(2 * T, H),
        ),
        out_shape=[jax.ShapeDtypeStruct(s, t) for s, t in shapes],
        compiler_params=params(PAIR_VMEM),
        name="pair",
    )(idx, par, mine, other, pmine, pother, got, dec, in_weight, out_weight)


def grads_kernel(idx, par, mine, other, got, dec, win, wout, packed, drive, *rest):
    states(
        idx, par, ((mine, other),), got, dec, win, wout, 0, (idx[4],), packed, drive, *rest
    )


def params(limit=VMEM):
    return pltpu.CompilerParams(vmem_limit_bytes=limit)


def whole(shape):
    return pl.BlockSpec(shape, lambda s, ix: (0,) * len(shape))


def grads_call(idx, par, mine, other, got, dec, in_weight, out_weight):
    far = pl.BlockSpec(memory_space=pltpu.HBM)
    return pl.pallas_call(
        grads_kernel,
        grid_spec=pltpu.PrefetchScalarGridSpec(
            num_scalar_prefetch=1,
            grid=(1,),
            in_specs=[
                whole((16, LANES)), whole((TOK + 8, 2 * D)), whole((TOK + 8, 2 * D)),
                whole((BLOCKS, 1, MSG)), whole((BLOCKS, LANES)), far, far,
            ],
            out_specs=[whole((T, 2 * W))] * 2,
            scratch_shapes=scratch(T, W),
        ),
        out_shape=[jax.ShapeDtypeStruct((T, 2 * W), BF16)] * 2,
        compiler_params=params(),
        name="grads",
    )(idx, par, mine, other, got, dec, in_weight, out_weight)


def second_kernel(idx, drive, lhs_in, first1, first3):
    for d, first in ((1, first1), (3, first3)):
        first[...] = jnp.dot(
            lhs_in[part(idx[1], d), :], drive[...], preferred_element_type=F32
        )


def second_call(idx, drive, lhs_in):
    return pl.pallas_call(
        second_kernel,
        grid_spec=pltpu.PrefetchScalarGridSpec(
            num_scalar_prefetch=1,
            grid=(1,),
            in_specs=[whole((2 * T, 2 * H)), whole((D, 2 * T))],
            out_specs=[whole((128, 2 * H))] * 2,
        ),
        out_shape=[jax.ShapeDtypeStruct((128, 2 * H), F32)] * 2,
        compiler_params=params(),
        name="second",
    )(idx, drive, lhs_in)


def chunk_kernel(idx, packed, drive, lhs_in, lhs_out, first, second):
    first[...] = jnp.dot(lhs_in[part(idx[1], 0), :], drive[...], preferred_element_type=F32)
    second[...] = jnp.dot(lhs_out[side(idx[2]), :], packed[...], preferred_element_type=F32)


def chunk_call(idx, packed, drive, lhs_in, lhs_out):
    shapes = [(128, 2 * H), (256, 2 * H)]
    return pl.pallas_call(
        chunk_kernel,
        grid_spec=pltpu.PrefetchScalarGridSpec(
            num_scalar_prefetch=1,
            grid=(1,),
            in_specs=[whole((2 * T, 2 * H))] * 2 + [whole((D, 2 * T))] * 2,
            out_specs=[whole(s) for s in shapes],
        ),
        out_shape=[jax.ShapeDtypeStruct(s, F32) for s in shapes],
        compiler_params=params(),
        name="chunk",
    )(idx, packed, drive, lhs_in, lhs_out)


def rows_kernel(idx, packed, drive, win_re, win_im, wout_re, wout_im, own, oth):
    c = idx[0]
    for out, at in ((own, c), (oth, 1 - c)):
        rows = pl.ds(pl.multiple_of(at * TOK, TOK), TOK)
        out[:, :D] = lax.dot_general(
            packed[rows, :W], wout_re[...], NT, preferred_element_type=F32
        ) + lax.dot_general(packed[rows, W:], wout_im[...], NT, preferred_element_type=F32)
        out[:, D:] = lax.dot_general(
            drive[rows, :W], win_re[...], NT, preferred_element_type=F32
        ) + lax.dot_general(drive[rows, W:], win_im[...], NT, preferred_element_type=F32)


def rows_call(idx, packed, drive, in_weight, out_weight):
    half = lambda k: pl.BlockSpec((D, W), lambda s, ix: (0, k * C + ix[0]))
    return pl.pallas_call(
        rows_kernel,
        grid_spec=pltpu.PrefetchScalarGridSpec(
            num_scalar_prefetch=1,
            grid=(1,),
            in_specs=[
                whole((T, 2 * W)), whole((T, 2 * W)), half(0), half(1), half(0), half(1),
            ],
            out_specs=[whole((TOK, 2 * D))] * 2,
        ),
        out_shape=[jax.ShapeDtypeStruct((TOK, 2 * D), F32)] * 2,
        compiler_params=params(),
        name="rows",
    )(idx, packed, drive, in_weight, in_weight, out_weight, out_weight)


def gathered(parts, at, count):
    out = []
    for k in range(count):
        first = ((at + k) & (count - 1)) * 64
        out.append(sum(lax.dynamic_slice(p, (first, 0), (64, 2 * H)) for p in parts))
    return out


def joined_kernel(a0, a1, b0, b1, b2, b3, out):
    out[:, 0:4, :] = (a0[...] + a1[...]).reshape(2 * Z, 4, 2 * H)
    total = b0[...] + b1[...] + b2[...] + b3[...]
    out[:, 4:8, :] = total.reshape(2 * Z, 4, 2 * H)


def joined_call(one, two):
    return pl.pallas_call(
        joined_kernel,
        out_shape=jax.ShapeDtypeStruct((2 * Z, 8, 2 * H), F32),
        compiler_params=params(),
        name="joined",
    )(*one, *two)


def tail_kernel(idx, keep, come, grad_in, grad_out):
    c = idx[0]
    for piece, at in ((keep, c), (come, 1 - c)):
        for k, out in enumerate((grad_in, grad_out)):
            for h in range(2):
                for w in range(2):
                    cols = pl.ds(pl.multiple_of(h * N + at * W + w * H, H), H)
                    out[:, cols] = piece[w, k, :, h * H : (h + 1) * H]


def tail_call(idx, keep, come):
    return pl.pallas_call(
        tail_kernel,
        grid_spec=pltpu.PrefetchScalarGridSpec(
            num_scalar_prefetch=1,
            grid=(1,),
            in_specs=[whole((2, 2, 2, 2 * H))] * 2,
            out_specs=[whole((2, 2 * N))] * 2,
        ),
        out_shape=[jax.ShapeDtypeStruct((2, 2 * N), F32)] * 2,
        compiler_params=params(),
        name="tail",
    )(idx, keep, come)


def body(signal, damping, nu_log, theta, in_weight, out_weight, skip_gain, cotangent):
    x, z, v = lax.axis_index("x"), lax.axis_index("z"), lax.axis_index("v")
    w, c = lax.axis_index("w"), lax.axis_index("c")
    idx = jnp.stack([c, x, v, w, z * Y + 2 * v + w]).astype(jnp.int32)
    rate = jnp.exp(nu_log)
    magnitude = jnp.exp(-rate)
    par = jnp.concatenate(
        [magnitude * jnp.cos(theta), magnitude * jnp.sin(theta), jnp.sqrt(-jnp.expm1(-2.0 * rate)), rate]
    ).reshape(4, C, CH, LANES)
    par = lax.dynamic_index_in_dim(par, c, 1, False).reshape(16, LANES)
    sig, cot = signal[0], cotangent[0]
    mine = (
        jnp.pad(sig.astype(F32), ((0, 8), (0, D)))
        + jnp.pad(cot.astype(F32), ((0, 8), (D, 0)))
        + jnp.pad(damping, ((TOK, 7), (0, 2 * D - TOK)))
    )
    swap = ring(C, 1)
    other = lax.ppermute(mine, "c", swap)
    pair = ring(2, 1)
    pmine = lax.ppermute(mine, "w", pair)
    pother = lax.ppermute(other, "w", pair)
    msg = local_call(
        idx, par, mine, other, in_weight, out_weight
    )
    got = lax.all_to_all(msg, ("z", "v", "w"), 0, 0)
    dec = jnp.maximum(got[:, 0, 4 * W :], 0.0)
    first2, far, packed2, drive2, lhs_in, lhs_out = pair_call(
        idx, par, mine, other, pmine, pother, got, dec, in_weight, out_weight
    )

    def hop(piece, axis, size, d):
        return lax.ppermute(piece, axis, ring(size, d))

    two = [hop(far, "v", 2, 1)]
    one = [hop(first2, "x", X, 2)]
    first1, first3 = second_call(idx, drive2, lhs_in)
    one += [hop(first1, "x", X, 1), hop(first3, "x", X, 3)]
    first, second = chunk_call(idx, packed2, drive2, lhs_in, lhs_out)
    two = gathered([second] + two, x, X)
    two = [two[0]] + [hop(two[d], "x", X, d) for d in (2, 1, 3)]
    one = gathered([first] + one, v, 2)
    one = [one[0], hop(one[1], "v", 2, 1)]
    packed, drive = grads_call(idx, par, mine, other, got, dec, in_weight, out_weight)
    own, oth = rows_call(idx, packed, drive, in_weight, out_weight)
    own = own + lax.ppermute(oth, "c", swap)
    gain = jnp.concatenate([skip_gain, skip_gain])
    rows = (own + gain * mine[:TOK]).astype(BF16)
    small = joined_call(one, two)
    small = lax.all_to_all(small, ("z", "w"), 0, 0)
    small = small.reshape(Z, 2, 2, C, 2, 2 * H).sum(0)
    keep = lax.dynamic_index_in_dim(small, c, 2, False)
    send = lax.dynamic_index_in_dim(small, 1 - c, 2, False)
    come = lax.ppermute(send, "c", swap)
    grad_in, grad_out = tail_call(idx, keep, come)
    return rows[None, :, :D], rows[None, :, D:], grad_in, grad_out


def solution(mesh):
    grid = Mesh(np.asarray(mesh.devices).reshape(X, Z, 2, 2, C), ("x", "z", "v", "w", "c"))
    tm = ("z", "v", "w", "c")
    placed = (P("x", tm, None), P("x", tm), P(), P(), P(), P(), P(), P("x", tm, None))
    rows = P(("x",) + tm, None)

    return jax.shard_map(
        body,
        mesh=grid,
        in_specs=placed,
        out_specs=(P("x", tm, None), P("x", tm, None), rows, rows),
        check_vma=False,
    )
```

time: 114 us -> 119 us (1.044)
  blocking collectives: 21.4 us -> 0 us
  waiting for transfers between devices: 21.2 us -> 41.8 us
  Pallas kernels: 15.1 us -> 26.3 us
  starting transfers between devices: 41.4 us -> 37.7 us
  local copies, waits for them, and re-layouts: 7.72 us -> 6.46 us
    all_to_all x1 -> x0, blocking collectives: 21.4 us -> none  [body(): got = lax.all_to_all(msg, ('z', 'y'), 0, 0)]
    all_to_all x1 -> x2, starting transfers between devices: 3.41 us -> 16.4 us  [the longest x1 9.5 us: body(): got = lax.all_to_all(msg, ('z', 'v', 'w'), 0, 0)]
    ppermute x12 -> x10, waiting for transfers between devices: 10.3 us -> 21.9 us  [the longest x1 11.9 us: body(): pother = lax.ppermute(other, 'w', pair)]
    ppermute x1, starting transfers between devices: 13.4 us -> 2.63 us  [body(): own = own + lax.ppermute(oth, 'c', swap)]
    pallas_call x1 -> x4, Pallas kernels: 0.74 us -> 11.4 us  [the longest x1 8.58 us: pair_call(): pl.pallas_call(pair_kernel, grid_spec=pltpu.PrefetchScalarGridSpec(num_sc...]
    all_to_all x1 -> x2, waiting for transfers between devices: 10 us -> 19 us  [the longest x1 10.5 us: body(): got = lax.all_to_all(msg, ('z', 'v', 'w'), 0, 0)]
    ppermute x12 -> x10, starting transfers between devices: 18.7 us -> 11.9 us  [the longest x8 10.4 us: hop(): return lax.ppermute(piece, axis, ring(size, d))]
    pallas_call x1, Pallas kernels: 3.93 us -> 5.32 us  [grads_call(): pl.pallas_call(grads_kernel, grid_spec=pltpu.PrefetchScalarGridSpec(num_s...]
  transfers between devices with their start and end apart: 16 -> 15, of which waited for: 7 -> 10; matrix products, arithmetic and copies ran while one was open for 4% -> 4% of each run, Pallas kernels for 3% -> 10%
where the time goes in v3:
time: 119 us
  waiting for transfers between devices  41.8 us (35%)
  starting transfers between devices  37.7 us (32%)
  Pallas kernels  26.3 us (22%)
  local copies, waits for them, and re-layouts  6.46 us (5%)
  other arithmetic  5.52 us (5%)
    ppermute x1, waiting for transfers between devices, body(): pother = lax.ppermute(other, 'w', pair)  11.9 us
    all_to_all x1, waiting for transfers between devices, body(): got = lax.all_to_all(msg, ('z', 'v', 'w'), 0, 0)  10.5 us
    ppermute x8, starting transfers between devices, hop(): return lax.ppermute(piece, axis, ring(size, d))  10.4 us
    all_to_all x1, starting transfers between devices, body(): got = lax.all_to_all(msg, ('z', 'v', 'w'), 0, 0)  9.5 us
    pallas_call x1, Pallas kernels, pair_call(): pl.pallas_call(pair_kernel, grid_spec=pltpu.PrefetchScalarGridSpec(num_sc...  8.58 us
    all_to_all x1, waiting for transfers between devices, body(): small = lax.all_to_all(small, ('z', 'w'), 0, 0)  8.53 us
    all_to_all x1, starting transfers between devices, body(): small = lax.all_to_all(small, ('z', 'w'), 0, 0)  6.88 us
    ppermute x8, waiting for transfers between devices, hop(): return lax.ppermute(piece, axis, ring(size, d))  5.5 us
  transfers between devices with their start and end apart: 15, of which 10 were waited for; matrix products, arithmetic and copies ran while one was open for 4% of the time, Pallas kernels for 10%

profile of v3, /device:TPU:1, one launch (start us, length us, event | category | flops | bytes accessed | tf_op | source)
XLA Modules:
  0.0 118.7 jit_solution(683773376032755945)
XLA Ops:
  0.6 1.0 pad_add_fusion.mine
  1.7 3.3 %collective-permute-start = (f32[136,1024]{1,0:T(8,128)S(1)}, f32[136,1024]{1,0:T(8,128)S(1)}, u32[]{:S(2)}, u32[]{:S(2)}) collective-permute-start(f32[136,1024]{1,0:T(8,128)S(1)} %pad_add_fusion.mine), channel_id=1, source_target_pairs={{0,1},{1,0},{2,3},{3,2},{4,5},{5,4},{6,7},{7,6},{8,9},{9,8},{10,11... | collective-permute-start | bytes 1671176 | tf_op jit(solution)/shard_map/ppermute | solution.py:569
  5.0 0.1 stack.23.idx
  5.0 0.7 fusion.5
  5.8 0.7 collective-permute-done.other
  6.5 5.2 %local.1 = f32[32,1,2176]{2,1,0:T(1,128)S(1)} custom-call(s32[5]{0:T(128)S(1)} %stack.23.idx, f32[16,128]{1,0:T(8,128)S(1)} %bitcast.23, f32[136,1024]{1,0:T(8,128)S(1)} %pad_add_fusion.mine, f32[136,1024]{1,0:T(8,128)S(1)} %collective-permute-done.other, bf16[512,2048]{1,0:T(8,128)(2,1)} %win.5, bf16[512,2048]{1,0:T(8,128)(2,1)} %wout.5), custom_call_target="tpu_custom_call" | custom-call | tf_op jit(solution)/shard_map/local/pallas_call | solution.py:167
  11.7 0.0 copy-start.7
  11.7 0.7 copy-done.7
  12.4 9.5 %all-to-all-start = ((f32[32,1,2176]{2,1,0:T(1,128)}), f32[32,1,2176]{2,1,0:T(1,128)S(1)}, u32[]{:S(2)}, u32[]{:S(2)}) async-start(f32[32,1,2176]{2,1,0:T(1,128)} %copy-done.7), calls=%async_computation | async-start | bytes 557056 | tf_op jit(solution)/shard_map/all_to_all | solution.py:576
  21.9 1.3 %collective-permute-start.2 = (f32[136,1024]{1,0:T(8,128)S(1)}, f32[136,1024]{1,0:T(8,128)}, u32[]{:S(2)}, u32[]{:S(2)}) collective-permute-start(f32[136,1024]{1,0:T(8,128)S(1)} %pad_add_fusion.mine), channel_id=1, source_target_pairs={{0,2},{2,0},{1,3},{3,1},{4,6},{6,4},{5,7},{7,5},{8,10},{10,8},{9,1... | collective-permute-start | bytes 1671176 | tf_op jit(solution)/shard_map/ppermute | solution.py:571
  23.3 0.2 collective-permute-start.3
  23.5 10.5 %all-to-all-done.got = f32[32,1,2176]{2,1,0:T(1,128)S(1)} async-done(((f32[32,1,2176]{2,1,0:T(1,128)}), f32[32,1,2176]{2,1,0:T(1,128)S(1)}, u32[]{:S(2)}, u32[]{:S(2)}) %all-to-all-start) | async-done | bytes 278560 | tf_op jit(solution)/shard_map/all_to_all | solution.py:576
  34.0 4.5 %collective-permute-done.2.pmine = f32[136,1024]{1,0:T(8,128)} collective-permute-done((f32[136,1024]{1,0:T(8,128)S(1)}, f32[136,1024]{1,0:T(8,128)}, u32[]{:S(2)}, u32[]{:S(2)}) %collective-permute-start.2) | collective-permute-done | bytes 557088 | tf_op jit(solution)/shard_map/ppermute | solution.py:571
  38.5 11.9 %collective-permute-done.3.pother = f32[136,1024]{1,0:T(8,128)} collective-permute-done((f32[136,1024]{1,0:T(8,128)S(1)}, f32[136,1024]{1,0:T(8,128)}, u32[]{:S(2)}, u32[]{:S(2)}) %collective-permute-start.3) | collective-permute-done | bytes 557088 | tf_op jit(solution)/shard_map/ppermute | solution.py:572
  50.4 0.0 copy-done
  50.4 1.6 %copy-done.1 = bf16[512,2048]{1,0:T(8,128)(2,1)S(1)} copy-done((bf16[512,2048]{1,0:T(8,128)(2,1)S(1)}, bf16[512,2048]{1,0:T(8,128)(2,1)}, u32[]{:S(2)}) %copy-start.1) | copy-done | bytes 2097176
  52.0 8.6 %pair.1 = (f32[128,512]{1,0:T(8,128)}, f32[256,512]{1,0:T(8,128)}, bf16[512,512]{1,0:T(8,128)(2,1)S(1)}, bf16[512,512]{1,0:T(8,128)(2,1)S(1)}, bf16[512,512]{1,0...) custom-call(s32[5]{0:T(128)S(1)} %stack.23.idx, f32[16,128]{1,0:T(8,128)S(1)} %bitcast.24, f32[136,1024]{1,0:T(8,128)S(1)} %pad_add_fusion.mine, ...), custom_call_target="tpu_custom_call" | custom-call | tf_op jit(solution)/shard_map/pair/pallas_call | solution.py:381
  60.6 0.0 copy-start.10
  60.6 0.8 copy-done.10
  61.4 2.7 %collective-permute-start.8 = (f32[256,512]{1,0:T(8,128)}, f32[256,512]{1,0:T(8,128)}, u32[]{:S(2)}, u32[]{:S(2)}) collective-permute-start(f32[256,512]{1,0:T(8,128)} %get-tuple-element.33), channel_id=1, source_target_pairs={{0,4},{4,0},{1,5},{5,1},{2,6},{6,2},{3,7},{7,3},{8,12},{12,8},{9,1... | collective-permute-start | bytes 1572872 | tf_op jit(solution)/shard_map/ppermute | solution.py:583
  64.1 1.6 %second.1 = (f32[128,512]{1,0:T(8,128)}, f32[128,512]{1,0:T(8,128)}) custom-call(s32[5]{0:T(128)S(1)} %stack.23.idx, bf16[512,512]{1,0:T(8,128)(2,1)S(1)} %get-tuple-element.25.drive, bf16[512,512]{1,0:T(8,128)(2,1)S(1)} %get-tuple-element.26.lhs_in), custom_call_target="tpu_custom_call" | custom-call | tf_op jit(solution)/shard_map/second/pallas_call | solution.py:439
  65.7 0.0 copy-done.5
  65.7 0.8 copy-done.3
  66.5 0.0 copy-done.8
  66.5 1.2 %collective-permute-start.5 = (f32[128,512]{1,0:T(8,128)}, f32[128,512]{1,0:T(8,128)}, u32[]{:S(2)}, u32[]{:S(2)}) collective-permute-start(f32[128,512]{1,0:T(8,128)} %get-tuple-element.30), channel_id=1, source_target_pairs={{0,64},{64,128},{128,192},{192,0},{1,65},{65,129},{129,193},{193,1... | collective-permute-start | bytes 786440 | tf_op jit(solution)/shard_map/ppermute | solution.py:583
  67.7 1.5 %collective-permute-start.6 = (f32[128,512]{1,0:T(8,128)}, f32[128,512]{1,0:T(8,128)}, u32[]{:S(2)}, u32[]{:S(2)}) collective-permute-start(f32[128,512]{1,0:T(8,128)} %get-tuple-element.31), channel_id=1, source_target_pairs={{0,192},{64,0},{128,64},{192,128},{1,193},{65,1},{129,65},{193,129... | collective-permute-start | bytes 786440 | tf_op jit(solution)/shard_map/ppermute | solution.py:583
  69.2 1.5 %collective-permute-start.4 = (f32[128,512]{1,0:T(8,128)}, f32[128,512]{1,0:T(8,128)}, u32[]{:S(2)}, u32[]{:S(2)}) collective-permute-start(f32[128,512]{1,0:T(8,128)} %get-tuple-element.29), channel_id=1, source_target_pairs={{0,128},{64,192},{128,0},{192,64},{1,129},{65,193},{129,1},{193,65... | collective-permute-start | bytes 786440 | tf_op jit(solution)/shard_map/ppermute | solution.py:583
  70.7 1.6 %copy-done.2 = bf16[512,2048]{1,0:T(8,128)(2,1)S(1)} copy-done((bf16[512,2048]{1,0:T(8,128)(2,1)S(1)}, bf16[512,2048]{1,0:T(8,128)(2,1)}, u32[]{:S(2)}) %copy-start.2) | copy-done | bytes 2097176
  72.3 5.3 %grads.1 = (bf16[256,1024]{1,0:T(8,128)(2,1)S(1)}, bf16[256,1024]{1,0:T(8,128)(2,1)S(1)}) custom-call(s32[5]{0:T(128)S(1)} %stack.23.idx, f32[16,128]{1,0:T(8,128)S(1)} %bitcast.25, f32[136,1024]{1,0:T(8,128)S(1)} %pad_add_fusion.mine, f32[136,1024]{1,0:T(8,128)S(1)} %collective-permute-done.other, f32[32,1,2176]{2,1,0:T(1,128)S(1)} %all-to-all-done.got, ...), custom_call_target="tpu_custom_call" | custom-call | tf_op jit(solution)/shard_map/grads/pallas_call | solution.py:413
  77.6 0.0 copy-start.4
  77.6 0.0 copy-start.6
  77.6 0.0 copy-start.9
  77.7 0.0 copy-start.11
  77.7 2.8 %rows.1 = (f32[128,1024]{1,0:T(8,128)S(1)}, f32[128,1024]{1,0:T(8,128)}) custom-call(s32[5]{0:T(128)S(1)} %stack.23.idx, bf16[256,1024]{1,0:T(8,128)(2,1)S(1)} %get-tuple-element.20.packed, bf16[256,1024]{1,0:T(8,128)(2,1)S(1)} %get-tuple-element.21.drive, bf16[512,2048]{1,0:T(8,128)(2,1)S(1)} %copy-done, bf16[512,2048]{1,0:T(8,128)(2,1)S(1)} %copy-done, ...), custom_call_target="tpu_custom_call" | custom-call | tf_op jit(solution)/shard_map/rows/pallas_call | solution.py:488
  80.5 2.6 %collective-permute-start.1 = (f32[128,1024]{1,0:T(8,128)}, f32[128,1024]{1,0:T(8,128)S(1)}, u32[]{:S(2)}, u32[]{:S(2)}) collective-permute-start(f32[128,1024]{1,0:T(8,128)} %get-tuple-element.23), channel_id=1, source_target_pairs={{0,1},{1,0},{2,3},{3,2},{4,5},{5,4},{6,7},{7,6},{8,9},{9,8},{10,11... | collective-permute-start | bytes 1572872 | tf_op jit(solution)/shard_map/ppermute | solution.py:596
  83.1 0.0 copy-done.4
  83.1 0.9 chunk.1
  84.1 0.0 collective-permute-done.5
  84.1 0.0 collective-permute-done.6
  84.1 0.0 collective-permute-done.4
  84.1 0.0 copy-start.13
  84.1 1.3 %dynamic-slice_add_fusion.4 = (f32[64,512]{1,0:T(8,128)S(1)}, f32[64,512]{1,0:T(8,128)S(1)}) fusion(f32[128,512]{1,0:T(8,128)} %collective-permute-done.6, s32[]{:T(128)S(6)} %select_n.39, f32[128,512]{1,0:T(8,128)} %collective-permute-done.5, f32[128,512]{1,0:T(8,128)} %collective-permute-done.4, f32[128,512]{1,0:T(8,128)S(1)} %get-tuple-element.28, ...), kind=kLoop, calls=%fused_computation.10 | loop fusion | flops 196608 | bytes 1310728 | tf_op jit(solution)/shard_map/add | solution.py:508
  85.4 0.3 collective-permute-start.7
  85.7 0.0 collective-permute-done.8
  85.7 1.2 dynamic-slice_add_fusion
  86.9 0.6 collective-permute-start.10
  87.5 2.4 %collective-permute-start.11 = (f32[64,512]{1,0:T(8,128)S(1)}, f32[64,512]{1,0:T(8,128)S(1)}, u32[]{:S(2)}, u32[]{:S(2)}) collective-permute-start(f32[64,512]{1,0:T(8,128)S(1)} %get-tuple-element.36), channel_id=1, source_target_pairs={{0,192},{64,0},{128,64},{192,128},{1,193},{65,1},{129,65},{193,129... | collective-permute-start | bytes 393224 | tf_op jit(solution)/shard_map/ppermute | solution.py:583
  89.9 0.2 collective-permute-start.9
  90.1 2.0 %collective-permute-done.7.a1 = f32[64,512]{1,0:T(8,128)S(1)} collective-permute-done((f32[64,512]{1,0:T(8,128)S(1)}, f32[64,512]{1,0:T(8,128)S(1)}, u32[]{:S(2)}, u32[]{:S(2)}) %collective-permute-start.7) | collective-permute-done | bytes 131104 | tf_op jit(solution)/shard_map/ppermute | solution.py:583
  92.0 1.1 collective-permute-done.10.b2
  93.2 0.1 collective-permute-done.11.b3
  93.3 2.3 %collective-permute-done.9.b1 = f32[64,512]{1,0:T(8,128)S(1)} collective-permute-done((f32[64,512]{1,0:T(8,128)S(1)}, f32[64,512]{1,0:T(8,128)S(1)}, u32[]{:S(2)}, u32[]{:S(2)}) %collective-permute-start.9) | collective-permute-done | bytes 131104 | tf_op jit(solution)/shard_map/ppermute | solution.py:583
  95.6 0.7 joined.1
  96.3 6.9 %all-to-all-start.1 = ((f32[16,8,512]{2,1,0:T(8,128)}), f32[16,8,512]{2,1,0:T(8,128)S(1)}, u32[]{:S(2)}, u32[]{:S(2)}) async-start(f32[16,8,512]{2,1,0:T(8,128)} %joined.1), calls=%async_computation.1 | async-start | bytes 524288 | tf_op jit(solution)/shard_map/all_to_all | solution.py:600
  103.2 0.0 copy-done.13
  103.2 0.0 collective-permute-done.1
  103.2 1.2 fusion.1
  104.4 8.5 %all-to-all-done.1 = f32[16,8,512]{2,1,0:T(8,128)S(1)} async-done(((f32[16,8,512]{2,1,0:T(8,128)}), f32[16,8,512]{2,1,0:T(8,128)S(1)}, u32[]{:S(2)}, u32[]{:S(2)}) %all-to-all-start.1) | async-done | bytes 262176 | tf_op jit(solution)/shard_map/all_to_all | solution.py:600
  112.9 0.1 reshape.28
  113.1 0.1 reduce_sum.9
  113.2 3.5 %collective-permute-start.12 = (f32[2,2,2,512]{3,2,1,0:T(2,128)S(1)}, f32[2,2,2,512]{3,2,1,0:T(2,128)S(1)}, u32[]{:S(2)}, u32[]{:S(2)}) collective-permute-start(f32[2,2,2,512]{3,2,1,0:T(2,128)S(1)} %get-tuple-element.44), channel_id=1, source_target_pairs={{0,1},{1,0},{2,3},{3,2},{4,5},{5,4},{6,7},{7,6},{8,9},{9,8},{10,11... | collective-permute-start | bytes 49160 | tf_op jit(solution)/shard_map/ppermute | solution.py:604
  116.7 0.7 slice_bitcast_fusion
  117.4 0.1 collective-permute-done.12.come
  117.5 1.2 tail.1
  (16 shorter events, 0.1 us)
Async XLA Ops:
  1.7 4.9 %collective-permute-start = (f32[136,1024]{1,0:T(8,128)S(1)}, f32[136,1024]{1,0:T(8,128)S(1)}, u32[]{:S(2)}, u32[]{:S(2)}) collective-permute-start(f32[136,1024]{1,0:T(8,128)S(1)} %pad_add_fusion.mine), channel_id=1, source_target_pairs={{0,1},{1,0},{2,3},{3,2},{4,5},{5,4},{6,7},{7,6},{8,9},{9,8},{10,11... | collective-permute-start | bytes 1671176 | tf_op jit(solution)/shard_map/ppermute | solution.py:569
  6.5 43.9 %copy-start = (bf16[512,2048]{1,0:T(8,128)(2,1)S(1)}, bf16[512,2048]{1,0:T(8,128)(2,1)}, u32[]{:S(2)}) copy-start(bf16[512,2048]{1,0:T(8,128)(2,1)} %win.5) | copy-start | bytes 6291460
  11.7 0.7 copy-start.7
  12.4 21.6 %all-to-all-start = ((f32[32,1,2176]{2,1,0:T(1,128)}), f32[32,1,2176]{2,1,0:T(1,128)S(1)}, u32[]{:S(2)}, u32[]{:S(2)}) async-start(f32[32,1,2176]{2,1,0:T(1,128)} %copy-done.7), calls=%async_computation | async-start | bytes 557056 | tf_op jit(solution)/shard_map/all_to_all | solution.py:576
  21.9 16.6 %collective-permute-start.2 = (f32[136,1024]{1,0:T(8,128)S(1)}, f32[136,1024]{1,0:T(8,128)}, u32[]{:S(2)}, u32[]{:S(2)}) collective-permute-start(f32[136,1024]{1,0:T(8,128)S(1)} %pad_add_fusion.mine), channel_id=1, source_target_pairs={{0,2},{2,0},{1,3},{3,1},{4,6},{6,4},{5,7},{7,5},{8,10},{10,8},{9,1... | collective-permute-start | bytes 1671176 | tf_op jit(solution)/shard_map/ppermute | solution.py:571
  23.3 27.2 %collective-permute-start.3 = (f32[136,1024]{1,0:T(8,128)S(1)}, f32[136,1024]{1,0:T(8,128)}, u32[]{:S(2)}, u32[]{:S(2)}) collective-permute-start(f32[136,1024]{1,0:T(8,128)S(1)} %collective-permute-done.other), channel_id=1, source_target_pairs={{0,2},{2,0},{1,3},{3,1},{4,6},{6,4},{5,7},{7,5},{8,10},{10,8},{9,1... | collective-permute-start | bytes 1671176 | tf_op jit(solution)/shard_map/ppermute | solution.py:572
  50.4 1.6 %copy-start.1 = (bf16[512,2048]{1,0:T(8,128)(2,1)S(1)}, bf16[512,2048]{1,0:T(8,128)(2,1)}, u32[]{:S(2)}) copy-start(bf16[512,2048]{1,0:T(8,128)(2,1)} %wout.5) | copy-start | bytes 6291460
  60.6 0.8 copy-start.10
  61.4 4.3 %copy-start.5 = (bf16[512,512]{1,0:T(8,128)(2,1)}, bf16[512,512]{1,0:T(8,128)(2,1)S(1)}, u32[]{:S(2)}) copy-start(bf16[512,512]{1,0:T(8,128)(2,1)S(1)} %get-tuple-element.26.lhs_in) | copy-start | bytes 1572868
  61.4 5.1 %copy-start.8 = (bf16[512,512]{1,0:T(8,128)(2,1)}, bf16[512,512]{1,0:T(8,128)(2,1)S(1)}, u32[]{:S(2)}) copy-start(bf16[512,512]{1,0:T(8,128)(2,1)S(1)} %get-tuple-element.24.packed) | copy-start | bytes 1572868
  61.4 24.3 %collective-permute-start.8 = (f32[256,512]{1,0:T(8,128)}, f32[256,512]{1,0:T(8,128)}, u32[]{:S(2)}, u32[]{:S(2)}) collective-permute-start(f32[256,512]{1,0:T(8,128)} %get-tuple-element.33), channel_id=1, source_target_pairs={{0,4},{4,0},{1,5},{5,1},{2,6},{6,2},{3,7},{7,3},{8,12},{12,8},{9,1... | collective-permute-start | bytes 1572872 | tf_op jit(solution)/shard_map/ppermute | solution.py:583
  65.7 0.8 copy-start.3
  66.5 17.6 %collective-permute-start.5 = (f32[128,512]{1,0:T(8,128)}, f32[128,512]{1,0:T(8,128)}, u32[]{:S(2)}, u32[]{:S(2)}) collective-permute-start(f32[128,512]{1,0:T(8,128)} %get-tuple-element.30), channel_id=1, source_target_pairs={{0,64},{64,128},{128,192},{192,0},{1,65},{65,129},{129,193},{193,1... | collective-permute-start | bytes 786440 | tf_op jit(solution)/shard_map/ppermute | solution.py:583
  67.7 16.4 %collective-permute-start.6 = (f32[128,512]{1,0:T(8,128)}, f32[128,512]{1,0:T(8,128)}, u32[]{:S(2)}, u32[]{:S(2)}) collective-permute-start(f32[128,512]{1,0:T(8,128)} %get-tuple-element.31), channel_id=1, source_target_pairs={{0,192},{64,0},{128,64},{192,128},{1,193},{65,1},{129,65},{193,129... | collective-permute-start | bytes 786440 | tf_op jit(solution)/shard_map/ppermute | solution.py:583
  69.2 14.9 %collective-permute-start.4 = (f32[128,512]{1,0:T(8,128)}, f32[128,512]{1,0:T(8,128)}, u32[]{:S(2)}, u32[]{:S(2)}) collective-permute-start(f32[128,512]{1,0:T(8,128)} %get-tuple-element.29), channel_id=1, source_target_pairs={{0,128},{64,192},{128,0},{192,64},{1,129},{65,193},{129,1},{193,65... | collective-permute-start | bytes 786440 | tf_op jit(solution)/shard_map/ppermute | solution.py:583
  70.7 1.6 %copy-start.2 = (bf16[512,2048]{1,0:T(8,128)(2,1)S(1)}, bf16[512,2048]{1,0:T(8,128)(2,1)}, u32[]{:S(2)}) copy-start(bf16[512,2048]{1,0:T(8,128)(2,1)} %wout.5) | copy-start | bytes 6291460
  77.6 5.5 %copy-start.4 = (bf16[512,512]{1,0:T(8,128)(2,1)S(1)}, bf16[512,512]{1,0:T(8,128)(2,1)}, u32[]{:S(2)}) copy-start(bf16[512,512]{1,0:T(8,128)(2,1)} %copy-done.3) | copy-start | bytes 1572868
  77.6 5.5 %copy-start.6 = (bf16[512,512]{1,0:T(8,128)(2,1)S(1)}, bf16[512,512]{1,0:T(8,128)(2,1)}, u32[]{:S(2)}) copy-start(bf16[512,512]{1,0:T(8,128)(2,1)} %copy-done.5) | copy-start | bytes 1572868
  77.6 5.5 %copy-start.9 = (bf16[512,512]{1,0:T(8,128)(2,1)S(1)}, bf16[512,512]{1,0:T(8,128)(2,1)}, u32[]{:S(2)}) copy-start(bf16[512,512]{1,0:T(8,128)(2,1)} %copy-done.8) | copy-start | bytes 1572868
  77.7 5.5 %copy-start.11 = (bf16[512,512]{1,0:T(8,128)(2,1)S(1)}, bf16[512,512]{1,0:T(8,128)(2,1)}, u32[]{:S(2)}) copy-start(bf16[512,512]{1,0:T(8,128)(2,1)} %copy-done.10) | copy-start | bytes 1572868
  80.5 6.4 %copy-start.12 = (f32[128,1024]{1,0:T(8,128)}, f32[128,1024]{1,0:T(8,128)S(1)}, u32[]{:S(2)}) copy-start(f32[128,1024]{1,0:T(8,128)S(1)} %get-tuple-element.22) | copy-start | bytes 1572868
  80.5 22.7 %collective-permute-start.1 = (f32[128,1024]{1,0:T(8,128)}, f32[128,1024]{1,0:T(8,128)S(1)}, u32[]{:S(2)}, u32[]{:S(2)}) collective-permute-start(f32[128,1024]{1,0:T(8,128)} %get-tuple-element.23), channel_id=1, source_target_pairs={{0,1},{1,0},{2,3},{3,2},{4,5},{5,4},{6,7},{7,6},{8,9},{9,8},{10,11... | collective-permute-start | bytes 1572872 | tf_op jit(solution)/shard_map/ppermute | solution.py:596
  84.1 19.1 %copy-start.13 = (f32[512]{0:T(512)S(1)}, f32[512]{0:T(512)}, u32[]{:S(2)}) copy-start(f32[512]{0:T(512)} %param.14) | copy-start | bytes 6148
  85.4 6.6 %collective-permute-start.7 = (f32[64,512]{1,0:T(8,128)S(1)}, f32[64,512]{1,0:T(8,128)S(1)}, u32[]{:S(2)}, u32[]{:S(2)}) collective-permute-start(f32[64,512]{1,0:T(8,128)S(1)} %get-tuple-element.40), channel_id=1, source_target_pairs={{0,4},{4,0},{1,5},{5,1},{2,6},{6,2},{3,7},{7,3},{8,12},{12,8},{9,1... | collective-permute-start | bytes 393224 | tf_op jit(solution)/shard_map/ppermute | solution.py:583
  86.9 6.2 %collective-permute-start.10 = (f32[64,512]{1,0:T(8,128)S(1)}, f32[64,512]{1,0:T(8,128)S(1)}, u32[]{:S(2)}, u32[]{:S(2)}) collective-permute-start(f32[64,512]{1,0:T(8,128)S(1)} %get-tuple-element.37), channel_id=1, source_target_pairs={{0,64},{64,128},{128,192},{192,0},{1,65},{65,129},{129,193},{193,1... | collective-permute-start | bytes 393224 | tf_op jit(solution)/shard_map/ppermute | solution.py:583
  87.5 5.8 %collective-permute-start.11 = (f32[64,512]{1,0:T(8,128)S(1)}, f32[64,512]{1,0:T(8,128)S(1)}, u32[]{:S(2)}, u32[]{:S(2)}) collective-permute-start(f32[64,512]{1,0:T(8,128)S(1)} %get-tuple-element.36), channel_id=1, source_target_pairs={{0,192},{64,0},{128,64},{192,128},{1,193},{65,1},{129,65},{193,129... | collective-permute-start | bytes 393224 | tf_op jit(solution)/shard_map/ppermute | solution.py:583
  89.9 5.7 %collective-permute-start.9 = (f32[64,512]{1,0:T(8,128)S(1)}, f32[64,512]{1,0:T(8,128)S(1)}, u32[]{:S(2)}, u32[]{:S(2)}) collective-permute-start(f32[64,512]{1,0:T(8,128)S(1)} %get-tuple-element.38), channel_id=1, source_target_pairs={{0,128},{64,192},{128,0},{192,64},{1,129},{65,193},{129,1},{193,65... | collective-permute-start | bytes 393224 | tf_op jit(solution)/shard_map/ppermute | solution.py:583
  96.3 16.6 %all-to-all-start.1 = ((f32[16,8,512]{2,1,0:T(8,128)}), f32[16,8,512]{2,1,0:T(8,128)S(1)}, u32[]{:S(2)}, u32[]{:S(2)}) async-start(f32[16,8,512]{2,1,0:T(8,128)} %joined.1), calls=%async_computation.1 | async-start | bytes 524288 | tf_op jit(solution)/shard_map/all_to_all | solution.py:600
  113.2 4.3 %collective-permute-start.12 = (f32[2,2,2,512]{3,2,1,0:T(2,128)S(1)}, f32[2,2,2,512]{3,2,1,0:T(2,128)S(1)}, u32[]{:S(2)}, u32[]{:S(2)}) collective-permute-start(f32[2,2,2,512]{3,2,1,0:T(2,128)S(1)} %get-tuple-element.44), channel_id=1, source_target_pairs={{0,1},{1,0},{2,3},{3,2},{4,5},{5,4},{6,7},{7,6},{8,9},{9,8},{10,11... | collective-permute-start | bytes 49160 | tf_op jit(solution)/shard_map/ppermute | solution.py:604

commit v4 on v3

--- a/solution.py
+++ b/solution.py
@@ -394,10 +394,18 @@
     )(idx, par, mine, other, pmine, pother, got, dec, in_weight, out_weight)
 
 
-def grads_kernel(idx, par, mine, other, got, dec, win, wout, packed, drive, *rest):
+def grads_kernel(idx, par, mine, other, got, dec, win, wout, own, oth, packed, drive, *rest):
     states(
         idx, par, ((mine, other),), got, dec, win, wout, 0, (idx[4],), packed, drive, *rest
     )
+    weights = rest[-2]
+    for out, at in ((own, idx[0]), (oth, 1 - idx[0])):
+        rows = pl.ds(pl.multiple_of(at * TOK, TOK), TOK)
+        for k, (lhs, cols) in enumerate(((packed, pl.ds(0, D)), (drive, pl.ds(D, D)))):
+            re, im = (weights[2], weights[3]) if k == 0 else (weights[0], weights[1])
+            out[:, cols] = lax.dot_general(
+                lhs[rows, :W], re, NT, preferred_element_type=F32
+            ) + lax.dot_general(lhs[rows, W:], im, NT, preferred_element_type=F32)
 
 
 def params(limit=VMEM):
@@ -419,46 +427,29 @@
                 whole((16, LANES)), whole((TOK + 8, 2 * D)), whole((TOK + 8, 2 * D)),
                 whole((BLOCKS, 1, MSG)), whole((BLOCKS, LANES)), far, far,
             ],
-            out_specs=[whole((T, 2 * W))] * 2,
-            scratch_shapes=scratch(T, W),
+            out_specs=[whole((TOK, 2 * D))] * 2,
+            scratch_shapes=[pltpu.VMEM((T, 2 * W), BF16)] * 2 + scratch(T, W),
         ),
-        out_shape=[jax.ShapeDtypeStruct((T, 2 * W), BF16)] * 2,
+        out_shape=[jax.ShapeDtypeStruct((TOK, 2 * D), F32)] * 2,
         compiler_params=params(),
         name="grads",
     )(idx, par, mine, other, got, dec, in_weight, out_weight)
 
 
-def second_kernel(idx, drive, lhs_in, first1, first3):
-    for d, first in ((1, first1), (3, first3)):
-        first[...] = jnp.dot(
+def second_kernel(
+    idx, packed, drive, lhs_in, lhs_out, first1, first3, first, second,
+):
+    for d, out in ((1, first1), (3, first3), (0, first)):
+        out[...] = jnp.dot(
             lhs_in[part(idx[1], d), :], drive[...], preferred_element_type=F32
         )
-
-
-def second_call(idx, drive, lhs_in):
+    second[...] = jnp.dot(lhs_out[side(idx[2]), :], packed[...], preferred_element_type=F32)
+
+
+def second_call(idx, packed, drive, lhs_in, lhs_out):
+    shapes = [(128, 2 * H)] * 3 + [(256, 2 * H)]
     return pl.pallas_call(
         second_kernel,
-        grid_spec=pltpu.PrefetchScalarGridSpec(
-            num_scalar_prefetch=1,
-            grid=(1,),
-            in_specs=[whole((2 * T, 2 * H)), whole((D, 2 * T))],
-            out_specs=[whole((128, 2 * H))] * 2,
-        ),
-        out_shape=[jax.ShapeDtypeStruct((128, 2 * H), F32)] * 2,
-        compiler_params=params(),
-        name="second",
-    )(idx, drive, lhs_in)
-
-
-def chunk_kernel(idx, packed, drive, lhs_in, lhs_out, first, second):
-    first[...] = jnp.dot(lhs_in[part(idx[1], 0), :], drive[...], preferred_element_type=F32)
-    second[...] = jnp.dot(lhs_out[side(idx[2]), :], packed[...], preferred_element_type=F32)
-
-
-def chunk_call(idx, packed, drive, lhs_in, lhs_out):
-    shapes = [(128, 2 * H), (256, 2 * H)]
-    return pl.pallas_call(
-        chunk_kernel,
         grid_spec=pltpu.PrefetchScalarGridSpec(
             num_scalar_prefetch=1,
             grid=(1,),
@@ -467,38 +458,8 @@
         ),
         out_shape=[jax.ShapeDtypeStruct(s, F32) for s in shapes],
         compiler_params=params(),
-        name="chunk",
+        name="second",
     )(idx, packed, drive, lhs_in, lhs_out)
-
-
-def rows_kernel(idx, packed, drive, win_re, win_im, wout_re, wout_im, own, oth):
-    c = idx[0]
-    for out, at in ((own, c), (oth, 1 - c)):
-        rows = pl.ds(pl.multiple_of(at * TOK, TOK), TOK)
-        out[:, :D] = lax.dot_general(
-            packed[rows, :W], wout_re[...], NT, preferred_element_type=F32
-        ) + lax.dot_general(packed[rows, W:], wout_im[...], NT, preferred_element_type=F32)
-        out[:, D:] = lax.dot_general(
-            drive[rows, :W], win_re[...], NT, preferred_element_type=F32
-        ) + lax.dot_general(drive[rows, W:], win_im[...], NT, preferred_element_type=F32)
-
-
-def rows_call(idx, packed, drive, in_weight, out_weight):
-    half = lambda k: pl.BlockSpec((D, W), lambda s, ix: (0, k * C + ix[0]))
-    return pl.pallas_call(
-        rows_kernel,
-        grid_spec=pltpu.PrefetchScalarGridSpec(
-            num_scalar_prefetch=1,
-            grid=(1,),
-            in_specs=[
-                whole((T, 2 * W)), whole((T, 2 * W)), half(0), half(1), half(0), half(1),
-            ],
-            out_specs=[whole((TOK, 2 * D))] * 2,
-        ),
-        out_shape=[jax.ShapeDtypeStruct((TOK, 2 * D), F32)] * 2,
-        compiler_params=params(),
-        name="rows",
-    )(idx, packed, drive, in_weight, in_weight, out_weight, out_weight)
 
 
 def gathered(parts, at, count):
@@ -584,15 +545,13 @@
 
     two = [hop(far, "v", 2, 1)]
     one = [hop(first2, "x", X, 2)]
-    first1, first3 = second_call(idx, drive2, lhs_in)
+    first1, first3, first, second = second_call(idx, packed2, drive2, lhs_in, lhs_out)
     one += [hop(first1, "x", X, 1), hop(first3, "x", X, 3)]
-    first, second = chunk_call(idx, packed2, drive2, lhs_in, lhs_out)
     two = gathered([second] + two, x, X)
     two = [two[0]] + [hop(two[d], "x", X, d) for d in (2, 1, 3)]
     one = gathered([first] + one, v, 2)
     one = [one[0], hop(one[1], "v", 2, 1)]
-    packed, drive = grads_call(idx, par, mine, other, got, dec, in_weight, out_weight)
-    own, oth = rows_call(idx, packed, drive, in_weight, out_weight)
+    own, oth = grads_call(idx, par, mine, other, got, dec, in_weight, out_weight)
     own = own + lax.ppermute(oth, "c", swap)
     gain = jnp.concatenate([skip_gain, skip_gain])
     rows = (own + gain * mine[:TOK]).astype(BF16)

time: 119 us -> 119 us (level)
  Pallas kernels: 26.3 us -> 24.8 us
    pallas_call x2 -> x0, Pallas kernels: 3.75 us -> none  [the longest x1 2.84 us: rows_call(): pl.pallas_call(rows_kernel, grid_spec=pltpu.PrefetchScalarGridSpec(num_sc...]
    pallas_call x1, Pallas kernels: 5.32 us -> 7.5 us  [grads_call(): pl.pallas_call(grads_kernel, grid_spec=pltpu.PrefetchScalarGridSpec(num_s...]
    unnamed x28 -> x22, local copies, waits for them, and re-layouts: 5.49 us -> 6.19 us
  transfers between devices with their start and end apart: 15 -> 15, of which waited for: 10 -> 10; matrix products, arithmetic and copies ran while one was open for 4% -> 4% of each run, Pallas kernels for 10% -> 8%
where the time goes in v4:
time: 119 us; the launch traced here: 118 us
  waiting for transfers between devices  42.6 us (36%)
  starting transfers between devices  38.1 us (32%)
  Pallas kernels  24.8 us (21%)
  local copies, waits for them, and re-layouts  7.16 us (6%)
  other arithmetic  4.55 us (4%)
    ppermute x1, waiting for transfers between devices, body(): pother = lax.ppermute(other, 'w', pair)  11.9 us
    all_to_all x1, waiting for transfers between devices, body(): got = lax.all_to_all(msg, ('z', 'v', 'w'), 0, 0)  10.5 us
    ppermute x8, starting transfers between devices, hop(): return lax.ppermute(piece, axis, ring(size, d))  10.5 us
    all_to_all x1, starting transfers between devices, body(): got = lax.all_to_all(msg, ('z', 'v', 'w'), 0, 0)  9.5 us
    all_to_all x1, waiting for transfers between devices, body(): small = lax.all_to_all(small, ('z', 'w'), 0, 0)  9.43 us
    pallas_call x1, Pallas kernels, pair_call(): pl.pallas_call(pair_kernel, grid_spec=pltpu.PrefetchScalarGridSpec(num_sc...  8.58 us
    pallas_call x1, Pallas kernels, grads_call(): pl.pallas_call(grads_kernel, grid_spec=pltpu.PrefetchScalarGridSpec(num_s...  7.5 us
    all_to_all x1, starting transfers between devices, body(): small = lax.all_to_all(small, ('z', 'w'), 0, 0)  6.6 us
  transfers between devices with their start and end apart: 15, of which 10 were waited for; matrix products, arithmetic and copies ran while one was open for 4% of the time, Pallas kernels for 8%

profile of v4, /device:TPU:1, one launch (start us, length us, event | category | flops | bytes accessed | tf_op | source)
XLA Modules:
  0.0 118.1 jit_solution(7946940902118960808)
XLA Ops:
  0.6 1.0 pad_add_fusion.mine
  1.7 3.3 %collective-permute-start = (f32[136,1024]{1,0:T(8,128)S(1)}, f32[136,1024]{1,0:T(8,128)S(1)}, u32[]{:S(2)}, u32[]{:S(2)}) collective-permute-start(f32[136,1024]{1,0:T(8,128)S(1)} %pad_add_fusion.mine), channel_id=1, source_target_pairs={{0,1},{1,0},{2,3},{3,2},{4,5},{5,4},{6,7},{7,6},{8,9},{9,8},{10,11... | collective-permute-start | bytes 1671176 | tf_op jit(solution)/shard_map/ppermute | solution.py:530
  5.0 0.1 stack.23.idx
  5.0 0.7 fusion.5
  5.8 0.7 collective-permute-done.other
  6.5 0.0 copy-start
  6.5 5.2 %local.1 = f32[32,1,2176]{2,1,0:T(1,128)S(1)} custom-call(s32[5]{0:T(128)S(1)} %stack.23.idx, f32[16,128]{1,0:T(8,128)S(1)} %bitcast.23, f32[136,1024]{1,0:T(8,128)S(1)} %pad_add_fusion.mine, f32[136,1024]{1,0:T(8,128)S(1)} %collective-permute-done.other, bf16[512,2048]{1,0:T(8,128)(2,1)} %win.5, bf16[512,2048]{1,0:T(8,128)(2,1)} %wout.5), custom_call_target="tpu_custom_call" | custom-call | tf_op jit(solution)/shard_map/local/pallas_call | solution.py:167
  11.7 0.0 copy-start.3
  11.7 0.7 copy-done.3
  12.4 9.5 %all-to-all-start = ((f32[32,1,2176]{2,1,0:T(1,128)}), f32[32,1,2176]{2,1,0:T(1,128)S(1)}, u32[]{:S(2)}, u32[]{:S(2)}) async-start(f32[32,1,2176]{2,1,0:T(1,128)} %copy-done.3), calls=%async_computation | async-start | bytes 557056 | tf_op jit(solution)/shard_map/all_to_all | solution.py:537
  21.9 1.3 %collective-permute-start.2 = (f32[136,1024]{1,0:T(8,128)S(1)}, f32[136,1024]{1,0:T(8,128)}, u32[]{:S(2)}, u32[]{:S(2)}) collective-permute-start(f32[136,1024]{1,0:T(8,128)S(1)} %pad_add_fusion.mine), channel_id=1, source_target_pairs={{0,2},{2,0},{1,3},{3,1},{4,6},{6,4},{5,7},{7,5},{8,10},{10,8},{9,1... | collective-permute-start | bytes 1671176 | tf_op jit(solution)/shard_map/ppermute | solution.py:532
  23.2 0.2 collective-permute-start.3
  23.5 10.5 %all-to-all-done.got = f32[32,1,2176]{2,1,0:T(1,128)S(1)} async-done(((f32[32,1,2176]{2,1,0:T(1,128)}), f32[32,1,2176]{2,1,0:T(1,128)S(1)}, u32[]{:S(2)}, u32[]{:S(2)}) %all-to-all-start) | async-done | bytes 278560 | tf_op jit(solution)/shard_map/all_to_all | solution.py:537
  34.0 4.5 %collective-permute-done.2.pmine = f32[136,1024]{1,0:T(8,128)} collective-permute-done((f32[136,1024]{1,0:T(8,128)S(1)}, f32[136,1024]{1,0:T(8,128)}, u32[]{:S(2)}, u32[]{:S(2)}) %collective-permute-start.2) | collective-permute-done | bytes 557088 | tf_op jit(solution)/shard_map/ppermute | solution.py:532
  38.5 11.9 %collective-permute-done.3.pother = f32[136,1024]{1,0:T(8,128)} collective-permute-done((f32[136,1024]{1,0:T(8,128)S(1)}, f32[136,1024]{1,0:T(8,128)}, u32[]{:S(2)}, u32[]{:S(2)}) %collective-permute-start.3) | collective-permute-done | bytes 557088 | tf_op jit(solution)/shard_map/ppermute | solution.py:533
  50.4 0.0 copy-done
  50.4 1.6 %copy-done.1 = bf16[512,2048]{1,0:T(8,128)(2,1)S(1)} copy-done((bf16[512,2048]{1,0:T(8,128)(2,1)S(1)}, bf16[512,2048]{1,0:T(8,128)(2,1)}, u32[]{:S(2)}) %copy-start.1) | copy-done | bytes 2097176
  52.0 8.6 %pair.1 = (f32[128,512]{1,0:T(8,128)}, f32[256,512]{1,0:T(8,128)}, bf16[512,512]{1,0:T(8,128)(2,1)S(1)}, bf16[512,512]{1,0:T(8,128)(2,1)S(1)}, bf16[512,512]{1,0...) custom-call(s32[5]{0:T(128)S(1)} %stack.23.idx, f32[16,128]{1,0:T(8,128)S(1)} %bitcast.24, f32[136,1024]{1,0:T(8,128)S(1)} %pad_add_fusion.mine, ...), custom_call_target="tpu_custom_call" | custom-call | tf_op jit(solution)/shard_map/pair/pallas_call | solution.py:381
  60.6 2.8 %collective-permute-start.8 = (f32[256,512]{1,0:T(8,128)}, f32[256,512]{1,0:T(8,128)}, u32[]{:S(2)}, u32[]{:S(2)}) collective-permute-start(f32[256,512]{1,0:T(8,128)} %get-tuple-element.29), channel_id=1, source_target_pairs={{0,4},{4,0},{1,5},{5,1},{2,6},{6,2},{3,7},{7,3},{8,12},{12,8},{9,1... | collective-permute-start | bytes 1572872 | tf_op jit(solution)/shard_map/ppermute | solution.py:544
  63.4 1.6 %second.1 = (f32[128,512]{1,0:T(8,128)}, f32[128,512]{1,0:T(8,128)}, f32[128,512]{1,0:T(8,128)S(1)}, f32[256,512]{1,0:T(8,128)S(1)}) custom-call(s32[5]{0:T(128)S(1)} %stack.23.idx, bf16[512,512]{1,0:T(8,128)(2,1)S(1)} %get-tuple-element.20.packed, bf16[512,512]{1,0:T(8,128)(2,1)S(1)} %get-tuple-element.21.drive, ...), custom_call_target="tpu_custom_call" | custom-call | tf_op jit(solution)/shard_map/second/pallas_call | solution.py:451
  65.0 0.0 copy-start.6
  65.0 0.8 copy-done.6
  65.8 0.0 copy-start.8
  65.9 0.7 copy-done.8
  66.5 1.2 %collective-permute-start.5 = (f32[128,512]{1,0:T(8,128)}, f32[128,512]{1,0:T(8,128)}, u32[]{:S(2)}, u32[]{:S(2)}) collective-permute-start(f32[128,512]{1,0:T(8,128)} %get-tuple-element.26), channel_id=1, source_target_pairs={{0,64},{64,128},{128,192},{192,0},{1,65},{65,129},{129,193},{193,1... | collective-permute-start | bytes 786440 | tf_op jit(solution)/shard_map/ppermute | solution.py:544
  67.8 1.5 %collective-permute-start.6 = (f32[128,512]{1,0:T(8,128)}, f32[128,512]{1,0:T(8,128)}, u32[]{:S(2)}, u32[]{:S(2)}) collective-permute-start(f32[128,512]{1,0:T(8,128)} %get-tuple-element.27), channel_id=1, source_target_pairs={{0,192},{64,0},{128,64},{192,128},{1,193},{65,1},{129,65},{193,129... | collective-permute-start | bytes 786440 | tf_op jit(solution)/shard_map/ppermute | solution.py:544
  69.2 1.5 %collective-permute-start.4 = (f32[128,512]{1,0:T(8,128)}, f32[128,512]{1,0:T(8,128)}, u32[]{:S(2)}, u32[]{:S(2)}) collective-permute-start(f32[128,512]{1,0:T(8,128)} %get-tuple-element.25), channel_id=1, source_target_pairs={{0,128},{64,192},{128,0},{192,64},{1,129},{65,193},{129,1},{193,65... | collective-permute-start | bytes 786440 | tf_op jit(solution)/shard_map/ppermute | solution.py:544
  70.8 0.0 copy-start.2
  70.8 1.6 %copy-done.2 = bf16[512,2048]{1,0:T(8,128)(2,1)S(1)} copy-done((bf16[512,2048]{1,0:T(8,128)(2,1)S(1)}, bf16[512,2048]{1,0:T(8,128)(2,1)}, u32[]{:S(2)}) %copy-start.2) | copy-done | bytes 2097176
  72.3 7.5 %grads.1 = (f32[128,1024]{1,0:T(8,128)S(1)}, f32[128,1024]{1,0:T(8,128)}) custom-call(s32[5]{0:T(128)S(1)} %stack.23.idx, f32[16,128]{1,0:T(8,128)S(1)} %bitcast.25, f32[136,1024]{1,0:T(8,128)S(1)} %pad_add_fusion.mine, f32[136,1024]{1,0:T(8,128)S(1)} %collective-permute-done.other, f32[32,1,2176]{2,1,0:T(1,128)S(1)} %all-to-all-done.got, ...), custom_call_target="tpu_custom_call" | custom-call | tf_op jit(solution)/shard_map/grads/pallas_call | solution.py:421
  79.9 0.0 copy-start.4
  79.9 0.8 copy-done.4
  80.7 2.6 %collective-permute-start.1 = (f32[128,1024]{1,0:T(8,128)}, f32[128,1024]{1,0:T(8,128)S(1)}, u32[]{:S(2)}, u32[]{:S(2)}) collective-permute-start(f32[128,1024]{1,0:T(8,128)} %get-tuple-element.19), channel_id=1, source_target_pairs={{0,1},{1,0},{2,3},{3,2},{4,5},{5,4},{6,7},{7,6},{8,9},{9,8},{10,11... | collective-permute-start | bytes 1572872 | tf_op jit(solution)/shard_map/ppermute | solution.py:555
  83.3 0.0 collective-permute-done.5
  83.3 0.0 collective-permute-done.6
  83.3 0.0 collective-permute-done.4
  83.3 0.0 copy-done.9
  83.3 0.0 copy-start.10
  83.3 0.0 copy-start.5
  83.3 1.4 %dynamic-slice_add_fusion.4 = (f32[64,512]{1,0:T(8,128)S(1)}, f32[64,512]{1,0:T(8,128)S(1)}) fusion(f32[128,512]{1,0:T(8,128)} %collective-permute-done.6, s32[]{:T(128)S(6)} %select_n.39, f32[128,512]{1,0:T(8,128)} %collective-permute-done.5, f32[128,512]{1,0:T(8,128)} %collective-permute-done.4, f32[128,512]{1,0:T(8,128)S(1)} %copy-done.9, s32[]{:T(128)S(6)} %select_n.38), kind=kLoop, calls=%fused_computation.10 | loop fusion | flops 196608 | bytes 1310728 | tf_op jit(solution)/shard_map/add | solution.py:469
  84.7 0.3 collective-permute-start.7
  85.0 0.0 collective-permute-done.8
  85.0 0.0 copy-done.7
  85.0 1.2 %dynamic-slice_add_fusion = (f32[64,512]{1,0:T(8,128)S(1)}, f32[64,512]{1,0:T(8,128)S(1)}, f32[64,512]{1,0:T(8,128)S(1)}, f32[64,512]{1,0:T(8,128)S(1)}) fusion(f32[256,512]{1,0:T(8,128)} %collective-permute-done.8, s32[]{:T(128)S(6)} %select_n.43, f32[256,512]{1,0:T(8,128)S(1)} %copy-done.7, s32[]{:T(128)S(6)} %select_n.42, s32[]{:T(128)S(6)} %select_n.41, ...), kind=kLoop, calls=%fused_computation.6 | loop fusion | flops 131072 | bytes 1572880 | tf_op jit(solution)/shard_map/add | solution.py:469
  86.2 0.6 collective-permute-start.10
  86.8 2.4 %collective-permute-start.11 = (f32[64,512]{1,0:T(8,128)S(1)}, f32[64,512]{1,0:T(8,128)S(1)}, u32[]{:S(2)}, u32[]{:S(2)}) collective-permute-start(f32[64,512]{1,0:T(8,128)S(1)} %get-tuple-element.32), channel_id=1, source_target_pairs={{0,192},{64,0},{128,64},{192,128},{1,193},{65,1},{129,65},{193,129... | collective-permute-start | bytes 393224 | tf_op jit(solution)/shard_map/ppermute | solution.py:544
  89.1 0.2 collective-permute-start.9
  89.4 1.9 %collective-permute-done.7.a1 = f32[64,512]{1,0:T(8,128)S(1)} collective-permute-done((f32[64,512]{1,0:T(8,128)S(1)}, f32[64,512]{1,0:T(8,128)S(1)}, u32[]{:S(2)}, u32[]{:S(2)}) %collective-permute-start.7) | collective-permute-done | bytes 131104 | tf_op jit(solution)/shard_map/ppermute | solution.py:544
  91.3 1.1 collective-permute-done.10.b2
  92.4 2.1 %collective-permute-done.11.b3 = f32[64,512]{1,0:T(8,128)S(1)} collective-permute-done((f32[64,512]{1,0:T(8,128)S(1)}, f32[64,512]{1,0:T(8,128)S(1)}, u32[]{:S(2)}, u32[]{:S(2)}) %collective-permute-start.11) | collective-permute-done | bytes 131104 | tf_op jit(solution)/shard_map/ppermute | solution.py:544
  94.5 0.3 collective-permute-done.9.b1
  94.8 0.7 joined.1
  95.5 6.6 %all-to-all-start.1 = ((f32[16,8,512]{2,1,0:T(8,128)}), f32[16,8,512]{2,1,0:T(8,128)S(1)}, u32[]{:S(2)}, u32[]{:S(2)}) async-start(f32[16,8,512]{2,1,0:T(8,128)} %joined.1), calls=%async_computation.1 | async-start | bytes 524288 | tf_op jit(solution)/shard_map/all_to_all | solution.py:559
  102.1 0.0 copy-done.10
  102.1 0.0 collective-permute-done.1
  102.2 0.0 copy-done.5
  102.2 0.1 fusion.1
  102.3 9.4 %all-to-all-done.1 = f32[16,8,512]{2,1,0:T(8,128)S(1)} async-done(((f32[16,8,512]{2,1,0:T(8,128)}), f32[16,8,512]{2,1,0:T(8,128)S(1)}, u32[]{:S(2)}, u32[]{:S(2)}) %all-to-all-start.1) | async-done | bytes 262176 | tf_op jit(solution)/shard_map/all_to_all | solution.py:559
  111.7 0.1 reshape.28
  111.9 0.1 reduce_sum.9
  112.0 4.1 %collective-permute-start.12 = (f32[2,2,2,512]{3,2,1,0:T(2,128)S(1)}, f32[2,2,2,512]{3,2,1,0:T(2,128)S(1)}, u32[]{:S(2)}, u32[]{:S(2)}) collective-permute-start(f32[2,2,2,512]{3,2,1,0:T(2,128)S(1)} %get-tuple-element.40), channel_id=1, source_target_pairs={{0,1},{1,0},{2,3},{3,2},{4,5},{5,4},{6,7},{7,6},{8,9},{9,8},{10,11... | collective-permute-start | bytes 49160 | tf_op jit(solution)/shard_map/ppermute | solution.py:563
  116.1 0.7 slice_bitcast_fusion
  116.8 0.1 collective-permute-done.12.come
  116.9 1.2 tail.1
  (8 shorter events, 0.1 us)
Async XLA Ops:
  1.7 4.9 %collective-permute-start = (f32[136,1024]{1,0:T(8,128)S(1)}, f32[136,1024]{1,0:T(8,128)S(1)}, u32[]{:S(2)}, u32[]{:S(2)}) collective-permute-start(f32[136,1024]{1,0:T(8,128)S(1)} %pad_add_fusion.mine), channel_id=1, source_target_pairs={{0,1},{1,0},{2,3},{3,2},{4,5},{5,4},{6,7},{7,6},{8,9},{9,8},{10,11... | collective-permute-start | bytes 1671176 | tf_op jit(solution)/shard_map/ppermute | solution.py:530
  6.5 43.9 %copy-start = (bf16[512,2048]{1,0:T(8,128)(2,1)S(1)}, bf16[512,2048]{1,0:T(8,128)(2,1)}, u32[]{:S(2)}) copy-start(bf16[512,2048]{1,0:T(8,128)(2,1)} %win.5) | copy-start | bytes 6291460
  11.7 0.7 copy-start.3
  12.4 21.6 %all-to-all-start = ((f32[32,1,2176]{2,1,0:T(1,128)}), f32[32,1,2176]{2,1,0:T(1,128)S(1)}, u32[]{:S(2)}, u32[]{:S(2)}) async-start(f32[32,1,2176]{2,1,0:T(1,128)} %copy-done.3), calls=%async_computation | async-start | bytes 557056 | tf_op jit(solution)/shard_map/all_to_all | solution.py:537
  21.9 16.6 %collective-permute-start.2 = (f32[136,1024]{1,0:T(8,128)S(1)}, f32[136,1024]{1,0:T(8,128)}, u32[]{:S(2)}, u32[]{:S(2)}) collective-permute-start(f32[136,1024]{1,0:T(8,128)S(1)} %pad_add_fusion.mine), channel_id=1, source_target_pairs={{0,2},{2,0},{1,3},{3,1},{4,6},{6,4},{5,7},{7,5},{8,10},{10,8},{9,1... | collective-permute-start | bytes 1671176 | tf_op jit(solution)/shard_map/ppermute | solution.py:532
  23.2 27.2 %collective-permute-start.3 = (f32[136,1024]{1,0:T(8,128)S(1)}, f32[136,1024]{1,0:T(8,128)}, u32[]{:S(2)}, u32[]{:S(2)}) collective-permute-start(f32[136,1024]{1,0:T(8,128)S(1)} %collective-permute-done.other), channel_id=1, source_target_pairs={{0,2},{2,0},{1,3},{3,1},{4,6},{6,4},{5,7},{7,5},{8,10},{10,8},{9,1... | collective-permute-start | bytes 1671176 | tf_op jit(solution)/shard_map/ppermute | solution.py:533
  50.4 1.6 %copy-start.1 = (bf16[512,2048]{1,0:T(8,128)(2,1)S(1)}, bf16[512,2048]{1,0:T(8,128)(2,1)}, u32[]{:S(2)}) copy-start(bf16[512,2048]{1,0:T(8,128)(2,1)} %wout.5) | copy-start | bytes 6291460
  60.6 24.4 %collective-permute-start.8 = (f32[256,512]{1,0:T(8,128)}, f32[256,512]{1,0:T(8,128)}, u32[]{:S(2)}, u32[]{:S(2)}) collective-permute-start(f32[256,512]{1,0:T(8,128)} %get-tuple-element.29), channel_id=1, source_target_pairs={{0,4},{4,0},{1,5},{5,1},{2,6},{6,2},{3,7},{7,3},{8,12},{12,8},{9,1... | collective-permute-start | bytes 1572872 | tf_op jit(solution)/shard_map/ppermute | solution.py:544
  65.0 0.8 copy-start.6
  65.8 0.7 copy-start.8
  66.5 16.7 %collective-permute-start.5 = (f32[128,512]{1,0:T(8,128)}, f32[128,512]{1,0:T(8,128)}, u32[]{:S(2)}, u32[]{:S(2)}) collective-permute-start(f32[128,512]{1,0:T(8,128)} %get-tuple-element.26), channel_id=1, source_target_pairs={{0,64},{64,128},{128,192},{192,0},{1,65},{65,129},{129,193},{193,1... | collective-permute-start | bytes 786440 | tf_op jit(solution)/shard_map/ppermute | solution.py:544
  67.8 15.5 %collective-permute-start.6 = (f32[128,512]{1,0:T(8,128)}, f32[128,512]{1,0:T(8,128)}, u32[]{:S(2)}, u32[]{:S(2)}) collective-permute-start(f32[128,512]{1,0:T(8,128)} %get-tuple-element.27), channel_id=1, source_target_pairs={{0,192},{64,0},{128,64},{192,128},{1,193},{65,1},{129,65},{193,129... | collective-permute-start | bytes 786440 | tf_op jit(solution)/shard_map/ppermute | solution.py:544
  69.2 14.1 %collective-permute-start.4 = (f32[128,512]{1,0:T(8,128)}, f32[128,512]{1,0:T(8,128)}, u32[]{:S(2)}, u32[]{:S(2)}) collective-permute-start(f32[128,512]{1,0:T(8,128)} %get-tuple-element.25), channel_id=1, source_target_pairs={{0,128},{64,192},{128,0},{192,64},{1,129},{65,193},{129,1},{193,65... | collective-permute-start | bytes 786440 | tf_op jit(solution)/shard_map/ppermute | solution.py:544
  70.8 1.6 %copy-start.2 = (bf16[512,2048]{1,0:T(8,128)(2,1)S(1)}, bf16[512,2048]{1,0:T(8,128)(2,1)}, u32[]{:S(2)}) copy-start(bf16[512,2048]{1,0:T(8,128)(2,1)} %wout.5) | copy-start | bytes 6291460
  72.3 11.0 %copy-start.9 = (f32[128,512]{1,0:T(8,128)S(1)}, f32[128,512]{1,0:T(8,128)}, u32[]{:S(2)}) copy-start(f32[128,512]{1,0:T(8,128)} %copy-done.8) | copy-start | bytes 786436
  72.3 12.7 %copy-start.7 = (f32[256,512]{1,0:T(8,128)S(1)}, f32[256,512]{1,0:T(8,128)}, u32[]{:S(2)}) copy-start(f32[256,512]{1,0:T(8,128)} %copy-done.6) | copy-start | bytes 1572868
  79.9 0.8 copy-start.4
  80.7 21.5 %collective-permute-start.1 = (f32[128,1024]{1,0:T(8,128)}, f32[128,1024]{1,0:T(8,128)S(1)}, u32[]{:S(2)}, u32[]{:S(2)}) collective-permute-start(f32[128,1024]{1,0:T(8,128)} %get-tuple-element.19), channel_id=1, source_target_pairs={{0,1},{1,0},{2,3},{3,2},{4,5},{5,4},{6,7},{7,6},{8,9},{9,8},{10,11... | collective-permute-start | bytes 1572872 | tf_op jit(solution)/shard_map/ppermute | solution.py:555
  83.3 18.8 %copy-start.10 = (f32[512]{0:T(512)S(1)}, f32[512]{0:T(512)}, u32[]{:S(2)}) copy-start(f32[512]{0:T(512)} %param.14) | copy-start | bytes 6148
  83.3 18.8 %copy-start.5 = (f32[128,1024]{1,0:T(8,128)S(1)}, f32[128,1024]{1,0:T(8,128)}, u32[]{:S(2)}) copy-start(f32[128,1024]{1,0:T(8,128)} %copy-done.4) | copy-start | bytes 1572868
  84.7 6.6 %collective-permute-start.7 = (f32[64,512]{1,0:T(8,128)S(1)}, f32[64,512]{1,0:T(8,128)S(1)}, u32[]{:S(2)}, u32[]{:S(2)}) collective-permute-start(f32[64,512]{1,0:T(8,128)S(1)} %get-tuple-element.36), channel_id=1, source_target_pairs={{0,4},{4,0},{1,5},{5,1},{2,6},{6,2},{3,7},{7,3},{8,12},{12,8},{9,1... | collective-permute-start | bytes 393224 | tf_op jit(solution)/shard_map/ppermute | solution.py:544
  86.2 6.2 %collective-permute-start.10 = (f32[64,512]{1,0:T(8,128)S(1)}, f32[64,512]{1,0:T(8,128)S(1)}, u32[]{:S(2)}, u32[]{:S(2)}) collective-permute-start(f32[64,512]{1,0:T(8,128)S(1)} %get-tuple-element.33), channel_id=1, source_target_pairs={{0,64},{64,128},{128,192},{192,0},{1,65},{65,129},{129,193},{193,1... | collective-permute-start | bytes 393224 | tf_op jit(solution)/shard_map/ppermute | solution.py:544
  86.8 7.7 %collective-permute-start.11 = (f32[64,512]{1,0:T(8,128)S(1)}, f32[64,512]{1,0:T(8,128)S(1)}, u32[]{:S(2)}, u32[]{:S(2)}) collective-permute-start(f32[64,512]{1,0:T(8,128)S(1)} %get-tuple-element.32), channel_id=1, source_target_pairs={{0,192},{64,0},{128,64},{192,128},{1,193},{65,1},{129,65},{193,129... | collective-permute-start | bytes 393224 | tf_op jit(solution)/shard_map/ppermute | solution.py:544
  89.1 5.6 %collective-permute-start.9 = (f32[64,512]{1,0:T(8,128)S(1)}, f32[64,512]{1,0:T(8,128)S(1)}, u32[]{:S(2)}, u32[]{:S(2)}) collective-permute-start(f32[64,512]{1,0:T(8,128)S(1)} %get-tuple-element.34), channel_id=1, source_target_pairs={{0,128},{64,192},{128,0},{192,64},{1,129},{65,193},{129,1},{193,65... | collective-permute-start | bytes 393224 | tf_op jit(solution)/shard_map/ppermute | solution.py:544
  95.5 16.2 %all-to-all-start.1 = ((f32[16,8,512]{2,1,0:T(8,128)}), f32[16,8,512]{2,1,0:T(8,128)S(1)}, u32[]{:S(2)}, u32[]{:S(2)}) async-start(f32[16,8,512]{2,1,0:T(8,128)} %joined.1), calls=%async_computation.1 | async-start | bytes 524288 | tf_op jit(solution)/shard_map/all_to_all | solution.py:559
  112.0 4.9 %collective-permute-start.12 = (f32[2,2,2,512]{3,2,1,0:T(2,128)S(1)}, f32[2,2,2,512]{3,2,1,0:T(2,128)S(1)}, u32[]{:S(2)}, u32[]{:S(2)}) collective-permute-start(f32[2,2,2,512]{3,2,1,0:T(2,128)S(1)} %get-tuple-element.40), channel_id=1, source_target_pairs={{0,1},{1,0},{2,3},{3,2},{4,5},{5,4},{6,7},{7,6},{8,9},{9,8},{10,11... | collective-permute-start | bytes 49160 | tf_op jit(solution)/shard_map/ppermute | solution.py:563

commit v5 on v2

--- a/solution.py
+++ b/solution.py
@@ -150,7 +150,7 @@
 
     zero = jnp.zeros((8, LANES), F32)
     start = [(zero, zero) for _ in range(CH)]
-    ff, mm, prod = lax.fori_loop(0, GROUPS, step, (start, start, zero + 1.0))
+    ff, mm, prod = lax.fori_loop(0, GROUPS, step, (start, start, zero + 1.0), unroll=2)
     rows = (
         [ff[j][0][7:8] for j in range(CH)]
         + [ff[j][1][7:8] for j in range(CH)]
@@ -281,7 +281,7 @@
             nm.append((spread(db * tr, 0), spread(db * ti, 0)))
         return nf, nm
 
-    lax.fori_loop(0, GROUPS, step, (ff, mm))
+    lax.fori_loop(0, GROUPS, step, (ff, mm), unroll=2)
     packed[...] = sr_[...].astype(BF16)
     drive[...] = ar_[...].astype(BF16)
     lhs_in[...] = lax.dot_general(
@@ -408,6 +408,30 @@
     )(*one, *two)
 
 
+def tail_kernel(idx, keep, come, grad_in, grad_out):
+    c = idx[0]
+    for part, at in ((keep, c), (come, 1 - c)):
+        for k, out in enumerate((grad_in, grad_out)):
+            for h in range(2):
+                cols = pl.ds(pl.multiple_of(h * N + at * W, W), W)
+                out[:, cols] = part[k, :, h * W : (h + 1) * W]
+
+
+def tail_call(idx, keep, come):
+    return pl.pallas_call(
+        tail_kernel,
+        grid_spec=pltpu.PrefetchScalarGridSpec(
+            num_scalar_prefetch=1,
+            grid=(1,),
+            in_specs=[whole((2, 2, 2 * W))] * 2,
+            out_specs=[whole((2, 2 * N))] * 2,
+        ),
+        out_shape=[jax.ShapeDtypeStruct((2, 2 * N), F32)] * 2,
+        compiler_params=params(),
+        name="tail",
+    )(idx, keep, come)
+
+
 def body(signal, damping, nu_log, theta, in_weight, out_weight, skip_gain, cotangent):
     x, z = lax.axis_index("x"), lax.axis_index("z")
     y, c = lax.axis_index("y"), lax.axis_index("c")
@@ -419,8 +443,11 @@
     ).reshape(4, C, CH, LANES)
     par = lax.dynamic_index_in_dim(par, c, 1, False).reshape(16, LANES)
     sig, cot = signal[0], cotangent[0]
-    wide = jnp.concatenate([sig, cot], 1).astype(F32)
-    mine = jnp.concatenate([wide, jnp.pad(damping, ((0, 7), (0, 2 * D - TOK)))], 0)
+    mine = (
+        jnp.pad(sig.astype(F32), ((0, 8), (0, D)))
+        + jnp.pad(cot.astype(F32), ((0, 8), (D, 0)))
+        + jnp.pad(damping, ((TOK, 7), (0, 2 * D - TOK)))
+    )
     swap = ring(C, 1)
     other = lax.ppermute(mine, "c", swap)
     sig_all, cot_all, fre, fim, bre, bim, msg, damp = local_call(
@@ -453,10 +480,8 @@
     keep = lax.dynamic_index_in_dim(small, c, 1, False)
     send = lax.dynamic_index_in_dim(small, 1 - c, 1, False)
     come = lax.ppermute(send, "c", swap)
-    first = jnp.where(c == 0, keep, come).reshape(2, 2, 2, 1, W)
-    second = jnp.where(c == 0, come, keep).reshape(2, 2, 2, 1, W)
-    full = jnp.concatenate([first, second], 3).reshape(2, 2, 2 * N)
-    return rows[None, :, :D], rows[None, :, D:], full[0], full[1]
+    grad_in, grad_out = tail_call(idx, keep, come)
+    return rows[None, :, :D], rows[None, :, D:], grad_in, grad_out
 
 
 def solution(mesh):

time: 114 us -> 114 us (level)
    squeeze x2 -> x0, local copies, waits for them, and re-layouts: 1.26 us -> none  [body(): return (rows[None, :, :D], rows[None, :, D:], full[0], full[1])]
    pallas_call x0 -> x1, Pallas kernels: none -> 1.16 us  [tail_call(): pl.pallas_call(tail_kernel, grid_spec=pltpu.PrefetchScalarGridSpec(num_sc...]
where the time goes in v5:
time: 114 us; the launch traced here: 113 us
  starting transfers between devices  41.4 us (36%)
  blocking collectives  21.4 us (19%)
  waiting for transfers between devices  21.2 us (19%)
  Pallas kernels  16 us (14%)
  local copies, waits for them, and re-layouts  7.54 us (7%)
  other arithmetic  5.13 us (4%)
    all_to_all x1, blocking collectives, body(): got = lax.all_to_all(msg, ('z', 'y'), 0, 0)  21.4 us
    ppermute x12, starting transfers between devices, hop(): return lax.ppermute(part, axis, ring(4, d))  18.7 us
    ppermute x1, starting transfers between devices, body(): own = own + lax.ppermute(oth, 'c', swap)  13.4 us
    ppermute x12, waiting for transfers between devices, hop(): return lax.ppermute(part, axis, ring(4, d))  10.3 us
    all_to_all x1, waiting for transfers between devices, body(): small = lax.all_to_all(small, 'z', 0, 0).sum(0).reshape(2, C, 2, 2 * W)  10 us
    unnamed x26, local copies, waits for them, and re-layouts  6.79 us
    pallas_call x1, Pallas kernels, local_call(): pl.pallas_call(local_kernel, grid_spec=pltpu.PrefetchScalarGridSpec(num_s...  5.21 us
    pallas_call x1, Pallas kernels, grads_call(): pl.pallas_call(grads_kernel, grid_spec=pltpu.PrefetchScalarGridSpec(num_s...  3.87 us
  transfers between devices with their start and end apart: 16, of which 7 were waited for; matrix products, arithmetic and copies ran while one was open for 4% of the time, Pallas kernels for 3%

profile of v5, /device:TPU:1, one launch (start us, length us, event | category | flops | bytes accessed | tf_op | source)
XLA Modules:
  0.0 113.3 jit_solution(7449974761560142307)
XLA Ops:
  0.6 1.0 pad_add_fusion.mine
  1.7 3.3 %collective-permute-start = (f32[136,1024]{1,0:T(8,128)S(1)}, f32[136,1024]{1,0:T(8,128)S(1)}, u32[]{:S(2)}, u32[]{:S(2)}) collective-permute-start(f32[136,1024]{1,0:T(8,128)S(1)} %pad_add_fusion.mine), channel_id=1, source_target_pairs={{0,1},{1,0},{2,3},{3,2},{4,5},{5,4},{6,7},{7,6},{8,9},{9,8},{10,11... | collective-permute-start | bytes 1671176 | tf_op jit(solution)/shard_map/ppermute | solution.py:452
  5.0 0.1 pad_add_fusion.1.idx
  5.0 0.7 fusion.5
  5.8 0.7 collective-permute-done.other
  6.5 5.2 %local.1 = (bf16[256,512]{1,0:T(8,128)(2,1)S(1)}, bf16[256,512]{1,0:T(8,128)(2,1)S(1)}, f32[256,512]{1,0:T(8,128)S(1)}, f32[256,512]{1,0:T(8,128)S(1)}, f32[256,...) custom-call(s32[4]{0:T(128)S(1)} %pad_add_fusion.1.idx, ...), custom_call_target="tpu_custom_call" | custom-call | tf_op jit(solution)/shard_map/local/pallas_call | solution.py:173
  11.8 21.4 %all_to_all.10.got = f32[32,1,2176]{2,1,0:T(1,128)S(1)} all-to-all(f32[32,1,2176]{2,1,0:T(1,128)S(1)} %get-tuple-element.35), channel_id=1, replica_groups=mesh['x'=4,'z'=8,'y'=4,'c'=2] {'z','y'}, dimensions={0} | all-to-all | bytes 557056 | tf_op jit(solution)/shard_map/all_to_all | solution.py:456
  33.1 0.0 copy-start
  33.1 3.9 %grads.1 = (f32[128,1024]{1,0:T(8,128)}, f32[128,1024]{1,0:T(8,128)}, bf16[256,1024]{1,0:T(8,128)(2,1)S(1)}, bf16[256,1024]{1,0:T(8,128)(2,1)S(1)}, bf16[512,256...) custom-call(s32[4]{0:T(128)S(1)} %pad_add_fusion.1.idx, f32[16,128]{1,0:T(8,128)S(1)} %bitcast.20, ...), custom_call_target="tpu_custom_call" | custom-call | tf_op jit(solution)/shard_map/grads/pallas_call | solution.py:311
  37.0 0.0 copy-start.4
  37.0 2.0 %second.1 = (f32[128,1024]{1,0:T(8,128)}, f32[128,1024]{1,0:T(8,128)}, f32[128,1024]{1,0:T(8,128)S(1)}, f32[128,1024]{1,0:T(8,128)}) custom-call(s32[4]{0:T(128)S(1)} %pad_add_fusion.1.idx, bf16[256,1024]{1,0:T(8,128)(2,1)S(1)} %get-tuple-element.36.packed, bf16[256,1024]{1,0:T(8,128)(2,1)S(1)} %get-tuple-element.37.drive, ...), custom_call_target="tpu_custom_call" | custom-call | tf_op jit(solution)/shard_map/second/pallas_call | solution.py:338
  39.0 0.0 copy-done.4
  39.0 0.0 copy-start.2
  39.0 0.8 copy-done.2
  39.8 2.5 %collective-permute-start.4 = (f32[128,1024]{1,0:T(8,128)S(1)}, f32[128,1024]{1,0:T(8,128)S(1)}, u32[]{:S(2)}, u32[]{:S(2)}) collective-permute-start(f32[128,1024]{1,0:T(8,128)S(1)} %get-tuple-element.45), channel_id=1, source_target_pairs={{0,192},{64,0},{128,64},{192,128},{1,193},{65,1},{129,65},{193,129... | collective-permute-start | bytes 1572872 | tf_op jit(solution)/shard_map/ppermute | solution.py:462
  42.2 0.0 collective-permute-start.3
  42.2 1.7 %collective-permute-start.2 = (f32[128,1024]{1,0:T(8,128)}, f32[128,1024]{1,0:T(8,128)}, u32[]{:S(2)}, u32[]{:S(2)}) collective-permute-start(f32[128,1024]{1,0:T(8,128)} %get-tuple-element.43), channel_id=1, source_target_pairs={{0,128},{64,192},{128,0},{192,64},{1,129},{65,193},{129,1},{193,65... | collective-permute-start | bytes 1572872 | tf_op jit(solution)/shard_map/ppermute | solution.py:462
  44.0 1.3 %collective-permute-start.10 = (f32[128,1024]{1,0:T(8,128)}, f32[128,1024]{1,0:T(8,128)}, u32[]{:S(2)}, u32[]{:S(2)}) collective-permute-start(f32[128,1024]{1,0:T(8,128)} %get-tuple-element.49), channel_id=1, source_target_pairs={{0,6},{2,0},{4,2},{6,4},{1,7},{3,1},{5,3},{7,5},{8,14},{10,8},{12,... | collective-permute-start | bytes 1572872 | tf_op jit(solution)/shard_map/ppermute | solution.py:462
  45.3 0.2 collective-permute-start.9
  45.4 6.7 %collective-permute-done.4 = f32[128,1024]{1,0:T(8,128)S(1)} collective-permute-done((f32[128,1024]{1,0:T(8,128)S(1)}, f32[128,1024]{1,0:T(8,128)S(1)}, u32[]{:S(2)}, u32[]{:S(2)}) %collective-permute-start.4) | collective-permute-done | bytes 524320 | tf_op jit(solution)/shard_map/ppermute | solution.py:462
  52.2 0.0 copy-start.10
  52.2 0.8 copy-done.10
  53.0 2.0 %collective-permute-start.8 = (f32[128,1024]{1,0:T(8,128)}, f32[128,1024]{1,0:T(8,128)}, u32[]{:S(2)}, u32[]{:S(2)}) collective-permute-start(f32[128,1024]{1,0:T(8,128)} %get-tuple-element.47), channel_id=1, source_target_pairs={{0,4},{2,6},{4,0},{6,2},{1,5},{3,7},{5,1},{7,3},{8,12},{10,14},{12... | collective-permute-start | bytes 1572872 | tf_op jit(solution)/shard_map/ppermute | solution.py:462
  55.0 0.0 copy-done
  55.0 0.0 copy-start.1
  55.0 1.6 %copy-done.1 = bf16[512,2048]{1,0:T(8,128)(2,1)S(1)} copy-done((bf16[512,2048]{1,0:T(8,128)(2,1)S(1)}, bf16[512,2048]{1,0:T(8,128)(2,1)}, u32[]{:S(2)}) %copy-start.1) | copy-done | bytes 2097176
  56.6 1.0 copy-done.3
  57.6 0.9 copy-done.5
  58.6 3.0 %rows.1 = (f32[128,1024]{1,0:T(8,128)S(1)}, f32[128,1024]{1,0:T(8,128)}, f32[128,1024]{1,0:T(8,128)S(1)}, f32[128,1024]{1,0:T(8,128)S(1)}) custom-call(s32[4]{0:T(128)S(1)} %pad_add_fusion.1.idx, bf16[256,1024]{1,0:T(8,128)(2,1)S(1)} %get-tuple-element.36.packed, bf16[256,1024]{1,0:T(8,128)(2,1)S(1)} %copy-done.3, ...), custom_call_target="tpu_custom_call" | custom-call | tf_op jit(solution)/shard_map/rows/pallas_call | solution.py:371
  61.6 0.8 copy-done.6
  62.4 0.8 copy-done.8
  63.2 0.0 collective-permute-done.3
  63.2 13.4 %collective-permute-start.1 = (f32[128,1024]{1,0:T(8,128)}, f32[128,1024]{1,0:T(8,128)S(1)}, u32[]{:S(2)}, u32[]{:S(2)}) collective-permute-start(f32[128,1024]{1,0:T(8,128)} %get-tuple-element.41), channel_id=1, source_target_pairs={{0,1},{1,0},{2,3},{3,2},{4,5},{5,4},{6,7},{7,6},{8,9},{9,8},{10,11... | collective-permute-start | bytes 1572872 | tf_op jit(solution)/shard_map/ppermute | solution.py:471
  76.6 0.0 collective-permute-done.2
  76.6 0.0 copy-done.11
  76.6 1.5 %dynamic-slice_add_fusion.4 = (f32[32,1024]{1,0:T(8,128)S(1)}, f32[32,1024]{1,0:T(8,128)S(1)}, f32[32,1024]{1,0:T(8,128)S(1)}, f32[32,1024]{1,0:T(8,128)S(1)}) fusion(f32[128,1024]{1,0:T(8,128)S(1)} %copy-done.11, s32[]{:T(128)S(6)} %select_n.28, f32[128,1024]{1,0:T(8,128)} %collective-permute-done.3, f32[128,1024]{1,0:T(8,128)} %collective-permute-done.2, ...), kind=kLoop, calls=%fused_computation.10 | loop fusion | flops 393216 | bytes 2621456 | tf_op jit(solution)/shard_map/add | solution.py:392
  78.1 1.4 %collective-permute-start.5 = (f32[32,1024]{1,0:T(8,128)S(1)}, f32[32,1024]{1,0:T(8,128)S(1)}, u32[]{:S(2)}, u32[]{:S(2)}) collective-permute-start(f32[32,1024]{1,0:T(8,128)S(1)} %get-tuple-element.58), channel_id=1, source_target_pairs={{0,4},{2,6},{4,0},{6,2},{1,5},{3,7},{5,1},{7,3},{8,12},{10,14},{12... | collective-permute-start | bytes 393224 | tf_op jit(solution)/shard_map/ppermute | solution.py:462
  79.4 0.0 collective-permute-done.10
  79.4 0.0 collective-permute-start.6
  79.5 0.0 collective-permute-done.9
  79.5 2.7 %collective-permute-start.7 = (f32[32,1024]{1,0:T(8,128)S(1)}, f32[32,1024]{1,0:T(8,128)S(1)}, u32[]{:S(2)}, u32[]{:S(2)}) collective-permute-start(f32[32,1024]{1,0:T(8,128)S(1)} %get-tuple-element.56), channel_id=1, source_target_pairs={{0,6},{2,0},{4,2},{6,4},{1,7},{3,1},{5,3},{7,5},{8,14},{10,8},{12,... | collective-permute-start | bytes 393224 | tf_op jit(solution)/shard_map/ppermute | solution.py:462
  82.1 0.0 collective-permute-done.8
  82.1 0.0 copy-done.9
  82.1 1.7 %dynamic-slice_add_fusion = (f32[32,1024]{1,0:T(8,128)S(1)}, f32[32,1024]{1,0:T(8,128)S(1)}, f32[32,1024]{1,0:T(8,128)S(1)}, f32[32,1024]{1,0:T(8,128)S(1)}) fusion(f32[128,1024]{1,0:T(8,128)} %collective-permute-done.10, s32[]{:T(128)S(6)} %select_n.32, f32[128,1024]{1,0:T(8,128)} %collective-permute-done.9, f32[128,1024]{1,0:T(8,128)} %collective-permute-done.8, ...), kind=kLoop, calls=%fused_computation.6 | loop fusion | flops 393216 | bytes 2621456 | tf_op jit(solution)/shard_map/add | solution.py:392
  83.8 0.3 collective-permute-start.11
  84.1 0.6 collective-permute-done.5.a1
  84.6 3.4 %collective-permute-start.12 = (f32[32,1024]{1,0:T(8,128)S(1)}, f32[32,1024]{1,0:T(8,128)S(1)}, u32[]{:S(2)}, u32[]{:S(2)}) collective-permute-start(f32[32,1024]{1,0:T(8,128)S(1)} %get-tuple-element.53), channel_id=1, source_target_pairs={{0,64},{64,128},{128,192},{192,0},{1,65},{65,129},{129,193},{193,1... | collective-permute-start | bytes 393224 | tf_op jit(solution)/shard_map/ppermute | solution.py:462
  88.0 0.0 collective-permute-done.6.a2
  88.0 3.3 %collective-permute-start.13 = (f32[32,1024]{1,0:T(8,128)S(1)}, f32[32,1024]{1,0:T(8,128)S(1)}, u32[]{:S(2)}, u32[]{:S(2)}) collective-permute-start(f32[32,1024]{1,0:T(8,128)S(1)} %get-tuple-element.52), channel_id=1, source_target_pairs={{0,192},{64,0},{128,64},{192,128},{1,193},{65,1},{129,65},{193,129... | collective-permute-start | bytes 393224 | tf_op jit(solution)/shard_map/ppermute | solution.py:462
  91.3 0.0 collective-permute-done.7.a3
  91.3 0.0 collective-permute-done.11.b1
  91.3 2.4 %collective-permute-done.12.b2 = f32[32,1024]{1,0:T(8,128)S(1)} collective-permute-done((f32[32,1024]{1,0:T(8,128)S(1)}, f32[32,1024]{1,0:T(8,128)S(1)}, u32[]{:S(2)}, u32[]{:S(2)}) %collective-permute-start.12) | collective-permute-done | bytes 131104 | tf_op jit(solution)/shard_map/ppermute | solution.py:462
  93.7 0.6 collective-permute-done.13.b3
  94.3 0.7 joined.1
  95.0 3.4 %all-to-all-start.1 = ((f32[8,8,1024]{2,1,0:T(8,128)}), f32[8,8,1024]{2,1,0:T(8,128)S(1)}, u32[]{:S(2)}, u32[]{:S(2)}) async-start(f32[8,8,1024]{2,1,0:T(8,128)} %joined.1), calls=%async_computation.1 | async-start | bytes 524288 | tf_op jit(solution)/shard_map/all_to_all | solution.py:479
  98.4 0.0 copy-done.12
  98.4 0.0 collective-permute-done.1
  98.5 0.0 copy-done.7
  98.5 0.1 fusion.1
  98.6 10.0 %all-to-all-done.1 = f32[8,8,1024]{2,1,0:T(8,128)S(1)} async-done(((f32[8,8,1024]{2,1,0:T(8,128)}), f32[8,8,1024]{2,1,0:T(8,128)S(1)}, u32[]{:S(2)}, u32[]{:S(2)}) %all-to-all-start.1) | async-done | bytes 262176 | tf_op jit(solution)/shard_map/all_to_all | solution.py:479
  108.7 2.6 %collective-permute-start.14 = (f32[2,2,1024]{2,1,0:T(2,128)S(1)}, f32[2,2,1024]{2,1,0:T(2,128)S(1)}, u32[]{:S(2)}, u32[]{:S(2)}) collective-permute-start(f32[2,2,1024]{2,1,0:T(2,128)S(1)} %get-tuple-element.62), channel_id=1, source_target_pairs={{0,1},{1,0},{2,3},{3,2},{4,5},{5,4},{6,7},{7,6},{8,9},{9,8},{10,11... | collective-permute-start | bytes 49160 | tf_op jit(solution)/shard_map/ppermute | solution.py:482
  111.3 0.7 slice_bitcast_fusion
  112.0 0.1 collective-permute-done.14.come
  112.2 1.2 %tail.1 = (f32[2,2048]{1,0:T(2,128)}, f32[2,2048]{1,0:T(2,128)}) custom-call(s32[4]{0:T(128)S(1)} %pad_add_fusion.1.idx, f32[2,2,1024]{2,1,0:T(2,128)S(1)} %get-tuple-element.63.keep, f32[2,2,1024]{2,1,0:T(2,128)S(1)} %collective-permute-done.14.come), custom_call_target="tpu_custom_call" | custom-call | tf_op jit(solution)/shard_map/tail/pallas_call | solution.py:421
  (13 shorter events, 0.1 us)
Async XLA Ops:
  1.7 4.9 %collective-permute-start = (f32[136,1024]{1,0:T(8,128)S(1)}, f32[136,1024]{1,0:T(8,128)S(1)}, u32[]{:S(2)}, u32[]{:S(2)}) collective-permute-start(f32[136,1024]{1,0:T(8,128)S(1)} %pad_add_fusion.mine), channel_id=1, source_target_pairs={{0,1},{1,0},{2,3},{3,2},{4,5},{5,4},{6,7},{7,6},{8,9},{9,8},{10,11... | collective-permute-start | bytes 1671176 | tf_op jit(solution)/shard_map/ppermute | solution.py:452
  33.1 21.9 %copy-start = (bf16[512,2048]{1,0:T(8,128)(2,1)S(1)}, bf16[512,2048]{1,0:T(8,128)(2,1)}, u32[]{:S(2)}) copy-start(bf16[512,2048]{1,0:T(8,128)(2,1)} %win_im.1) | copy-start | bytes 6291460
  37.0 2.0 %copy-start.4 = (bf16[512,256]{1,0:T(8,128)(2,1)}, bf16[512,256]{1,0:T(8,128)(2,1)S(1)}, u32[]{:S(2)}) copy-start(bf16[512,256]{1,0:T(8,128)(2,1)S(1)} %get-tuple-element.39.lhs_out) | copy-start | bytes 786436
  39.0 0.8 copy-start.2
  39.8 12.4 %collective-permute-start.4 = (f32[128,1024]{1,0:T(8,128)S(1)}, f32[128,1024]{1,0:T(8,128)S(1)}, u32[]{:S(2)}, u32[]{:S(2)}) collective-permute-start(f32[128,1024]{1,0:T(8,128)S(1)} %get-tuple-element.45), channel_id=1, source_target_pairs={{0,192},{64,0},{128,64},{192,128},{1,193},{65,1},{129,65},{193,129... | collective-permute-start | bytes 1572872 | tf_op jit(solution)/shard_map/ppermute | solution.py:462
  42.2 21.0 %collective-permute-start.3 = (f32[128,1024]{1,0:T(8,128)}, f32[128,1024]{1,0:T(8,128)}, u32[]{:S(2)}, u32[]{:S(2)}) collective-permute-start(f32[128,1024]{1,0:T(8,128)} %get-tuple-element.44), channel_id=1, source_target_pairs={{0,64},{64,128},{128,192},{192,0},{1,65},{65,129},{129,193},{193,1... | collective-permute-start | bytes 1572872 | tf_op jit(solution)/shard_map/ppermute | solution.py:462
  42.2 34.3 %collective-permute-start.2 = (f32[128,1024]{1,0:T(8,128)}, f32[128,1024]{1,0:T(8,128)}, u32[]{:S(2)}, u32[]{:S(2)}) collective-permute-start(f32[128,1024]{1,0:T(8,128)} %get-tuple-element.43), channel_id=1, source_target_pairs={{0,128},{64,192},{128,0},{192,64},{1,129},{65,193},{129,1},{193,65... | collective-permute-start | bytes 1572872 | tf_op jit(solution)/shard_map/ppermute | solution.py:462
  44.0 35.5 %collective-permute-start.10 = (f32[128,1024]{1,0:T(8,128)}, f32[128,1024]{1,0:T(8,128)}, u32[]{:S(2)}, u32[]{:S(2)}) collective-permute-start(f32[128,1024]{1,0:T(8,128)} %get-tuple-element.49), channel_id=1, source_target_pairs={{0,6},{2,0},{4,2},{6,4},{1,7},{3,1},{5,3},{7,5},{8,14},{10,8},{12,... | collective-permute-start | bytes 1572872 | tf_op jit(solution)/shard_map/ppermute | solution.py:462
  45.3 34.2 %collective-permute-start.9 = (f32[128,1024]{1,0:T(8,128)}, f32[128,1024]{1,0:T(8,128)}, u32[]{:S(2)}, u32[]{:S(2)}) collective-permute-start(f32[128,1024]{1,0:T(8,128)} %get-tuple-element.48), channel_id=1, source_target_pairs={{0,2},{2,4},{4,6},{6,0},{1,3},{3,5},{5,7},{7,1},{8,10},{10,12},{12... | collective-permute-start | bytes 1572872 | tf_op jit(solution)/shard_map/ppermute | solution.py:462
  52.2 0.8 copy-start.10
  53.0 29.1 %collective-permute-start.8 = (f32[128,1024]{1,0:T(8,128)}, f32[128,1024]{1,0:T(8,128)}, u32[]{:S(2)}, u32[]{:S(2)}) collective-permute-start(f32[128,1024]{1,0:T(8,128)} %get-tuple-element.47), channel_id=1, source_target_pairs={{0,4},{2,6},{4,0},{6,2},{1,5},{3,7},{5,1},{7,3},{8,12},{10,14},{12... | collective-permute-start | bytes 1572872 | tf_op jit(solution)/shard_map/ppermute | solution.py:462
  55.0 1.6 %copy-start.1 = (bf16[512,2048]{1,0:T(8,128)(2,1)S(1)}, bf16[512,2048]{1,0:T(8,128)(2,1)}, u32[]{:S(2)}) copy-start(bf16[512,2048]{1,0:T(8,128)(2,1)} %wout_im.1) | copy-start | bytes 6291460
  56.6 1.0 copy-start.3
  57.6 0.9 copy-start.5
  58.6 18.0 %copy-start.11 = (f32[128,1024]{1,0:T(8,128)S(1)}, f32[128,1024]{1,0:T(8,128)}, u32[]{:S(2)}) copy-start(f32[128,1024]{1,0:T(8,128)} %copy-done.10) | copy-start | bytes 1572868
  61.6 0.8 copy-start.6
  62.4 0.8 copy-start.8
  63.2 18.9 %copy-start.9 = (f32[128,1024]{1,0:T(8,128)S(1)}, f32[128,1024]{1,0:T(8,128)}, u32[]{:S(2)}) copy-start(f32[128,1024]{1,0:T(8,128)} %copy-done.8) | copy-start | bytes 1572868
  63.2 35.2 %collective-permute-start.1 = (f32[128,1024]{1,0:T(8,128)}, f32[128,1024]{1,0:T(8,128)S(1)}, u32[]{:S(2)}, u32[]{:S(2)}) collective-permute-start(f32[128,1024]{1,0:T(8,128)} %get-tuple-element.41), channel_id=1, source_target_pairs={{0,1},{1,0},{2,3},{3,2},{4,5},{5,4},{6,7},{7,6},{8,9},{9,8},{10,11... | collective-permute-start | bytes 1572872 | tf_op jit(solution)/shard_map/ppermute | solution.py:471
  78.1 6.6 %collective-permute-start.5 = (f32[32,1024]{1,0:T(8,128)S(1)}, f32[32,1024]{1,0:T(8,128)S(1)}, u32[]{:S(2)}, u32[]{:S(2)}) collective-permute-start(f32[32,1024]{1,0:T(8,128)S(1)} %get-tuple-element.58), channel_id=1, source_target_pairs={{0,4},{2,6},{4,0},{6,2},{1,5},{3,7},{5,1},{7,3},{8,12},{10,14},{12... | collective-permute-start | bytes 393224 | tf_op jit(solution)/shard_map/ppermute | solution.py:462
  79.4 8.6 %collective-permute-start.6 = (f32[32,1024]{1,0:T(8,128)S(1)}, f32[32,1024]{1,0:T(8,128)S(1)}, u32[]{:S(2)}, u32[]{:S(2)}) collective-permute-start(f32[32,1024]{1,0:T(8,128)S(1)} %get-tuple-element.57), channel_id=1, source_target_pairs={{0,2},{2,4},{4,6},{6,0},{1,3},{3,5},{5,7},{7,1},{8,10},{10,12},{12... | collective-permute-start | bytes 393224 | tf_op jit(solution)/shard_map/ppermute | solution.py:462
  79.5 11.8 %collective-permute-start.7 = (f32[32,1024]{1,0:T(8,128)S(1)}, f32[32,1024]{1,0:T(8,128)S(1)}, u32[]{:S(2)}, u32[]{:S(2)}) collective-permute-start(f32[32,1024]{1,0:T(8,128)S(1)} %get-tuple-element.56), channel_id=1, source_target_pairs={{0,6},{2,0},{4,2},{6,4},{1,7},{3,1},{5,3},{7,5},{8,14},{10,8},{12,... | collective-permute-start | bytes 393224 | tf_op jit(solution)/shard_map/ppermute | solution.py:462
  82.1 16.3 %copy-start.12 = (f32[512]{0:T(512)S(1)}, f32[512]{0:T(512)}, u32[]{:S(2)}) copy-start(f32[512]{0:T(512)} %param.14) | copy-start | bytes 6148
  82.1 16.3 %copy-start.7 = (f32[128,1024]{1,0:T(8,128)S(1)}, f32[128,1024]{1,0:T(8,128)}, u32[]{:S(2)}) copy-start(f32[128,1024]{1,0:T(8,128)} %copy-done.6) | copy-start | bytes 1572868
  83.8 7.5 %collective-permute-start.11 = (f32[32,1024]{1,0:T(8,128)S(1)}, f32[32,1024]{1,0:T(8,128)S(1)}, u32[]{:S(2)}, u32[]{:S(2)}) collective-permute-start(f32[32,1024]{1,0:T(8,128)S(1)} %get-tuple-element.54), channel_id=1, source_target_pairs={{0,128},{64,192},{128,0},{192,64},{1,129},{65,193},{129,1},{193,65... | collective-permute-start | bytes 393224 | tf_op jit(solution)/shard_map/ppermute | solution.py:462
  84.6 9.0 %collective-permute-start.12 = (f32[32,1024]{1,0:T(8,128)S(1)}, f32[32,1024]{1,0:T(8,128)S(1)}, u32[]{:S(2)}, u32[]{:S(2)}) collective-permute-start(f32[32,1024]{1,0:T(8,128)S(1)} %get-tuple-element.53), channel_id=1, source_target_pairs={{0,64},{64,128},{128,192},{192,0},{1,65},{65,129},{129,193},{193,1... | collective-permute-start | bytes 393224 | tf_op jit(solution)/shard_map/ppermute | solution.py:462
  88.0 6.2 %collective-permute-start.13 = (f32[32,1024]{1,0:T(8,128)S(1)}, f32[32,1024]{1,0:T(8,128)S(1)}, u32[]{:S(2)}, u32[]{:S(2)}) collective-permute-start(f32[32,1024]{1,0:T(8,128)S(1)} %get-tuple-element.52), channel_id=1, source_target_pairs={{0,192},{64,0},{128,64},{192,128},{1,193},{65,1},{129,65},{193,129... | collective-permute-start | bytes 393224 | tf_op jit(solution)/shard_map/ppermute | solution.py:462
  95.0 13.6 %all-to-all-start.1 = ((f32[8,8,1024]{2,1,0:T(8,128)}), f32[8,8,1024]{2,1,0:T(8,128)S(1)}, u32[]{:S(2)}, u32[]{:S(2)}) async-start(f32[8,8,1024]{2,1,0:T(8,128)} %joined.1), calls=%async_computation.1 | async-start | bytes 524288 | tf_op jit(solution)/shard_map/all_to_all | solution.py:479
  108.7 3.5 %collective-permute-start.14 = (f32[2,2,1024]{2,1,0:T(2,128)S(1)}, f32[2,2,1024]{2,1,0:T(2,128)S(1)}, u32[]{:S(2)}, u32[]{:S(2)}) collective-permute-start(f32[2,2,1024]{2,1,0:T(2,128)S(1)} %get-tuple-element.62), channel_id=1, source_target_pairs={{0,1},{1,0},{2,3},{3,2},{4,5},{5,4},{6,7},{7,6},{8,9},{9,8},{10,11... | collective-permute-start | bytes 49160 | tf_op jit(solution)/shard_map/ppermute | solution.py:482
